TPU v7x, 32 devices: a whole 2x2x4 slice. The times are simulated.
32 devices in a mesh: branch: 8 (over y, x, core), dap: 4 (over z).
Axes of the slice: x: 2, y: 2, z: 4, core: 2. Of those that a mesh axis runs over, the one named last changes fastest.
Arguments:
- homolog_embedding: bfloat16 [128, 256, 256], P(('branch', 'dap')), may hold values from -6 to 6
- couple_embedding: bfloat16 [256, 256, 128], P(('branch', 'dap')), may hold values from -6 to 6
- homolog_present: int32 [128, 256], P(('branch', 'dap')), may hold values from 0 to 1
- observed_position: int32 [256], replicated, may hold values 0 or 1
- couple_logit_kernel: bfloat16 [128, 8], replicated, may hold values from -40 to 40
- lookup_kernels: bfloat16 [256, 768], replicated, may hold values from -0.375 to 0.375
- heads_sigmoid_kernel: bfloat16 [256, 256], replicated, may hold values from -0.375 to 0.375
- heads_merge_kernel: bfloat16 [256, 256], replicated, may hold values from -0.375 to 0.375
- tensor_halves_kernel: bfloat16 [256, 64], replicated, may hold values from -0.375 to 0.375
- tensor_merge_kernel: bfloat16 [1024, 128], replicated, may hold values from -0.1875 to 0.1875
- edge_entry_kernel: bfloat16 [128, 512], replicated, may hold values from -0.5 to 0.5
- closing_sigmoid_kernel: bfloat16 [128, 128], replicated, may hold values from -0.5 to 0.5
- closing_merge_kernel: bfloat16 [128, 128], replicated, may hold values from -0.5 to 0.5
Outputs:
- homolog_refreshed: bfloat16 [128, 256, 256], P(('branch', 'dap'))
- pair_output: bfloat16 [256, 256, 128], P(('branch', 'dap'))
All inputs are finite; a program needn't handle non-finite values.
Results may differ from a plain program's by a relative error of at most 0.013.
The roundings to bfloat16 on the way count: a program that leaves them out, or rounds other values in their place, can miss the bound.
Values may be sent and summed in bfloat16 or wider, within the bound.
No kernel may reach another device: no remote copies, remote signals or barrier semaphores. Data moves between devices by JAX's collectives and lax.ppermute only.
A program may use at most 128 MiB of HBM per device.

v0:
```python
import jax
import jax.numpy as jnp
from jax import lax
from jax.sharding import PartitionSpec as P

epsilon = 1e-05


def normalize(values):
    values = values.astype(jnp.float32)
    centred = values - jnp.mean(values, axis=-1, keepdims=True)
    spread = jnp.mean(centred * centred, axis=-1, keepdims=True)
    return centred * lax.rsqrt(spread + epsilon)


def row_update(
    sequence,
    keep,
    bias_full,
    lookup_kernels,
    heads_sigmoid_kernel,
    heads_merge_kernel,
    tensor_halves_kernel,
):
    heads = bias_full.shape[0]
    inner = lookup_kernels.shape[1] // 3
    head_width = inner // heads
    normed = normalize(sequence).astype(jnp.bfloat16)
    projected = jnp.dot(normed, lookup_kernels, preferred_element_type=jnp.float32).astype(
        jnp.bfloat16
    )
    queries = projected[:, :inner].reshape(-1, heads, head_width)
    key_rows = projected[:, inner : 2 * inner].reshape(-1, heads, head_width)
    value_rows = projected[:, 2 * inner :].reshape(-1, heads, head_width)
    gating = jax.nn.sigmoid(
        jnp.dot(normed, heads_sigmoid_kernel, preferred_element_type=jnp.float32)
    ).reshape(-1, heads, head_width)
    logits = jnp.einsum("ihd,jhd->hij", queries, key_rows, preferred_element_type=jnp.float32)
    masking = jnp.where(keep == 1, 0.0, -1000000000.0)
    logits = logits * head_width ** (-0.5) + bias_full.astype(jnp.float32) + masking[None, None, :]
    weights = jax.nn.softmax(logits, axis=-1).astype(jnp.bfloat16)
    mixed = jnp.einsum("hij,jhd->ihd", weights, value_rows, preferred_element_type=jnp.float32)
    attended = (mixed * gating).astype(jnp.bfloat16).reshape(-1, inner)
    updated = sequence.astype(jnp.float32) + jnp.dot(
        attended, heads_merge_kernel, preferred_element_type=jnp.float32
    )
    updated = updated.astype(jnp.bfloat16)
    projected_halves = jnp.dot(
        normalize(updated).astype(jnp.bfloat16),
        tensor_halves_kernel,
        preferred_element_type=jnp.float32,
    )
    projected_halves = (projected_halves * keep.astype(jnp.float32)[:, None]).astype(jnp.bfloat16)
    return (updated, projected_halves)


def edge_factors(normed, row_marks, observed_position, edge_entry_kernel):
    inner = edge_entry_kernel.shape[1] // 4
    projected = jnp.dot(normed, edge_entry_kernel, preferred_element_type=jnp.float32)
    pair_marks = (row_marks[:, None] * observed_position[None, :]).astype(jnp.float32)[:, :, None]
    left_edge = (
        jax.nn.sigmoid(projected[..., inner : 2 * inner]) * projected[..., :inner] * pair_marks
    )
    right_edge = (
        jax.nn.sigmoid(projected[..., 3 * inner :])
        * projected[..., 2 * inner : 3 * inner]
        * pair_marks
    )
    return (left_edge.astype(jnp.bfloat16), right_edge.astype(jnp.bfloat16))


def finish_triangle(pair_next, normed_next, combined, closing_sigmoid_kernel, closing_merge_kernel):
    combined_normed = normalize(combined).astype(jnp.bfloat16)
    update = jnp.dot(combined_normed, closing_merge_kernel, preferred_element_type=jnp.float32)
    gating = jax.nn.sigmoid(
        jnp.dot(normed_next, closing_sigmoid_kernel, preferred_element_type=jnp.float32)
    )
    return (pair_next.astype(jnp.float32) + gating * update).astype(jnp.bfloat16)


def accumulate(carry, left_piece, own_marks, right_piece, other_marks, table):
    totals, counts = carry
    piece_seqs, row_count, width = left_piece.shape
    channels = table.shape[2]
    projected_left = jnp.einsum(
        "sip,pqc->icsq", left_piece.astype(jnp.float32), table, precision=lax.Precision.HIGHEST
    )
    projected_left = projected_left.reshape(row_count * channels, piece_seqs * width)
    right_flat = (
        right_piece.astype(jnp.float32)
        .transpose(0, 2, 1)
        .reshape(piece_seqs * width, right_piece.shape[1])
    )
    update = jnp.dot(projected_left, right_flat, precision=lax.Precision.HIGHEST)
    counts = jnp.einsum("si,sj->ij", own_marks, other_marks, preferred_element_type=jnp.float32)
    return (update.reshape(totals.shape), counts)


def per_device(
    homolog_embedding,
    couple_embedding,
    homolog_present,
    observed_position,
    couple_logit_kernel,
    lookup_kernels,
    heads_sigmoid_kernel,
    heads_merge_kernel,
    tensor_halves_kernel,
    tensor_merge_kernel,
    edge_entry_kernel,
    closing_sigmoid_kernel,
    closing_merge_kernel,
):
    row_count = couple_embedding.shape[0]
    residues = couple_embedding.shape[1]
    channels = couple_embedding.shape[2]
    first_row = lax.axis_index(("branch", "dap")) * row_count
    pair_normed = normalize(couple_embedding).astype(jnp.bfloat16)
    local_bias = jnp.einsum(
        "ijc,ch->hij", pair_normed, couple_logit_kernel, preferred_element_type=jnp.float32
    ).astype(jnp.bfloat16)
    bias_full = lax.all_gather(local_bias, ("branch", "dap"), axis=1, tiled=True)

    def homolog_along(item):
        return row_update(
            item[0],
            item[1],
            bias_full,
            lookup_kernels,
            heads_sigmoid_kernel,
            heads_merge_kernel,
            tensor_halves_kernel,
        )

    homolog_refreshed, projected_halves = lax.map(
        homolog_along, (homolog_embedding, homolog_present)
    )
    width = projected_halves.shape[2] // 2
    leading_projected = projected_halves[..., :width]
    right_factor = projected_halves[..., width:]
    presence_indicators = homolog_present.astype(jnp.bfloat16)
    table = tensor_merge_kernel.astype(jnp.float32).reshape(width, width, channels)
    start_sums = (
        jnp.zeros((row_count, channels, residues), jnp.float32),
        jnp.zeros((row_count, residues), jnp.float32),
    )
    left_rows, mark_rows = (
        lax.all_to_all(
            leading_projected, ("branch", "dap"), split_axis=1, concat_axis=0, tiled=True
        ),
        lax.all_to_all(
            presence_indicators, ("branch", "dap"), split_axis=1, concat_axis=0, tiled=True
        ),
    )
    totals, counts = accumulate(
        start_sums,
        left_rows,
        mark_rows,
        lax.all_gather(right_factor, ("branch", "dap"), axis=0, tiled=True),
        lax.all_gather(presence_indicators, ("branch", "dap"), axis=0, tiled=True),
        table,
    )
    projected = totals.transpose(0, 2, 1)
    pair_next = (
        couple_embedding.astype(jnp.float32) + projected / jnp.maximum(counts, 1.0)[:, :, None]
    ).astype(jnp.bfloat16)
    normed_next = normalize(pair_next).astype(jnp.bfloat16)
    row_marks = lax.dynamic_slice_in_dim(observed_position, first_row, row_count, 0)
    left_edge, right_edge = edge_factors(
        normed_next, row_marks, observed_position, edge_entry_kernel
    )
    combined = jnp.einsum(
        "ikc,jkc->ijc",
        left_edge,
        lax.all_gather(right_edge, ("branch", "dap"), axis=0, tiled=True),
        preferred_element_type=jnp.float32,
    )
    pair_output = finish_triangle(
        pair_next, normed_next, combined, closing_sigmoid_kernel, closing_merge_kernel
    )
    return (homolog_refreshed, pair_output)


def solution(mesh):
    in_specs = (
        P(("branch", "dap"), None, None),
        P(("branch", "dap"), None, None),
        P(("branch", "dap"), None),
        P(),
        P(),
        P(),
        P(),
        P(),
        P(),
        P(),
        P(),
        P(),
        P(),
    )
    out_specs = (P(("branch", "dap"), None, None), P(("branch", "dap"), None, None))
    return jax.shard_map(
        per_device, mesh=mesh, in_specs=in_specs, out_specs=out_specs, check_vma=False
    )
```

profile of v0, /device:TPU:0, one launch (start us, length us, event | category | flops | bytes accessed | tf_op | source)
XLA Modules:
  0.0 371.7 jit_solution(772327837201820340)
XLA Ops:
  9.8 58.4 %all-gather.5.cloned.1.call-done = bf16[8,256,256]{2,0,1:T(8,128)(2,1)} async-done(((bf16[8,8,256]{2,0,1:T(8,128)(2,1)}), bf16[8,256,256]{2,0,1:T(8,128)(2,1)}) %all-gather.5.cloned.1.call-update) | async-done | bytes 1048592 | tf_op jit(solution)/shard_map/all_gather | solution.py:122
  68.1 1.6 copy.69
  69.8 34.3 %while.12 = (s32[]{:T(128)}, bf16[4,256,256]{2,1,0:T(8,128)(2,1)S(1)}, bf16[4,256,64]{1,2,0:T(8,128)(2,1)S(1)}, bf16[4,256,256]{2,1,0:T(8,128)(2,1)}, bf16[256,7...) while((s32[]{:T(128)}, ...), condition=%wide.region_9.10_spmd, body=%wide.region_2.9_spmd.sunk | while | flops 249792000 | bytes 11380901 | solution.py:135
  71.0 1.9 fusion.145
  73.6 2.3 fusion.147
  75.8 1.9 fusion.148
  79.6 1.9 fusion.145
  82.1 2.3 fusion.147
  84.4 1.9 fusion.148
  88.2 1.9 fusion.145
  90.7 2.3 fusion.147
  93.0 1.9 fusion.148
  96.7 1.9 fusion.145
  99.3 2.3 fusion.147
  101.5 1.9 fusion.148
  105.5 3.6 all-to-all-start.1
  109.1 69.1 %all-gather = bf16[32,4,256]{2,1,0:T(4,128)(2,1)S(1)} all-gather(bf16[1,4,256]{2,1,0:T(4,128)(2,1)S(1)} %convert_bitcast_fusion.1), channel_id=1, replica_groups=mesh['branch'=8,'dap'=4] {'branch','dap'}, dimensions={0}, use_global_device_ids=true | all-gather | bytes 67584 | tf_op jit(solution)/shard_map/all_gather | solution.py:160
  179.6 2.6 all-to-all-start
  182.4 7.3 %all-to-all-done = bf16[32,2,512]{2,1,0:T(2,128)(2,1)S(1)} async-done(((bf16[32,2,512]{2,1,0:T(2,128)(2,1)}), bf16[32,2,512]{2,1,0:T(2,128)(2,1)S(1)}, u32[]{:S(2)}, u32[]{:S(2)}) %all-to-all-start) | async-done | bytes 65568 | tf_op jit(solution)/shard_map/all_to_all | solution.py:148
  189.9 8.0 %fusion.92 = f32[128,8,32,128]{3,0,2,1:T(8,128)} fusion(bf16[128,8,32,1]{2,1,0,3:T(8,128)(2,1)S(1)} %bitcast.177, bf16[32,32,128]{2,1,0:T(8,128)(2,1)S(1)} %bitcast.180), kind=kOutput, calls=%fused_computation.102 | convolution fusion | flops 268435456 | bytes 17104896 | tf_op jit(solution)/shard_map/sip,pqc->icsq/dot_general | solution.py:85
  198.0 20.6 %convert_reduce_fusion.2 = (f32[8,256]{1,0:T(8,128)S(1)}, bf16[8,256,128]{1,2,0:T(8,128)(2,1)S(1)}) fusion(f32[8,256]{1,0:T(8,128)S(1)} %convolution_maximum_fusion, bf16[128,256,32]{1,2,0:T(8,128)(2,1)} %all-gather.7.cloned.1.call-done, f32[128,8,32,128]{3,0,2,1:T(8,128)} %fusion.92, bf16[8,256,128]{1,2,0:T(8,128)(2,1)S(1)} %copy.66), kind=kOutput, calls=%fused_computation.50 | convolution fusion | flops 12886472704 | bytes 19939328 | tf_op jit(solution)/shard_map/dot_general | solution.py:94
  221.2 111.1 %all-gather.9.cloned.1.call-done = bf16[256,256,128]{2,1,0:T(8,128)(2,1)} async-done(((bf16[8,256,128]{2,1,0:T(8,128)(2,1)}), bf16[256,256,128]{2,1,0:T(8,128)(2,1)}) %all-gather.9.cloned.1.call-update) | async-done | bytes 16777232 | tf_op jit(solution)/shard_map/all_gather | solution.py:175
  332.3 22.1 %copy.86 = bf16[256,256,128]{1,0,2:T(8,128)(2,1)} copy(bf16[256,256,128]{2,1,0:T(8,128)(2,1)} %all-gather.9.cloned.1.call-done) | data formatting | bytes 33554432 | tf_op jit(solution)/shard_map/all_gather | solution.py:175
  354.4 8.1 %fusion.102 = (f32[8,256]{1,0:T(8,128)S(1)}, f32[8,256,128]{1,0,2:T(8,128)S(1)}) fusion(bf16[256,256,128]{1,0,2:T(8,128)(2,1)} %copy.86, bf16[8,256,128]{1,2,0:T(8,128)(2,1)S(1)} %get-tuple-element.120), kind=kOutput, calls=%fused_computation.120 | convolution fusion | flops 134477824 | bytes 18358272 | tf_op jit(solution)/shard_map/ikc,jkc->ijc/dot_general | solution.py:172
  (152 shorter events, 20.5 us)
Async XLA Ops:
  7.2 211.6 %copy-start = (bf16[128,512]{1,0:T(8,128)(2,1)S(1)}, bf16[128,512]{1,0:T(8,128)(2,1)}, u32[]{:S(2)}) copy-start(bf16[128,512]{1,0:T(8,128)(2,1)} %param.25) | copy-start | bytes 393220
  7.2 1.6 copy-start.10
  7.2 60.9 %all-gather.5.cloned.1.call-start = ((), (), s32[]{:S(2)}) async-start(), calls=%async_computation.2 | async-start | bytes 1081344 | tf_op jit(solution)/shard_map/all_gather | solution.py:122
  8.5 61.3 %copy-start.1 = (bf16[256,768]{1,0:T(8,128)(2,1)S(1)}, bf16[256,768]{1,0:T(8,128)(2,1)}, u32[]{:S(2)}) copy-start(bf16[256,768]{1,0:T(8,128)(2,1)} %param.20) | copy-start | bytes 1179652
  8.5 61.3 %copy-start.2 = (bf16[256,256]{1,0:T(8,128)(2,1)S(1)}, bf16[256,256]{1,0:T(8,128)(2,1)}, u32[]{:S(2)}) copy-start(bf16[256,256]{1,0:T(8,128)(2,1)} %param.22) | copy-start | bytes 393220
  8.5 61.3 %copy-start.4 = (s32[4,256]{1,0:T(4,128)S(1)}, s32[4,256]{1,0:T(4,128)}, u32[]{:S(2)}) copy-start(s32[4,256]{1,0:T(4,128)} %param.17) | copy-start | bytes 12292
  9.7 188.3 %all-gather.7.cloned.1.call-start = ((), (), s32[]{:S(2)}) async-start(), calls=%async_computation.3 | async-start | bytes 2162688 | tf_op jit(solution)/shard_map/all_gather | solution.py:159
  69.8 108.5 %copy-start.6 = (s32[256]{0:T(256)S(1)}, s32[256]{0:T(256)}, u32[]{:S(2)}) copy-start(s32[256]{0:T(256)} %param.18) | copy-start | bytes 3076
  75.8 2.3 copy-start.8
  84.4 2.3 copy-start.8
  93.0 2.3 copy-start.8
  101.5 2.3 copy-start.8
  104.1 93.9 %copy-start.7 = (bf16[4,256,256]{2,1,0:T(8,128)(2,1)}, bf16[4,256,256]{2,1,0:T(8,128)(2,1)S(1)}, u32[]{:S(2)}) copy-start(bf16[4,256,256]{2,1,0:T(8,128)(2,1)S(1)} %get-tuple-element.91) | copy-start | bytes 1572868
  104.1 85.8 %copy-start.3 = (bf16[1024,128]{1,0:T(8,128)(2,1)S(1)}, bf16[1024,128]{1,0:T(8,128)(2,1)}, u32[]{:S(2)}) copy-start(bf16[1024,128]{1,0:T(8,128)(2,1)} %param.24) | copy-start | bytes 786436
  105.5 74.1 %all-to-all-start.1 = ((bf16[4,32,8]{2,0,1:T(4,128)(2,1)}), bf16[4,32,8]{2,0,1:T(4,128)(2,1)S(1)}, u32[]{:S(2)}, u32[]{:S(2)}) async-start(bf16[4,32,8]{2,0,1:T(4,128)(2,1)} %copy.77), calls=%async_computation.1 | async-start | bytes 65536 | tf_op jit(solution)/shard_map/all_to_all | solution.py:151
  179.6 10.1 %all-to-all-start = ((bf16[32,2,512]{2,1,0:T(2,128)(2,1)}), bf16[32,2,512]{2,1,0:T(2,128)(2,1)S(1)}, u32[]{:S(2)}, u32[]{:S(2)}) async-start(bf16[32,2,512]{2,1,0:T(2,128)(2,1)} %reshape.150), calls=%async_computation | async-start | bytes 131072 | tf_op jit(solution)/shard_map/all_to_all | solution.py:148
  182.1 150.1 %all-gather.9.cloned.1.call-start = ((), (), s32[]{:S(2)}) async-start(), calls=%async_computation.4 | async-start | bytes 17301504 | tf_op jit(solution)/shard_map/all_gather | solution.py:175
  362.4 0.8 copy-start.5
  362.5 1.1 copy-start.9
Sparse Core Ops, SparseCore 0:
  11.6 56.5 all-gather.4
  104.9 55.3 all-gather.6
  221.3 110.9 all-gather.8
where the time goes:
time: 373 us; the launch traced here: 372 us
  waiting for transfers between devices  177 us (47%)
  blocking collectives  69.1 us (19%)
  matrix products  66.4 us (18%)
  local copies, waits for them, and re-layouts  36.2 us (10%)
  between operations  14.1 us (4%)
  starting transfers between devices  6.27 us (2%)
    all_gather x1, waiting for transfers between devices, per_device(): lax.all_gather(right_edge, ('branch', 'dap'), axis=0, tiled=True)  111 us
    all_gather x1, blocking collectives, per_device(): lax.all_gather(presence_indicators, ('branch', 'dap'), axis=0, tiled=True)  69.1 us
    all_gather x1, waiting for transfers between devices, per_device(): lax.all_gather(local_bias, ('branch', 'dap'), axis=1, tiled=True)  58.4 us
    all_gather x1, local copies, waits for them, and re-layouts, per_device(): lax.all_gather(right_edge, ('branch', 'dap'), axis=0, tiled=True)  22.1 us
    dot_general x1, matrix products, accumulate(): jnp.dot(projected_left, right_flat, precision=lax.Precision.HIGHEST)  20.6 us
    sub x4, matrix products, row_update(): weights = jax.nn.softmax(logits, axis=-1).astype(jnp.bfloat16)  9.02 us
    dot_general x1, matrix products, per_device(): jnp.einsum('ikc,jkc->ijc', left_edge, lax.all_gather(right_edge, ('branch...  8.06 us
    dot_general x1, matrix products, accumulate(): jnp.einsum('sip,pqc->icsq', left_piece.astype(jnp.float32), table, precis...  8.04 us
  transfers between devices with their start and end apart: 5, of which 3 were waited for; matrix products, arithmetic and copies ran while one was open for 3% of the time, Pallas kernels for 0%

commit v1 on v0

v1 whole, which is shorter than its diff:
```python
import functools

import jax
import jax.numpy as jnp
from jax import lax
from jax.experimental import pallas as pl
from jax.experimental.pallas import tpu as pltpu
from jax.sharding import PartitionSpec as P

EPSILON = 1e-05
EVERY = ("branch", "dap")
VMEM = pltpu.VMEM
F32 = jnp.float32
BF16 = jnp.bfloat16

NT = (((1,), (1,)), ((), ()))
TN = (((0,), (0,)), ((), ()))
NN = (((1,), (0,)), ((), ()))


def mm(a, b, dims=NN):
    return lax.dot_general(a, b, dims, preferred_element_type=F32)


def normalize(values, axis=-1):
    values = values.astype(F32)
    centred = values - jnp.mean(values, axis=axis, keepdims=True)
    spread = jnp.mean(centred * centred, axis=axis, keepdims=True)
    return centred * lax.rsqrt(spread + EPSILON)


def vspec():
    return pl.BlockSpec(memory_space=VMEM)


def sspec():
    return pl.BlockSpec(memory_space=pltpu.SMEM)


LANES = 128


def sheets(rows, columns):
    return VMEM((columns // LANES, rows, LANES), F32)


def put(scr, start, values, stride):
    for k in range(scr.shape[0]):
        part = values[:, k * LANES : (k + 1) * LANES]
        scr[k, pl.ds(start, values.shape[0], stride=stride), :] = part


def take(scr, start, count, stride=1):
    parts = [scr[k, pl.ds(start, count, stride=stride), :] for k in range(scr.shape[0])]
    return parts[0] if len(parts) == 1 else jnp.concatenate(parts, axis=1)


def fill(scr, values):
    for k in range(scr.shape[0]):
        scr[k] = values[:, k * LANES : (k + 1) * LANES]


def call(body, out, args, scratch=(), name=None, in_specs=None, flops=0, **kw):
    single = not isinstance(out, (tuple, list))
    return pl.pallas_call(
        body,
        out_shape=out,
        in_specs=in_specs or [vspec() for _ in args],
        out_specs=vspec() if single else tuple(vspec() for _ in out),
        scratch_shapes=list(scratch),
        name=name,
        cost_estimate=pl.CostEstimate(flops=flops, bytes_accessed=2**20, transcendentals=0),
        **kw,
    )(*args)


def bias_kernel(cores, couple_ref, weight_ref, out_ref, scr):
    rows = couple_ref.shape[0]
    heads = weight_ref.shape[0]
    for i in range(rows):
        normed = normalize(couple_ref[i]).astype(BF16)
        put(scr, i, mm(weight_ref[...], normed, NT), rows)
    part = heads // 2 * rows
    halves = [take(scr, k * part, part).astype(BF16) for k in range(2)]
    for t, core in enumerate(cores):
        out_ref[t] = halves[core]


def project_kernel(seq_ref, qkv_w_ref, gate_w_ref, qkv_ref, gate_ref):
    normed = normalize(seq_ref[0]).astype(BF16)
    qkv_ref[0] = mm(normed, qkv_w_ref[...]).astype(BF16)
    gate_ref[0] = jax.nn.sigmoid(mm(normed, gate_w_ref[...]))


def attend_kernel(
    heads,
    core_ref,
    seq_ref,
    keep_ref,
    qkv_ref,
    gate_ref,
    own_ref,
    other_ref,
    merge_ref,
    halves_ref,
    new_ref,
    left_ref,
    right_ref,
):
    core = core_ref[0]
    inner = gate_ref.shape[2]
    residues = gate_ref.shape[1]
    head_width = inner // heads
    half = inner // 2
    scale = head_width ** (-0.5)
    queries = qkv_ref[0, :, :inner]
    key_rows = qkv_ref[0, :, inner : 2 * inner]
    value_rows = qkv_ref[0, :, 2 * inner :]
    keep = keep_ref[0]
    masking = jnp.where(keep == 1, 0.0, -1000000000.0).astype(F32)
    lane = lax.broadcasted_iota(jnp.int32, (residues, inner), 1) // head_width
    lane_half = lax.broadcasted_iota(jnp.int32, (residues, half), 1) // head_width
    zero = jnp.zeros((), BF16)
    mixed = []
    for bias_ref, group in ((own_ref, core), (other_ref, 1 - core)):
        values = jnp.where(group == 0, value_rows[:, :half], value_rows[:, half:])
        total = jnp.zeros((residues, inner), F32)
        for h in range(heads // 2):
            head = group * (heads // 2) + h
            keys = jnp.where(lane == head, key_rows, zero)
            logits = mm(queries, keys, NT)
            logits = logits * scale + bias_ref[h].astype(F32) + masking
            top = jnp.max(logits, axis=-1, keepdims=True)
            weights = jnp.exp(logits - top).astype(BF16)
            mine = lane_half == h
            table = jnp.concatenate(
                [
                    jnp.where(mine, values, zero),
                    jnp.where(mine, jnp.ones((), BF16), zero),
                ],
                axis=1,
            )
            total = total + mm(weights, table)
        mixed.append(total[:, :half] / total[:, half:])
    first = jnp.where(core == 0, mixed[0], mixed[1])
    second = jnp.where(core == 0, mixed[1], mixed[0])
    attended = (jnp.concatenate([first, second], axis=1) * gate_ref[0]).astype(BF16)
    updated = (seq_ref[0].astype(F32) + mm(attended, merge_ref[...])).astype(BF16)
    new_ref[0] = updated
    factors = mm(halves_ref[...], normalize(updated).astype(BF16), NT)
    factors = factors * keep.astype(F32)
    width = factors.shape[0] // 2
    right_ref[0] = factors[width:].astype(BF16)
    left_ref[0] = factors[:width].T.astype(BF16)


def outer_kernel(
    seqs,
    width,
    core_ref,
    first_ref,
    marks_ref,
    own_ref,
    other_ref,
    couple_ref,
    table_ref,
    value_w_ref,
    gate_w_ref,
    observed_ref,
    pair_ref,
    edges_ref,
    right_scr,
    right_all,
    small_scr,
    keep_scr,
    edge_scr,
):
    n = own_ref.shape[0]
    rows, residues, channels = couple_ref.shape
    span = seqs * width
    half = residues // 2
    total_seqs = n * seqs
    core = core_ref[0]

    def halves(own, other):
        own, other = own.astype(F32), other.astype(F32)
        return jnp.where(core == 0, own, other), jnp.where(core == 0, other, own)

    low, high = halves(own_ref[:, :span, :], other_ref[:, :span, :])
    fill(right_scr, jnp.concatenate([low, high], axis=2).reshape(n * span, residues))
    for q in range(width):
        parts = [take(right_scr, s * width + q, n, span) for s in range(seqs)]
        right_all[q * total_seqs : (q + 1) * total_seqs, :] = jnp.concatenate(parts, axis=0).astype(
            BF16
        )
    extra = own_ref.shape[1] - span
    low, high = halves(own_ref[:, span:, :], other_ref[:, span:, :])
    fill(small_scr, own_ref[:, span:, :].astype(F32).reshape(n * extra, half))
    fill(keep_scr, jnp.concatenate([low, high], axis=2).reshape(n * extra, residues))
    left_rows = []
    for i in range(rows):
        block = take(small_scr, i, n, extra)
        for s in range(seqs):
            left_rows.append(block[:, s * width : (s + 1) * width])
    left_all = jnp.concatenate(left_rows, axis=0).astype(BF16)
    keep = jnp.concatenate(
        [take(keep_scr, rows + s, n, extra) for s in range(seqs)], axis=0
    ).astype(BF16)
    row_ids = lax.broadcasted_iota(jnp.int32, (8, residues), 0) + first_ref[0]
    chosen = (row_ids == lax.broadcasted_iota(jnp.int32, (8, residues), 1)).astype(BF16)
    own_keep = mm(chosen, keep, NT).astype(BF16)
    counts = mm(own_keep, keep)
    scale = 1.0 / jnp.maximum(counts, 1.0)
    observed = observed_ref[...].astype(F32)
    step = 2 if rows % 2 == 0 else 1
    for i0 in range(0, rows, step):
        block = left_all[i0 * total_seqs : (i0 + step) * total_seqs, :]
        projected = mm(table_ref[...], block, NT).astype(BF16)
        for i in range(i0, i0 + step):
            at = (i - i0) * total_seqs
            lhs = jnp.concatenate(
                [
                    projected[q * channels : (q + 1) * channels, at : at + total_seqs]
                    for q in range(width)
                ],
                axis=1,
            )
            update = mm(lhs, right_all[...]) * scale[i : i + 1, :]
            pair = (couple_ref[i].astype(F32) + update.T).astype(BF16)
            pair_ref[i] = pair
            normed = normalize(pair).astype(BF16)
            value = mm(value_w_ref[...], normed, NT)
            gate = mm(gate_w_ref[...], normed, NT)
            mark = observed * marks_ref[i].astype(F32)
            put(edge_scr, i, jax.nn.sigmoid(gate) * value * mark, rows)
    edges_ref[...] = take(edge_scr, 0, edges_ref.shape[0]).astype(BF16)


def close_gate_kernel(pair_ref, weight_ref, gate_ref):
    for i in range(pair_ref.shape[0]):
        normed = normalize(pair_ref[i]).astype(BF16)
        gate_ref[i] = jax.nn.sigmoid(mm(normed, weight_ref[...]))


def triangle_kernel(per, rows, in_ref, out_ref, in_scr, out_scr):
    n = in_ref.shape[0]
    residues = in_ref.shape[2]
    in_scr[...] = in_ref[...].astype(F32)
    for c in range(per):
        left = in_scr[:, c * rows : (c + 1) * rows, :].reshape(n * rows, residues).astype(BF16)
        at = (per + c) * rows
        right = in_scr[:, at : at + rows, :].reshape(n * rows, residues).astype(BF16)
        out_scr[:, c * rows : (c + 1) * rows, :] = mm(left, right, NT).reshape(n, rows, residues)
    out_ref[...] = out_scr[...].astype(BF16)


def plain_triangle_kernel(left_ref, right_ref, out_ref):
    for c in range(left_ref.shape[0]):
        out_ref[c] = mm(left_ref[c], right_ref[c], NT).astype(BF16)


def close_kernel(in_ref, pair_ref, gate_ref, weight_ref, out_ref, scr):
    rows, residues, channels = pair_ref.shape
    fill(scr, in_ref[...].astype(F32))
    for i in range(rows):
        normed = normalize(take(scr, i, channels, rows), axis=0).astype(BF16)
        update = mm(normed, weight_ref[...], TN)
        out_ref[i] = (pair_ref[i].astype(F32) + gate_ref[i] * update).astype(BF16)


def per_device(
    branch,
    dap,
    homolog_embedding,
    couple_embedding,
    homolog_present,
    observed_position,
    couple_logit_kernel,
    lookup_kernels,
    heads_sigmoid_kernel,
    heads_merge_kernel,
    tensor_halves_kernel,
    tensor_merge_kernel,
    edge_entry_kernel,
    closing_sigmoid_kernel,
    closing_merge_kernel,
):
    n = branch * dap
    rows, residues, channels = couple_embedding.shape
    seqs = homolog_embedding.shape[0]
    features = homolog_embedding.shape[2]
    heads = couple_logit_kernel.shape[1]
    inner = heads_sigmoid_kernel.shape[1]
    width = tensor_halves_kernel.shape[1] // 2
    per = channels // n
    half = residues // 2
    cores = [(t // dap) % 2 for t in range(n)]
    core = (lax.axis_index("branch") % 2).astype(jnp.int32).reshape(1)
    first_row = lax.axis_index(EVERY) * rows
    partner = [(b, b ^ 1) for b in range(branch)]

    def exchange(values):
        return lax.all_to_all(values, EVERY, split_axis=0, concat_axis=0, tiled=True)

    def swap(values):
        return lax.ppermute(values, "branch", partner)

    table = (
        tensor_merge_kernel.reshape(width, width, channels)
        .transpose(1, 2, 0)
        .reshape(width * channels, width)
    )
    entry = edge_entry_kernel.reshape(channels, 2, 2, n, per)
    value_w = entry[:, :, 0].transpose(2, 1, 3, 0).reshape(2 * channels, channels)
    gate_w = entry[:, :, 1].transpose(2, 1, 3, 0).reshape(2 * channels, channels)

    half_heads = heads // 2
    message = call(
        functools.partial(bias_kernel, cores),
        jax.ShapeDtypeStruct((n, half_heads * rows, residues), BF16),
        (couple_embedding, couple_logit_kernel.T),
        [sheets(heads * rows, residues)],
        name="bias",
    )
    own_bias = exchange(message).reshape(n, half_heads, rows, residues)
    own_bias = own_bias.transpose(1, 0, 2, 3).reshape(half_heads, residues, residues)
    other_bias = swap(own_bias)

    def whole(*shape):
        return pl.BlockSpec(shape, lambda s: (0,) * len(shape))

    def per_seq(*shape):
        return pl.BlockSpec((1, *shape), lambda s: (s,) + (0,) * len(shape))

    qkv, gates = pl.pallas_call(
        project_kernel,
        grid=(seqs,),
        out_shape=(
            jax.ShapeDtypeStruct((seqs, residues, 3 * inner), BF16),
            jax.ShapeDtypeStruct((seqs, residues, inner), F32),
        ),
        in_specs=[
            per_seq(residues, features),
            whole(features, 3 * inner),
            whole(features, inner),
        ],
        out_specs=(per_seq(residues, 3 * inner), per_seq(residues, inner)),
        name="project",
        cost_estimate=pl.CostEstimate(flops=2**29, bytes_accessed=2**22, transcendentals=0),
    )(homolog_embedding, lookup_kernels, heads_sigmoid_kernel)
    homolog_refreshed, left, right = pl.pallas_call(
        functools.partial(attend_kernel, heads),
        grid=(seqs,),
        out_shape=(
            jax.ShapeDtypeStruct((seqs, residues, features), BF16),
            jax.ShapeDtypeStruct((seqs, residues, width), BF16),
            jax.ShapeDtypeStruct((seqs, width, residues), BF16),
        ),
        in_specs=[
            sspec(),
            per_seq(residues, features),
            per_seq(1, residues),
            per_seq(residues, 3 * inner),
            per_seq(residues, inner),
            whole(half_heads, residues, residues),
            whole(half_heads, residues, residues),
            whole(inner, features),
            whole(2 * width, features),
        ],
        out_specs=(
            per_seq(residues, features),
            per_seq(residues, width),
            per_seq(width, residues),
        ),
        name="attend",
        cost_estimate=pl.CostEstimate(flops=2**31, bytes_accessed=2**22, transcendentals=0),
    )(
        core,
        homolog_embedding,
        homolog_present.reshape(seqs, 1, residues),
        qkv,
        gates,
        own_bias,
        other_bias,
        heads_merge_kernel,
        tensor_halves_kernel.T,
    )

    span = seqs * width
    right_halves = right.reshape(span, 2, half).transpose(1, 0, 2)
    keep_halves = homolog_present.astype(BF16).reshape(seqs, 2, half).transpose(1, 0, 2)
    left_part = left.reshape(seqs, n, rows, width).transpose(1, 2, 0, 3).reshape(n, rows, span)
    extra = -(-(rows + seqs) // 16) * 16
    pad = jnp.zeros((n, extra - rows - seqs, half), BF16)

    def spread(parts):
        return jnp.broadcast_to(
            parts[None, :, None], (branch // 2, 2, dap) + parts.shape[1:]
        ).reshape((n,) + parts.shape[1:])

    message = jnp.concatenate([spread(right_halves), left_part, spread(keep_halves), pad], axis=1)
    own = exchange(message)
    other = swap(own)
    pair_next, edges = call(
        functools.partial(outer_kernel, seqs, width),
        (
            jax.ShapeDtypeStruct((rows, residues, channels), BF16),
            jax.ShapeDtypeStruct((2 * channels * rows, residues), BF16),
        ),
        (
            core,
            first_row.astype(jnp.int32).reshape(1),
            lax.dynamic_slice_in_dim(observed_position, first_row, rows, 0),
            own,
            other,
            couple_embedding,
            table,
            value_w,
            gate_w,
            observed_position.reshape(1, residues),
        ),
        [
            sheets(n * span, residues),
            VMEM((width * n * seqs, residues), BF16),
            sheets(n * extra, half),
            sheets(n * extra, residues),
            sheets(2 * channels * rows, residues),
        ],
        name="outer",
        in_specs=[sspec(), sspec(), sspec()] + [vspec()] * 7,
        flops=2**31,
    )

    received = exchange(edges.reshape(n, 2 * per * rows, residues))
    gate = call(
        close_gate_kernel,
        jax.ShapeDtypeStruct((rows, residues, channels), F32),
        (pair_next, closing_sigmoid_kernel),
        name="close_gate",
        flops=2**27,
    )
    if rows % 8 == 0:
        combined = call(
            functools.partial(triangle_kernel, per, rows),
            jax.ShapeDtypeStruct((n, per * rows, residues), BF16),
            (received,),
            [
                VMEM((n, 2 * per * rows, residues), F32),
                VMEM((n, per * rows, residues), F32),
            ],
            name="triangle",
            flops=2**28,
        )
    else:
        both = received.reshape(n, 2, per, rows, residues).transpose(1, 2, 0, 3, 4)
        both = both.reshape(2, per, residues, residues)
        combined = call(
            plain_triangle_kernel,
            jax.ShapeDtypeStruct((per, residues, residues), BF16),
            (both[0], both[1]),
            name="triangle",
            flops=2**28,
        )
        combined = combined.reshape(per, n, rows, residues).transpose(1, 0, 2, 3)
        combined = combined.reshape(n, per * rows, residues)
    combined = exchange(combined).reshape(channels * rows, residues)
    pair_output = call(
        close_kernel,
        jax.ShapeDtypeStruct((rows, residues, channels), BF16),
        (combined, pair_next, gate, closing_merge_kernel),
        [sheets(channels * rows, residues)],
        name="close",
        flops=2**27,
    )
    return (homolog_refreshed, pair_output)


def solution(mesh):
    split = P(EVERY, None, None)
    in_specs = (split, split, P(EVERY, None)) + (P(),) * 10
    return jax.shard_map(
        functools.partial(per_device, mesh.shape["branch"], mesh.shape["dap"]),
        mesh=mesh,
        in_specs=in_specs,
        out_specs=(split, split),
        check_vma=False,
    )
```

time: 373 us -> 155 us (0.42)
  waiting for transfers between devices: 177 us -> 11.3 us
  matrix products: 66.4 us -> 0 us
  Pallas kernels: 0 us -> 42.9 us
  local copies, waits for them, and re-layouts: 36.2 us -> 9.38 us
  blocking collectives: 69.1 us -> 82.9 us
  between operations: 14.1 us -> 0.77 us
    all_gather x3 -> x0, waiting for transfers between devices: 169 us -> none  [the longest x1 111 us: per_device(): lax.all_gather(right_edge, ('branch', 'dap'), axis=0, tiled=True)]
    all_to_all x0 -> x3, blocking collectives: none -> 82.9 us  [exchange(): lax.all_to_all(values, EVERY, split_axis=0, concat_axis=0, tiled=True)]
    all_gather x1 -> x0, blocking collectives: 69.1 us -> none  [per_device(): lax.all_gather(presence_indicators, ('branch', 'dap'), axis=0, tiled=True)]
    dot_general x28 -> x0, matrix products: 57.4 us -> none  [the longest x1 20.6 us: accumulate(): jnp.dot(projected_left, right_flat, precision=lax.Precision.HIGHEST)]
    pallas_call x0 -> x7, Pallas kernels: none -> 42.9 us  [the longest x5 29.5 us: call(): pl.pallas_call(body, out_shape=out, in_specs=in_specs or [vspec() for _ i...]
    all_gather x1 -> x0, local copies, waits for them, and re-layouts: 22.1 us -> none  [per_device(): lax.all_gather(right_edge, ('branch', 'dap'), axis=0, tiled=True)]
    sub x4 -> x0, matrix products: 9.02 us -> none  [row_update(): weights = jax.nn.softmax(logits, axis=-1).astype(jnp.bfloat16)]
    reshape x0 -> x7, local copies, waits for them, and re-layouts: none -> 4.23 us  [the longest x1 1.41 us: per_device(): tensor_merge_kernel.reshape(width, width, channels).transpose(1, 2, 0)]
  transfers between devices with their start and end apart: 5 -> 3, of which waited for: 3 -> 1; matrix products, arithmetic and copies ran while one was open for 3% -> 3% of each run, Pallas kernels for 0% -> 5%
where the time goes in v1:
time: 155 us; the launch traced here: 154 us
  blocking collectives  82.9 us (53%)
  Pallas kernels  42.9 us (28%)
  waiting for transfers between devices  11.3 us (7%)
  local copies, waits for them, and re-layouts  9.38 us (6%)
  starting transfers between devices  6.13 us (4%)
    all_to_all x3, blocking collectives, exchange(): lax.all_to_all(values, EVERY, split_axis=0, concat_axis=0, tiled=True)  82.9 us
    pallas_call x5, Pallas kernels, call(): pl.pallas_call(body, out_shape=out, in_specs=in_specs or [vspec() for _ i...  29.5 us
    all_to_all x1, waiting for transfers between devices, exchange(): lax.all_to_all(values, EVERY, split_axis=0, concat_axis=0, tiled=True)  11.3 us
    pallas_call x1, Pallas kernels, per_device(): pl.pallas_call(functools.partial(attend_kernel, heads), grid=(seqs,), out...  8.8 us
    pallas_call x1, Pallas kernels, per_device(): pl.pallas_call(project_kernel, grid=(seqs,), out_shape=(jax.ShapeDtypeStr...  4.64 us
    all_to_all x1, starting transfers between devices, exchange(): lax.all_to_all(values, EVERY, split_axis=0, concat_axis=0, tiled=True)  4.53 us
  transfers between devices with their start and end apart: 3, of which 1 were waited for; matrix products, arithmetic and copies ran while one was open for 3% of the time, Pallas kernels for 5%

profile of v1, /device:TPU:0, one launch (start us, length us, event | category | flops | bytes accessed | tf_op | source)
XLA Modules:
  0.0 153.7 jit_solution(16183137508169167123)
XLA Ops:
  0.6 2.8 %bias.1 = bf16[32,32,256]{2,1,0:T(8,128)(2,1)} custom-call(bf16[8,256,128]{2,1,0:T(8,128)(2,1)} %couple_ref.3, bf16[8,128]{1,0:T(8,128)(2,1)} %bitcast.50), custom_call_target="tpu_custom_call" | custom-call | bytes 1048576 | tf_op jit(solution)/shard_map/bias/pallas_call | solution.py:65
  3.4 21.6 %all_to_all.20 = bf16[32,32,256]{2,1,0:T(8,128)(2,1)S(1)} all-to-all(bf16[32,32,256]{2,1,0:T(8,128)(2,1)} %bias.1), channel_id=1, replica_groups=mesh['branch'=8,'dap'=4] {'branch','dap'}, dimensions={0} | all-to-all | bytes 1048576 | tf_op jit(solution)/shard_map/all_to_all | solution.py:303
  25.1 1.3 collective-permute-start
  26.4 0.6 reshape.64.keep_ref
  27.1 4.6 %project.1 = (bf16[4,256,768]{2,1,0:T(8,128)(2,1)}, f32[4,256,256]{2,1,0:T(8,128)}) custom-call(bf16[4,256,256]{2,1,0:T(8,128)(2,1)} %seq_ref.3, bf16[256,768]{1,0:T(8,128)(2,1)} %qkv_w_ref.1, bf16[256,256]{1,0:T(8,128)(2,1)} %gate_w_ref.1), custom_call_target="tpu_custom_call" | custom-call | flops 536870912 | bytes 4194304 | tf_op jit(solution)/shard_map/project/pallas_call | solution.py:335
  31.8 0.8 copy-done.7
  32.6 8.8 %attend.1 = (bf16[4,256,256]{2,1,0:T(8,128)(2,1)}, bf16[4,256,32]{2,1,0:T(8,128)(2,1)}, bf16[4,32,256]{2,1,0:T(8,128)(2,1)}) custom-call(s32[1]{0:T(128)} %bitcast.core_ref, bf16[4,256,256]{2,1,0:T(8,128)(2,1)} %seq_ref.3, s32[4,1,256]{2,1,0:T(1,128)} %reshape.64.keep_ref, bf16[4,256,768]{2,1,0:T(8,128)(2,1)} %get-tuple-element.9.qkv_ref, ...), custom_call_target="tpu_custom_call" | custom-call | flops 2147483648 | bytes 4194304 | tf_op jit(solution)/shard_map/attend/pallas_call | solution.py:351
  41.4 1.2 copy.32
  42.7 0.9 reshape.68
  43.8 0.3 maximum_maximum_fusion
  44.2 33.0 %all_to_all.21.own_ref = bf16[32,144,128]{2,1,0:T(8,128)(2,1)S(1)} all-to-all(bf16[32,144,128]{2,1,0:T(8,128)(2,1)S(1)} %maximum_maximum_fusion), channel_id=1, replica_groups=mesh['branch'=8,'dap'=4] {'branch','dap'}, dimensions={0} | all-to-all | bytes 2359296 | tf_op jit(solution)/shard_map/all_to_all | solution.py:303
  77.5 1.4 copy.26
  79.0 0.7 copy.28
  79.7 0.7 copy.29
  80.4 0.7 dynamic_slice.3.marks_ref
  81.0 1.0 copy-done.6
  82.0 18.5 %outer.1 = (bf16[8,256,128]{2,1,0:T(8,128)(2,1)}, bf16[2048,256]{1,0:T(8,128)(2,1)}) custom-call(s32[1]{0:T(128)} %bitcast.core_ref, s32[1]{0:T(128)} %bitcast.7.first_ref, s32[8]{0:T(128)} %dynamic_slice.3.marks_ref, bf16[32,144,128]{2,1,0:T(8,128)(2,1)} %copy-done.1, bf16[32,144,128]{2,1,0:T(8,128)(2,1)} %copy-done.6, bf16[8,256,128]{2,1,0:T(8,128)(2,1)} %couple_ref.3, ...), custom_call_target="tpu_custom_call" | custom-call | flops 2147483648 | bytes 1048576 | tf_op jit(solution)/shard_map/outer/pallas_call | solution.py:65
  100.5 28.3 %all_to_all.22.in_ref = bf16[32,64,256]{2,1,0:T(8,128)(2,1)} all-to-all(bf16[32,64,256]{2,1,0:T(8,128)(2,1)} %bitcast.41), channel_id=1, replica_groups=mesh['branch'=8,'dap'=4] {'branch','dap'}, dimensions={0} | all-to-all | bytes 2097152 | tf_op jit(solution)/shard_map/all_to_all | solution.py:303
  128.8 2.3 %triangle.1 = bf16[32,32,256]{2,1,0:T(8,128)(2,1)} custom-call(bf16[32,64,256]{2,1,0:T(8,128)(2,1)} %all_to_all.22.in_ref), custom_call_target="tpu_custom_call" | custom-call | flops 268435456 | bytes 1048576 | tf_op jit(solution)/shard_map/triangle/pallas_call | solution.py:65
  131.1 4.5 %all-to-all-start.3 = ((bf16[32,32,256]{2,1,0:T(8,128)(2,1)}), bf16[32,32,256]{2,1,0:T(8,128)(2,1)S(1)}, u32[]{:S(2)}, u32[]{:S(2)}) async-start(bf16[32,32,256]{2,1,0:T(8,128)(2,1)} %triangle.1), calls=%async_computation.3 | async-start | bytes 1048576 | tf_op jit(solution)/shard_map/all_to_all | solution.py:303
  135.7 2.9 %close_gate.1.gate_ref = f32[8,256,128]{2,1,0:T(8,128)} custom-call(bf16[8,256,128]{2,1,0:T(8,128)(2,1)} %get-tuple-element.15.pair_ref, bf16[128,128]{1,0:T(8,128)(2,1)} %weight_ref.2), custom_call_target="tpu_custom_call" | custom-call | flops 134217728 | bytes 1048576 | tf_op jit(solution)/shard_map/close_gate/pallas_call | solution.py:65
  138.6 11.3 %all-to-all-done.3 = bf16[32,32,256]{2,1,0:T(8,128)(2,1)S(1)} async-done(((bf16[32,32,256]{2,1,0:T(8,128)(2,1)}), bf16[32,32,256]{2,1,0:T(8,128)(2,1)S(1)}, u32[]{:S(2)}, u32[]{:S(2)}) %all-to-all-start.3) | async-done | bytes 524320 | tf_op jit(solution)/shard_map/all_to_all | solution.py:303
  149.9 0.8 copy-done
  150.7 2.9 %close.1 = bf16[8,256,128]{2,1,0:T(8,128)(2,1)} custom-call(bf16[1024,256]{1,0:T(8,128)(2,1)} %bitcast.38, bf16[8,256,128]{2,1,0:T(8,128)(2,1)} %get-tuple-element.15.pair_ref, f32[8,256,128]{2,1,0:T(8,128)} %close_gate.1.gate_ref, bf16[128,128]{1,0:T(8,128)(2,1)} %weight_ref.3), custom_call_target="tpu_custom_call" | custom-call | flops 134217728 | bytes 1048576 | tf_op jit(solution)/shard_map/close/pallas_call | solution.py:65
  (30 shorter events, 1.0 us)
Async XLA Ops:
  0.6 25.8 %copy-start.5 = (s32[4,256]{1,0:T(4,128)S(1)}, s32[4,256]{1,0:T(4,128)}, u32[]{:S(2)}) copy-start(s32[4,256]{1,0:T(4,128)} %param.15) | copy-start | bytes 12292
  25.0 6.7 %copy-start.2 = (bf16[4,256,256]{2,1,0:T(8,128)(2,1)}, bf16[4,256,256]{2,1,0:T(8,128)(2,1)S(1)}, u32[]{:S(2)}) copy-start(bf16[4,256,256]{2,1,0:T(8,128)(2,1)S(1)} %copy_bitcast_fusion.own_ref) | copy-start | bytes 1572868
  25.1 6.7 %collective-permute-start = (bf16[4,256,256]{2,1,0:T(8,128)(2,1)S(1)}, bf16[4,256,256]{2,1,0:T(8,128)(2,1)S(1)}, u32[]{:S(2)}, u32[]{:S(2)}) collective-permute-start(bf16[4,256,256]{2,1,0:T(8,128)(2,1)S(1)} %copy_bitcast_fusion.own_ref), channel_id=1, source_target_pairs={{0,4},{4,0},{8,12},{12,8},{16,20},{20,16},{24,28},{28,24},{1,5},{5... | collective-permute-start | bytes 1572872 | tf_op jit(solution)/shard_map/ppermute | solution.py:306
  31.8 0.8 copy-start.7
  44.1 33.3 %copy-start.3 = (bf16[1024,128]{1,0:T(8,128)(2,1)S(1)}, bf16[1024,128]{1,0:T(8,128)(2,1)}, u32[]{:S(2)}) copy-start(bf16[1024,128]{1,0:T(8,128)(2,1)} %param.22) | copy-start | bytes 786436
  44.2 34.7 %copy-start.4 = (bf16[128,512]{1,0:T(8,128)(2,1)S(1)}, bf16[128,512]{1,0:T(8,128)(2,1)}, u32[]{:S(2)}) copy-start(bf16[128,512]{1,0:T(8,128)(2,1)} %param.23) | copy-start | bytes 393220
  77.2 3.8 %copy-start.1 = (bf16[32,144,128]{2,1,0:T(8,128)(2,1)}, bf16[32,144,128]{2,1,0:T(8,128)(2,1)S(1)}, u32[]{:S(2)}) copy-start(bf16[32,144,128]{2,1,0:T(8,128)(2,1)S(1)} %all_to_all.21.own_ref) | copy-start | bytes 3538948
  77.2 3.2 %copy-start.8 = (s32[256]{0:T(256)S(1)}, s32[256]{0:T(256)}, u32[]{:S(2)}) copy-start(s32[256]{0:T(256)} %param.16) | copy-start | bytes 3076
  77.2 3.8 %collective-permute-start.1 = (bf16[32,144,128]{2,1,0:T(8,128)(2,1)S(1)}, bf16[32,144,128]{2,1,0:T(8,128)(2,1)S(1)}, u32[]{:S(2)}, u32[]{:S(2)}) collective-permute-start(bf16[32,144,128]{2,1,0:T(8,128)(2,1)S(1)} %all_to_all.21.own_ref), channel_id=1, source_target_pairs={{0,4},{4,0},{8,12},{12,8},{16,20},{20,16},{24,28},{28,24},{1,5},{5... | collective-permute-start | bytes 3538952 | tf_op jit(solution)/shard_map/ppermute | solution.py:306
  81.0 1.0 copy-start.6
  131.1 18.8 %all-to-all-start.3 = ((bf16[32,32,256]{2,1,0:T(8,128)(2,1)}), bf16[32,32,256]{2,1,0:T(8,128)(2,1)S(1)}, u32[]{:S(2)}, u32[]{:S(2)}) async-start(bf16[32,32,256]{2,1,0:T(8,128)(2,1)} %triangle.1), calls=%async_computation.3 | async-start | bytes 1048576 | tf_op jit(solution)/shard_map/all_to_all | solution.py:303
  149.9 0.8 copy-start

commit v2 on v1

v2 whole, which is shorter than its diff:
```python
import functools

import jax
import jax.numpy as jnp
from jax import lax
from jax.experimental import pallas as pl
from jax.experimental.pallas import tpu as pltpu
from jax.sharding import PartitionSpec as P


EPSILON = 1e-05
EVERY = ("branch", "dap")
VMEM = pltpu.VMEM
F32 = jnp.float32
BF16 = jnp.bfloat16

NT = (((1,), (1,)), ((), ()))
TN = (((0,), (0,)), ((), ()))
NN = (((1,), (0,)), ((), ()))


def mm(a, b, dims=NN):
    return lax.dot_general(a, b, dims, preferred_element_type=F32)


def normalize(values, axis=-1):
    values = values.astype(F32)
    centred = values - jnp.mean(values, axis=axis, keepdims=True)
    spread = jnp.mean(centred * centred, axis=axis, keepdims=True)
    return centred * lax.rsqrt(spread + EPSILON)


def vspec():
    return pl.BlockSpec(memory_space=VMEM)


def sspec():
    return pl.BlockSpec(memory_space=pltpu.SMEM)


LANES = 128


def sheets(rows, columns):
    return VMEM((columns // LANES, rows, LANES), F32)


def put(scr, start, values, stride):
    for k in range(scr.shape[0]):
        part = values[:, k * LANES : (k + 1) * LANES]
        scr[k, pl.ds(start, values.shape[0], stride=stride), :] = part


def take(scr, start, count, stride=1):
    parts = [scr[k, pl.ds(start, count, stride=stride), :] for k in range(scr.shape[0])]
    return parts[0] if len(parts) == 1 else jnp.concatenate(parts, axis=1)


def fill(scr, values):
    for k in range(scr.shape[0]):
        scr[k] = values[:, k * LANES : (k + 1) * LANES]


def call(body, out, args, scratch=(), in_specs=None, flops=0, **kw):
    single = not isinstance(out, (tuple, list))
    return pl.pallas_call(
        body,
        out_shape=out,
        in_specs=in_specs or [vspec() for _ in args],
        out_specs=vspec() if single else tuple(vspec() for _ in out),
        scratch_shapes=list(scratch),
        cost_estimate=pl.CostEstimate(flops=flops, bytes_accessed=2**20, transcendentals=0),
        **kw,
    )(*args)


def sigmoid(values):
    return 0.5 * jnp.tanh(0.5 * values) + 0.5


def bias_kernel(cores, side_ref, couple_ref, weight_ref, out_ref, mine_ref, theirs_ref, scr):
    rows, residues, _ = couple_ref.shape
    heads = weight_ref.shape[0]
    half = residues // 2
    mine = pl.multiple_of(side_ref[0] * half, half)
    theirs = pl.multiple_of((1 - side_ref[0]) * half, half)
    for i in range(rows):
        normed = normalize(couple_ref[i]).astype(BF16)
        put(scr, i, mm(weight_ref[...], normed, NT), rows)
        mine_ref[i] = couple_ref[i, pl.ds(mine, half), :]
        theirs_ref[i] = couple_ref[i, pl.ds(theirs, half), :]
    part = heads // 2 * rows
    halves = [take(scr, k * part, part).astype(BF16) for k in range(2)]
    for t, core in enumerate(cores):
        out_ref[t] = halves[core]


def prepare_kernel(
    seqs, per, merge_ref, entry_ref, halves_ref, table_ref, value_ref, gate_ref, left_ref, right_ref,
    merge_scr, entry_scr, edge_scr,
):
    channels = merge_ref.shape[1]
    width = halves_ref.shape[0] // 2
    part = width // 2
    merge_scr[...] = merge_ref[...].astype(F32)
    for k in range(2):
        rows = [merge_scr[pl.ds(k * part + q, width, stride=width), :] for q in range(part)]
        table_ref[k] = jnp.concatenate(rows, axis=0).T.astype(BF16)
    for k in range(4):
        entry_scr[k * channels : (k + 1) * channels, :] = (
            entry_ref[:, k * channels : (k + 1) * channels].astype(F32).T
        )
    for kind, ref in enumerate((value_ref, gate_ref)):
        for k in range(2):
            for c in range(per):
                at = (2 * k + kind) * channels + c
                edge_scr[pl.ds(k * per + c, channels // per, stride=2 * per), :] = entry_scr[
                    pl.ds(at, channels // per, stride=per), :
                ]
        ref[...] = edge_scr[...].astype(BF16)
    left = halves_ref[:width].astype(F32).T.astype(BF16)
    for s in range(seqs):
        parts = [left if u == s else jnp.zeros_like(left) for u in range(seqs)]
        left_ref[s] = jnp.concatenate(parts, axis=1)
    right_ref[...] = halves_ref[width:]


def project_kernel(heads, seq_ref, qkv_w_ref, gate_w_ref, logit_ref, value_ref, gate_ref):
    residues = seq_ref.shape[1]
    inner = gate_w_ref.shape[1]
    head_width = inner // heads
    normed = normalize(seq_ref[0]).astype(BF16)
    projected = mm(normed, qkv_w_ref[...]).astype(BF16)
    queries = projected[:, :inner]
    key_rows = projected[:, inner : 2 * inner]
    value_ref[0] = projected[:, 2 * inner :]
    gate_ref[0] = sigmoid(mm(normed, gate_w_ref[...]))
    lane = lax.broadcasted_iota(jnp.int32, (residues, inner), 1) // head_width
    for h in range(heads):
        keys = jnp.where(lane == h, key_rows, jnp.zeros((), BF16))
        logit_ref[0, h] = mm(queries, keys, NT) * head_width ** (-0.5)


def attend_kernel(
    heads,
    places,
    core_ref,
    seq_ref,
    keep_ref,
    logit_ref,
    value_ref,
    gate_ref,
    own_ref,
    other_ref,
    merge_ref,
    left_w_ref,
    right_w_ref,
    new_ref,
    message_ref,
    left_scr,
):
    s = pl.program_id(0)
    seqs = keep_ref.shape[0]
    core = core_ref[0]
    inner = gate_ref.shape[2]
    residues = gate_ref.shape[1]
    head_width = inner // heads
    half = inner // 2
    value_rows = value_ref[0]
    keep = keep_ref[pl.ds(s, 1), :]
    masking = jnp.where(keep == 1, 0.0, -1000000000.0).astype(F32)
    lane_half = lax.broadcasted_iota(jnp.int32, (residues, half), 1) // head_width
    zero = jnp.zeros((), BF16)
    mixed = []
    for bias_ref, group in ((own_ref, core), (other_ref, 1 - core)):
        values = jnp.where(group == 0, value_rows[:, :half], value_rows[:, half:])
        total = jnp.zeros((residues, inner), F32)
        for h in range(heads // 2):
            head = group * (heads // 2) + h
            logits = logit_ref[0, head] + bias_ref[h].astype(F32) + masking
            top = jnp.max(logits, axis=-1, keepdims=True)
            weights = jnp.exp(logits - top).astype(BF16)
            mine = lane_half == h
            table = jnp.concatenate(
                [
                    jnp.where(mine, values, zero),
                    jnp.where(mine, jnp.ones((), BF16), zero),
                ],
                axis=1,
            )
            total = total + mm(weights, table)
        mixed.append(total[:, :half] / total[:, half:])
    first = jnp.where(core == 0, mixed[0], mixed[1])
    second = jnp.where(core == 0, mixed[1], mixed[0])
    attended = (jnp.concatenate([first, second], axis=1) * gate_ref[0]).astype(BF16)
    updated = (seq_ref[0].astype(F32) + mm(attended, merge_ref[...])).astype(BF16)
    new_ref[0] = updated
    normed = normalize(updated).astype(BF16)
    present = keep.astype(F32)
    width = right_w_ref.shape[0]
    part = width // 2
    columns = message_ref.shape[2]
    span = seqs * part
    right = (mm(right_w_ref[...], normed, NT) * present).astype(BF16)
    at = pl.multiple_of(s * part, part)
    for t, (core_of, side, _) in enumerate(places):
        message_ref[t, pl.ds(at, part), :] = right[
            core_of * part : (core_of + 1) * part, side * columns : (side + 1) * columns
        ]
    present_column = jnp.broadcast_to(present, (8, residues)).T[:, :1]
    left = mm(normed, left_w_ref[s]) * present_column

    @pl.when(s == 0)
    def _():
        left_scr[...] = left

    @pl.when(s > 0)
    def _():
        left_scr[...] += left

    @pl.when(s == seqs - 1)
    def _():
        rows = residues // len(places)
        marks = keep_ref[...].astype(F32)
        marks = jnp.concatenate(
            [marks[:, k * columns : (k + 1) * columns] for k in range(2)], axis=0
        ).astype(BF16)
        for t, (_, _, mate) in enumerate(places):
            block = jnp.concatenate(
                [left_scr[u * rows : (u + 1) * rows, :] for u in (t, mate)], axis=0
            )
            message_ref[t, span : span + 2 * rows, :] = block.astype(BF16)
            message_ref[t, span + 2 * rows :, :] = marks


def outer_kernel(
    seqs,
    width,
    core_ref,
    side_ref,
    first_mine_ref,
    first_theirs_ref,
    marks_ref,
    own_ref,
    other_ref,
    couple_mine_ref,
    couple_theirs_ref,
    table_ref,
    value_w_ref,
    gate_w_ref,
    observed_ref,
    pair_mine_ref,
    pair_theirs_ref,
    edges_ref,
    right_scr,
    small_scr,
    products,
    edge_scr,
):
    n = own_ref.shape[0]
    rows, columns, channels = couple_mine_ref.shape
    block = 2 * rows
    part = width // 2
    span = seqs * part
    total_seqs = n * seqs
    core, side = core_ref[0], side_ref[0]
    first_mine, first_theirs = first_mine_ref[0], first_theirs_ref[0]

    extra = own_ref.shape[1] - span
    small_scr[...] = own_ref[:, span:, :].astype(F32).reshape(n * extra, columns)
    left_rows = []
    for i in range(block):
        piece = small_scr[pl.ds(i, n, stride=extra), :]
        for s in range(seqs):
            left_rows.append(piece[:, s * width : (s + 1) * width])
    left_all = jnp.concatenate(left_rows, axis=0).T
    left = jnp.concatenate(
        [left_all[:, i * total_seqs : (i + 1) * total_seqs] for i in range(block)], axis=0
    ).astype(BF16)
    keep_halves = []
    for k in range(2):
        at = block + k * seqs
        keep_halves.append(
            jnp.concatenate(
                [small_scr[pl.ds(at + s, n, stride=extra), :] for s in range(seqs)], axis=0
            )
        )
    keep_columns = jnp.where(side == 0, keep_halves[0], keep_halves[1]).astype(BF16)
    keep = jnp.concatenate(keep_halves, axis=1).astype(BF16)
    pad = -(-block // 8) * 8
    order = lax.broadcasted_iota(jnp.int32, (pad, 2 * columns), 0)
    row_ids = jnp.where(order < rows, first_mine + order, first_theirs + order - rows)
    chosen = (row_ids == lax.broadcasted_iota(jnp.int32, (pad, 2 * columns), 1)).astype(BF16)
    counts = mm(mm(chosen, keep, NT).astype(BF16), keep_columns)
    scale = 1.0 / jnp.maximum(counts, 1.0)

    for k, ref in enumerate((own_ref, other_ref)):
        right_scr[...] = ref[:, :span, :].astype(F32).reshape(n * span, columns)
        for q in range(0, part, 2):
            pair = [
                jnp.concatenate(
                    [
                        right_scr[pl.ds(s * part + q + d, n, stride=span), :]
                        for s in range(seqs)
                    ],
                    axis=0,
                ).astype(BF16)
                for d in range(2)
            ]
            outer = mm(left, jnp.concatenate(pair, axis=1)).astype(BF16)
            for d in range(2):
                at = (k * part + q + d) * width
                for i in range(block):
                    products[i, at : at + width, :] = outer[
                        i * width : (i + 1) * width, d * columns : (d + 1) * columns
                    ]
    table = jnp.concatenate([table_ref[core], table_ref[1 - core]], axis=1)
    half = pl.multiple_of(side * columns, columns)
    observed = observed_ref[:, pl.ds(half, columns)].astype(F32)
    row_marks = [marks_ref[first_mine + r] for r in range(rows)]
    row_marks += [marks_ref[first_theirs + r] for r in range(rows)]
    for i in range(0, block, 2):
        update = mm(table, jnp.concatenate([products[i], products[i + 1]], axis=1))
        normed = []
        for d in range(2):
            piece = update[:, d * columns : (d + 1) * columns] * scale[i + d : i + d + 1, :]
            couple_ref, pair_ref = (
                (couple_mine_ref, pair_mine_ref)
                if i + d < rows
                else (couple_theirs_ref, pair_theirs_ref)
            )
            r = (i + d) % rows
            pair = (couple_ref[r].astype(F32) + piece.T).astype(BF16)
            pair_ref[r] = pair
            normed.append(normalize(pair).astype(BF16))
        normed = jnp.concatenate(normed, axis=0)
        edge = mm(value_w_ref[...], normed, NT) * sigmoid(mm(gate_w_ref[...], normed, NT))
        for d in range(2):
            mark = observed * row_marks[i + d].astype(F32)
            edge_scr[pl.ds(i + d, 2 * channels, stride=block), :] = (
                edge[:, d * columns : (d + 1) * columns] * mark
            )
    edges_ref[...] = edge_scr[...].astype(BF16)


def close_gate_kernel(mine_ref, theirs_ref, weight_ref, mine_gate_ref, theirs_gate_ref):
    for pair_ref, gate_ref in ((mine_ref, mine_gate_ref), (theirs_ref, theirs_gate_ref)):
        for i in range(pair_ref.shape[0]):
            normed = normalize(pair_ref[i]).astype(BF16)
            gate_ref[i] = sigmoid(mm(normed, weight_ref[...]))


def triangle_kernel(per, rows, places, in_ref, out_ref, in_scr, out_scr):
    n = in_ref.shape[0]
    residues = n * rows
    in_scr[...] = in_ref[...].astype(F32)

    def whole(at):
        tiles = []
        for t, (_, side, mate) in enumerate(places):
            pair = []
            for k in range(2):
                source, shift = (t, 0) if side == k else (mate, rows)
                pair.append(in_scr[source, at + shift : at + shift + rows, :])
            tiles.append(jnp.concatenate(pair, axis=1))
        return jnp.concatenate(tiles, axis=0).astype(BF16)

    for c in range(per):
        left = whole(c * 2 * rows)
        right = whole((per + c) * 2 * rows)
        out_scr[:, c * rows : (c + 1) * rows, :] = mm(left, right, NT).reshape(n, rows, residues)
    out_ref[...] = out_scr[...].astype(BF16)


def plain_triangle_kernel(left_ref, right_ref, out_ref):
    for c in range(left_ref.shape[0]):
        out_ref[c] = mm(left_ref[c], right_ref[c], NT).astype(BF16)


def close_kernel(
    side_ref, in_ref, mine_ref, theirs_ref, mine_gate_ref, theirs_gate_ref, weight_ref, out_ref, scr
):
    rows, columns, channels = mine_ref.shape
    fill(scr, in_ref[...].astype(F32))
    side = side_ref[0]
    for half, pair_ref, gate_ref in (
        (side, mine_ref, mine_gate_ref),
        (1 - side, theirs_ref, theirs_gate_ref),
    ):
        at = pl.multiple_of(half * columns, columns)
        for i in range(rows):
            piece = scr[half, pl.ds(i, channels, stride=rows), :]
            update = mm(normalize(piece, axis=0).astype(BF16), weight_ref[...], TN)
            out_ref[i, pl.ds(at, columns), :] = (
                pair_ref[i].astype(F32) + gate_ref[i] * update
            ).astype(BF16)


def per_device(
    branch,
    dap,
    homolog_embedding,
    couple_embedding,
    homolog_present,
    observed_position,
    couple_logit_kernel,
    lookup_kernels,
    heads_sigmoid_kernel,
    heads_merge_kernel,
    tensor_halves_kernel,
    tensor_merge_kernel,
    edge_entry_kernel,
    closing_sigmoid_kernel,
    closing_merge_kernel,
):
    n = branch * dap
    rows, residues, channels = couple_embedding.shape
    seqs = homolog_embedding.shape[0]
    features = homolog_embedding.shape[2]
    heads = couple_logit_kernel.shape[1]
    inner = heads_sigmoid_kernel.shape[1]
    width = tensor_halves_kernel.shape[1] // 2
    per = channels // n
    half = residues // 2
    block = 2 * rows
    places = [((t // dap) % 2, (t // dap // 2) % 2, (t // dap ^ 2) * dap + t % dap) for t in range(n)]
    me = lax.axis_index("branch").astype(jnp.int32)
    core = (me % 2).reshape(1)
    side = (me // 2 % 2).reshape(1)
    place = lax.axis_index("dap").astype(jnp.int32)
    first_mine = (me * dap + place) * rows
    first_theirs = ((me ^ 2) * dap + place) * rows
    chip = [(b, b ^ 1) for b in range(branch)]
    across = [(b, b ^ 2) for b in range(branch)]

    def exchange(values):
        return lax.all_to_all(values, EVERY, split_axis=0, concat_axis=0, tiled=True)

    def permute(values, pairs):
        return lax.ppermute(values, "branch", pairs)

    table, value_w, gate_w, left_w, right_w = call(
        functools.partial(prepare_kernel, seqs, per),
        (
            jax.ShapeDtypeStruct((2, channels, width // 2 * width), BF16),
            jax.ShapeDtypeStruct((2 * channels, channels), BF16),
            jax.ShapeDtypeStruct((2 * channels, channels), BF16),
            jax.ShapeDtypeStruct((seqs, features, seqs * width), BF16),
            jax.ShapeDtypeStruct((width, features), BF16),
        ),
        (tensor_merge_kernel, edge_entry_kernel, tensor_halves_kernel.T),
        [
            VMEM((width * width, channels), F32),
            VMEM((4 * channels, channels), F32),
            VMEM((2 * channels, channels), F32),
        ],
    )

    half_heads = heads // 2
    message, couple_mine, couple_send = call(
        functools.partial(bias_kernel, [place[0] for place in places]),
        (
            jax.ShapeDtypeStruct((n, half_heads * rows, residues), BF16),
            jax.ShapeDtypeStruct((rows, half, channels), BF16),
            jax.ShapeDtypeStruct((rows, half, channels), BF16),
        ),
        (side, couple_embedding, couple_logit_kernel.T),
        [sheets(heads * rows, residues)],
        in_specs=[sspec(), vspec(), vspec()],
    )
    own_bias = exchange(message).reshape(n, half_heads, rows, residues)
    own_bias = own_bias.transpose(1, 0, 2, 3).reshape(half_heads, residues, residues)
    other_bias = permute(own_bias, chip)
    couple_theirs = permute(couple_send, across)

    def whole(*shape):
        return pl.BlockSpec(shape, lambda s: (0,) * len(shape))

    def per_seq(*shape):
        return pl.BlockSpec((1, *shape), lambda s: (s,) + (0,) * len(shape))

    logits, values, gates = pl.pallas_call(
        functools.partial(project_kernel, heads),
        grid=(seqs,),
        out_shape=(
            jax.ShapeDtypeStruct((seqs, heads, residues, residues), F32),
            jax.ShapeDtypeStruct((seqs, residues, inner), BF16),
            jax.ShapeDtypeStruct((seqs, residues, inner), F32),
        ),
        in_specs=[per_seq(residues, features), whole(features, 3 * inner), whole(features, inner)],
        out_specs=(
            per_seq(heads, residues, residues),
            per_seq(residues, inner),
            per_seq(residues, inner),
        ),
        name="project",
        cost_estimate=pl.CostEstimate(flops=2**29, bytes_accessed=2**22, transcendentals=0),
    )(homolog_embedding, lookup_kernels, heads_sigmoid_kernel)
    span = seqs * width // 2
    depth = span + block + 2 * seqs
    homolog_refreshed, message = pl.pallas_call(
        functools.partial(attend_kernel, heads, places),
        grid=(seqs,),
        out_shape=(
            jax.ShapeDtypeStruct((seqs, residues, features), BF16),
            jax.ShapeDtypeStruct((n, depth, half), BF16),
        ),
        in_specs=[
            sspec(),
            per_seq(residues, features),
            whole(seqs, residues),
            per_seq(heads, residues, residues),
            per_seq(residues, inner),
            per_seq(residues, inner),
            whole(half_heads, residues, residues),
            whole(half_heads, residues, residues),
            whole(inner, features),
            whole(seqs, features, seqs * width),
            whole(width, features),
        ],
        out_specs=(per_seq(residues, features), whole(n, depth, half)),
        scratch_shapes=[VMEM((residues, seqs * width), F32)],
        name="attend",
        cost_estimate=pl.CostEstimate(flops=2**31, bytes_accessed=2**22, transcendentals=0),
    )(
        core,
        homolog_embedding,
        homolog_present,
        logits,
        values,
        gates,
        own_bias,
        other_bias,
        heads_merge_kernel,
        left_w,
        right_w,
    )

    own = exchange(message)
    other = permute(own, chip)
    piece = jax.ShapeDtypeStruct((rows, half, channels), BF16)
    pair_mine, pair_send, edges = call(
        functools.partial(outer_kernel, seqs, width),
        (piece, piece, jax.ShapeDtypeStruct((2 * channels * block, half), BF16)),
        (
            core,
            side,
            first_mine.reshape(1),
            first_theirs.reshape(1),
            observed_position,
            own,
            other,
            couple_mine,
            couple_theirs,
            table,
            value_w,
            gate_w,
            observed_position.reshape(1, residues),
        ),
        [
            VMEM((n * span, half), F32),
            VMEM((n * (depth - span), half), F32),
            VMEM((block, width * width, half), BF16),
            VMEM((2 * channels * block, half), F32),
        ],
        in_specs=[sspec()] * 5 + [vspec()] * 8,
        flops=2**31,
    )

    received = exchange(edges.reshape(n, 2 * per * block, half))
    pair_theirs = permute(pair_send, across)
    gate_piece = jax.ShapeDtypeStruct((rows, half, channels), F32)
    gate_mine, gate_theirs = call(
        close_gate_kernel,
        (gate_piece, gate_piece),
        (pair_mine, pair_theirs, closing_sigmoid_kernel),
        flops=2**27,
    )
    if rows % 8 == 0:
        combined = call(
            functools.partial(triangle_kernel, per, rows, places),
            jax.ShapeDtypeStruct((n, per * rows, residues), BF16),
            (received,),
            [
                VMEM((n, 2 * per * block, half), F32),
                VMEM((n, per * rows, residues), F32),
            ],
            flops=2**28,
        )
    else:
        both = received.reshape(branch // 4, 2, 2, dap, 2, per, 2, rows, half)
        both = jnp.stack([both[:, 0], both[:, 1, :, :, :, :, ::-1]], axis=1)
        both = both.transpose(4, 5, 0, 6, 2, 3, 7, 1, 8).reshape(2, per, residues, residues)
        combined = call(
            plain_triangle_kernel,
            jax.ShapeDtypeStruct((per, residues, residues), BF16),
            (both[0], both[1]),
            flops=2**28,
        )
        combined = combined.reshape(per, n, rows, residues).transpose(1, 0, 2, 3)
        combined = combined.reshape(n, per * rows, residues)
    combined = exchange(combined).reshape(channels * rows, residues)
    pair_output = call(
        close_kernel,
        jax.ShapeDtypeStruct((rows, residues, channels), BF16),
        (side, combined, pair_mine, pair_theirs, gate_mine, gate_theirs, closing_merge_kernel),
        [sheets(channels * rows, residues)],
        in_specs=[sspec()] + [vspec()] * 6,
        flops=2**27,
    )
    return (homolog_refreshed, pair_output)


def solution(mesh):
    split = P(EVERY, None, None)
    in_specs = (split, split, P(EVERY, None)) + (P(),) * 10

    def body(*args):
        return per_device(mesh.shape["branch"], mesh.shape["dap"], *args)

    return jax.shard_map(
        body, mesh=mesh, in_specs=in_specs, out_specs=(split, split), check_vma=False
    )
```

time: 155 us -> 141 us (0.910)
  blocking collectives: 82.9 us -> 71.1 us
  waiting for transfers between devices: 11.3 us -> 18.3 us
  Pallas kernels: 42.9 us -> 36.3 us
  local copies, waits for them, and re-layouts: 9.38 us -> 3.29 us
  starting transfers between devices: 6.13 us -> 10.7 us
    ppermute x2 -> x4, waiting for transfers between devices: 0.01 us -> 18.3 us  [permute(): return lax.ppermute(values, 'branch', pairs)]
    all_to_all x3, blocking collectives: 82.9 us -> 71.1 us  [exchange(): lax.all_to_all(values, EVERY, split_axis=0, concat_axis=0, tiled=True)]
    all_to_all x1, waiting for transfers between devices: 11.3 us -> 0.01 us  [exchange(): lax.all_to_all(values, EVERY, split_axis=0, concat_axis=0, tiled=True)]
    pallas_call x5 -> x6, Pallas kernels: 29.5 us -> 20.6 us  [call(): pl.pallas_call(body, out_shape=out, in_specs=in_specs or [vspec() for _ i...]
    ppermute x2 -> x4, starting transfers between devices: 1.6 us -> 6.19 us  [permute(): return lax.ppermute(values, 'branch', pairs)]
    reshape x6 -> x0, local copies, waits for them, and re-layouts: 4.2 us -> none  [the longest x1 1.41 us: per_device(): tensor_merge_kernel.reshape(width, width, channels).transpose(1, 2, 0)]
    pallas_call x2, Pallas kernels: 13.4 us -> 15.7 us  [the longest x1 9.21 us: per_device(): pl.pallas_call(functools.partial(attend_kernel, heads, places), grid=(seq...]
    unnamed x19 -> x16, local copies, waits for them, and re-layouts: 2.79 us -> 3.26 us
  transfers between devices with their start and end apart: 3 -> 5, of which waited for: 1 -> 2; matrix products, arithmetic and copies ran while one was open for 3% -> 0% of each run, Pallas kernels for 5% -> 8%
where the time goes in v2:
time: 141 us
  blocking collectives  71.1 us (50%)
  Pallas kernels  36.3 us (26%)
  waiting for transfers between devices  18.3 us (13%)
  starting transfers between devices  10.7 us (8%)
  local copies, waits for them, and re-layouts  3.29 us (2%)
    all_to_all x3, blocking collectives, exchange(): lax.all_to_all(values, EVERY, split_axis=0, concat_axis=0, tiled=True)  71.1 us
    pallas_call x6, Pallas kernels, call(): pl.pallas_call(body, out_shape=out, in_specs=in_specs or [vspec() for _ i...  20.6 us
    ppermute x4, waiting for transfers between devices, permute(): return lax.ppermute(values, 'branch', pairs)  18.3 us
    pallas_call x1, Pallas kernels, per_device(): pl.pallas_call(functools.partial(attend_kernel, heads, places), grid=(seq...  9.21 us
    pallas_call x1, Pallas kernels, per_device(): pl.pallas_call(functools.partial(project_kernel, heads), grid=(seqs,), ou...  6.5 us
    ppermute x4, starting transfers between devices, permute(): return lax.ppermute(values, 'branch', pairs)  6.19 us
    all_to_all x1, starting transfers between devices, exchange(): lax.all_to_all(values, EVERY, split_axis=0, concat_axis=0, tiled=True)  4.55 us
    unnamed x16, local copies, waits for them, and re-layouts  3.26 us
  transfers between devices with their start and end apart: 5, of which 2 were waited for; matrix products, arithmetic and copies ran while one was open for 0% of the time, Pallas kernels for 8%

profile of v2, /device:TPU:0, one launch (start us, length us, event | category | flops | bytes accessed | tf_op | source)
XLA Modules:
  0.0 140.5 jit_solution(13944030790290472261)
XLA Ops:
  0.7 2.8 %shard_map.140 = (bf16[32,32,256]{2,1,0:T(8,128)(2,1)}, bf16[8,128,128]{2,1,0:T(8,128)(2,1)}, bf16[8,128,128]{2,1,0:T(8,128)(2,1)}) custom-call(s32[1]{0:T(128)} %bitcast.1.side_ref, bf16[8,256,128]{2,1,0:T(8,128)(2,1)} %couple_ref.1, bf16[8,128]{1,0:T(8,128)(2,1)} %bitcast.19), custom_call_target="tpu_custom_call" | custom-call | bytes 1048576 | tf_op jit(solution)/shard_map/pallas_call | solution.py:66
  3.5 21.6 %all_to_all.20 = bf16[32,32,256]{2,1,0:T(8,128)(2,1)S(1)} all-to-all(bf16[32,32,256]{2,1,0:T(8,128)(2,1)} %get-tuple-element.23), channel_id=1, replica_groups=mesh['branch'=8,'dap'=4] {'branch','dap'}, dimensions={0} | all-to-all | bytes 1048576 | tf_op jit(solution)/shard_map/all_to_all | solution.py:437
  25.1 1.3 collective-permute-start
  26.5 2.3 %shard_map.141 = (bf16[2,128,512]{2,1,0:T(8,128)(2,1)}, bf16[256,128]{1,0:T(8,128)(2,1)}, bf16[256,128]{1,0:T(8,128)(2,1)}, bf16[4,256,128]{2,1,0:T(8,128)(2,1)}, bf16[32,256]{1,0:T(8,128)(2,1)}) custom-call(bf16[1024,128]{1,0:T(8,128)(2,1)} %merge_ref.2, bf16[128,512]{1,0:T(8,128)(2,1)} %entry_ref.1, bf16[64,256]{1,0:T(8,128)(2,1)} %bitcast.18), custom_call_target="tpu_custom_call" | custom-call | bytes 1048576 | tf_op jit(solution)/shard_map/pallas_call | solution.py:66
  28.8 6.5 %project.1 = (f32[4,8,256,256]{3,2,1,0:T(8,128)}, bf16[4,256,256]{2,1,0:T(8,128)(2,1)}, f32[4,256,256]{2,1,0:T(8,128)}) custom-call(bf16[4,256,256]{2,1,0:T(8,128)(2,1)} %seq_ref.3, bf16[256,768]{1,0:T(8,128)(2,1)} %qkv_w_ref.1, bf16[256,256]{1,0:T(8,128)(2,1)} %gate_w_ref.1), custom_call_target="tpu_custom_call" | custom-call | flops 536870912 | bytes 4194304 | tf_op jit(solution)/shard_map/project/pallas_call | solution.py:482
  35.3 0.0 collective-permute-done.other_ref
  35.3 0.8 copy-done.4
  36.1 9.2 %attend.1 = (bf16[4,256,256]{2,1,0:T(8,128)(2,1)}, bf16[32,88,128]{2,1,0:T(8,128)(2,1)}) custom-call(s32[1]{0:T(128)} %bitcast.core_ref, bf16[4,256,256]{2,1,0:T(8,128)(2,1)} %seq_ref.3, s32[4,256]{1,0:T(4,128)} %keep_ref.1, f32[4,8,256,256]{3,2,1,0:T(8,128)} %get-tuple-element.20.logit_ref, bf16[4,256,256]{2,1,0:T(8,128)(2,1)} %get-tuple-element.21.value_ref, ...), custom_call_target="tpu_custom_call" | custom-call | flops 2147483648 | bytes 4194304 | tf_op jit(solution)/shard_map/attend/pallas_call | solution.py:501
  45.4 21.2 %all_to_all.21.own_ref = bf16[32,88,128]{2,1,0:T(8,128)(2,1)S(1)} all-to-all(bf16[32,88,128]{2,1,0:T(8,128)(2,1)} %get-tuple-element.27), channel_id=1, replica_groups=mesh['branch'=8,'dap'=4] {'branch','dap'}, dimensions={0} | all-to-all | bytes 1441792 | tf_op jit(solution)/shard_map/all_to_all | solution.py:437
  66.5 1.5 %collective-permute-start.1 = (bf16[32,88,128]{2,1,0:T(8,128)(2,1)S(1)}, bf16[32,88,128]{2,1,0:T(8,128)(2,1)S(1)}, u32[]{:S(2)}, u32[]{:S(2)}) collective-permute-start(bf16[32,88,128]{2,1,0:T(8,128)(2,1)S(1)} %all_to_all.21.own_ref), channel_id=1, source_target_pairs={{0,4},{4,0},{8,12},{12,8},{16,20},{20,16},{24,28},{28,24},{1,5},{5... | collective-permute-start | bytes 2162696 | tf_op jit(solution)/shard_map/ppermute | solution.py:440
  68.1 1.5 %collective-permute-start.2 = (bf16[8,128,128]{2,1,0:T(8,128)(2,1)S(1)}, bf16[8,128,128]{2,1,0:T(8,128)(2,1)S(1)}, u32[]{:S(2)}, u32[]{:S(2)}) collective-permute-start(bf16[8,128,128]{2,1,0:T(8,128)(2,1)S(1)} %copy-done.6), channel_id=1, source_target_pairs={{0,8},{4,12},{8,0},{12,4},{16,24},{20,28},{24,16},{28,20},{1,9},{5... | collective-permute-start | bytes 786440 | tf_op jit(solution)/shard_map/ppermute | solution.py:440
  69.6 6.8 %collective-permute-done.2.couple_theirs_ref = bf16[8,128,128]{2,1,0:T(8,128)(2,1)S(1)} collective-permute-done((bf16[8,128,128]{2,1,0:T(8,128)(2,1)S(1)}, bf16[8,128,128]{2,1,0:T(8,128)(2,1)S(1)}, u32[]{:S(2)}, u32[]{:S(2)}) %collective-permute-start.2) | collective-permute-done | bytes 262176 | tf_op jit(solution)/shard_map/ppermute | solution.py:440
  76.4 0.7 copy-done.7
  77.1 0.3 copy-done.5
  77.3 7.1 %shard_map.142 = (bf16[8,128,128]{2,1,0:T(8,128)(2,1)}, bf16[8,128,128]{2,1,0:T(8,128)(2,1)}, bf16[4096,128]{1,0:T(8,128)(2,1)}) custom-call(s32[1]{0:T(128)} %bitcast.core_ref, s32[1]{0:T(128)} %bitcast.1.side_ref, s32[1]{0:T(128)} %bitcast.8.first_mine_ref, s32[1]{0:T(128)} %bitcast.9.first_theirs_ref, s32[256]{0:T(256)} %marks_ref.1, ...), custom_call_target="tpu_custom_call" | custom-call | flops 2147483648 | bytes 1048576 | tf_op jit(solution)/shard_map/pallas_call | solution.py:66
  84.5 28.4 %all_to_all.22.in_ref = bf16[32,128,128]{2,1,0:T(8,128)(2,1)} all-to-all(bf16[32,128,128]{2,1,0:T(8,128)(2,1)} %bitcast.17), channel_id=1, replica_groups=mesh['branch'=8,'dap'=4] {'branch','dap'}, dimensions={0} | all-to-all | bytes 2097152 | tf_op jit(solution)/shard_map/all_to_all | solution.py:437
  112.9 2.4 %shard_map.143 = bf16[32,32,256]{2,1,0:T(8,128)(2,1)} custom-call(bf16[32,128,128]{2,1,0:T(8,128)(2,1)} %all_to_all.22.in_ref), custom_call_target="tpu_custom_call" | custom-call | flops 268435456 | bytes 1048576 | tf_op jit(solution)/shard_map/pallas_call | solution.py:66
  115.2 4.5 %all-to-all-start.3 = ((bf16[32,32,256]{2,1,0:T(8,128)(2,1)}), bf16[32,32,256]{2,1,0:T(8,128)(2,1)S(1)}, u32[]{:S(2)}, u32[]{:S(2)}) async-start(bf16[32,32,256]{2,1,0:T(8,128)(2,1)} %shard_map.143), calls=%async_computation.3 | async-start | bytes 1048576 | tf_op jit(solution)/shard_map/all_to_all | solution.py:437
  119.8 1.8 %collective-permute-start.3 = (bf16[8,128,128]{2,1,0:T(8,128)(2,1)}, bf16[8,128,128]{2,1,0:T(8,128)(2,1)S(1)}, u32[]{:S(2)}, u32[]{:S(2)}) collective-permute-start(bf16[8,128,128]{2,1,0:T(8,128)(2,1)} %get-tuple-element.35), channel_id=1, source_target_pairs={{0,8},{4,12},{8,0},{12,4},{16,24},{20,28},{24,16},{28,20},{1,9},{5... | collective-permute-start | bytes 786440 | tf_op jit(solution)/shard_map/ppermute | solution.py:440
  121.6 11.5 %collective-permute-done.3.theirs_ref = bf16[8,128,128]{2,1,0:T(8,128)(2,1)S(1)} collective-permute-done((bf16[8,128,128]{2,1,0:T(8,128)(2,1)}, bf16[8,128,128]{2,1,0:T(8,128)(2,1)S(1)}, u32[]{:S(2)}, u32[]{:S(2)}) %collective-permute-start.3) | collective-permute-done | bytes 262176 | tf_op jit(solution)/shard_map/ppermute | solution.py:440
  133.1 0.7 copy-done.2
  133.8 3.0 %shard_map.144 = (f32[8,128,128]{2,1,0:T(8,128)}, f32[8,128,128]{2,1,0:T(8,128)}) custom-call(bf16[8,128,128]{2,1,0:T(8,128)(2,1)} %get-tuple-element.34.mine_ref, bf16[8,128,128]{2,1,0:T(8,128)(2,1)} %copy-done.2, bf16[128,128]{1,0:T(8,128)(2,1)} %weight_ref.2), custom_call_target="tpu_custom_call" | custom-call | flops 134217728 | bytes 1048576 | tf_op jit(solution)/shard_map/pallas_call | solution.py:66
  136.8 0.8 copy-done.1
  137.6 2.9 %shard_map.145 = bf16[8,256,128]{2,1,0:T(8,128)(2,1)} custom-call(s32[1]{0:T(128)} %bitcast.1.side_ref, bf16[1024,256]{1,0:T(8,128)(2,1)} %bitcast.16, bf16[8,128,128]{2,1,0:T(8,128)(2,1)} %get-tuple-element.34.mine_ref, bf16[8,128,128]{2,1,0:T(8,128)(2,1)} %copy-done.2, f32[8,128,128]{2,1,0:T(8,128)} %get-tuple-element.36.mine_gate_ref, ...), custom_call_target="tpu_custom_call" | custom-call | flops 134217728 | bytes 1048576 | tf_op jit(solution)/shard_map/pallas_call | solution.py:66
  (14 shorter events, 0.1 us)
Async XLA Ops:
  25.1 43.0 %copy-start.6 = (bf16[8,128,128]{2,1,0:T(8,128)(2,1)S(1)}, bf16[8,128,128]{2,1,0:T(8,128)(2,1)}, u32[]{:S(2)}) copy-start(bf16[8,128,128]{2,1,0:T(8,128)(2,1)} %get-tuple-element.29) | copy-start | bytes 786436
  25.1 10.2 %copy-start = (bf16[4,256,256]{2,1,0:T(8,128)(2,1)}, bf16[4,256,256]{2,1,0:T(8,128)(2,1)S(1)}, u32[]{:S(2)}) copy-start(bf16[4,256,256]{2,1,0:T(8,128)(2,1)S(1)} %copy_bitcast_fusion.own_ref) | copy-start | bytes 1572868
  25.1 10.2 %collective-permute-start = (bf16[4,256,256]{2,1,0:T(8,128)(2,1)S(1)}, bf16[4,256,256]{2,1,0:T(8,128)(2,1)S(1)}, u32[]{:S(2)}, u32[]{:S(2)}) collective-permute-start(bf16[4,256,256]{2,1,0:T(8,128)(2,1)S(1)} %copy_bitcast_fusion.own_ref), channel_id=1, source_target_pairs={{0,4},{4,0},{8,12},{12,8},{16,20},{20,16},{24,28},{28,24},{1,5},{5... | collective-permute-start | bytes 1572872 | tf_op jit(solution)/shard_map/ppermute | solution.py:440
  35.3 0.8 copy-start.4
  66.5 9.8 %copy-start.3 = (bf16[32,88,128]{2,1,0:T(8,128)(2,1)}, bf16[32,88,128]{2,1,0:T(8,128)(2,1)S(1)}, u32[]{:S(2)}) copy-start(bf16[32,88,128]{2,1,0:T(8,128)(2,1)S(1)} %all_to_all.21.own_ref) | copy-start | bytes 2162692
  66.5 9.8 %collective-permute-start.1 = (bf16[32,88,128]{2,1,0:T(8,128)(2,1)S(1)}, bf16[32,88,128]{2,1,0:T(8,128)(2,1)S(1)}, u32[]{:S(2)}, u32[]{:S(2)}) collective-permute-start(bf16[32,88,128]{2,1,0:T(8,128)(2,1)S(1)} %all_to_all.21.own_ref), channel_id=1, source_target_pairs={{0,4},{4,0},{8,12},{12,8},{16,20},{20,16},{24,28},{28,24},{1,5},{5... | collective-permute-start | bytes 2162696 | tf_op jit(solution)/shard_map/ppermute | solution.py:440
  68.1 8.3 %collective-permute-start.2 = (bf16[8,128,128]{2,1,0:T(8,128)(2,1)S(1)}, bf16[8,128,128]{2,1,0:T(8,128)(2,1)S(1)}, u32[]{:S(2)}, u32[]{:S(2)}) collective-permute-start(bf16[8,128,128]{2,1,0:T(8,128)(2,1)S(1)} %copy-done.6), channel_id=1, source_target_pairs={{0,8},{4,12},{8,0},{12,4},{16,24},{20,28},{24,16},{28,20},{1,9},{5... | collective-permute-start | bytes 786440 | tf_op jit(solution)/shard_map/ppermute | solution.py:440
  76.4 0.7 copy-start.7
  76.4 1.0 copy-start.5
  115.2 21.6 %all-to-all-start.3 = ((bf16[32,32,256]{2,1,0:T(8,128)(2,1)}), bf16[32,32,256]{2,1,0:T(8,128)(2,1)S(1)}, u32[]{:S(2)}, u32[]{:S(2)}) async-start(bf16[32,32,256]{2,1,0:T(8,128)(2,1)} %shard_map.143), calls=%async_computation.3 | async-start | bytes 1048576 | tf_op jit(solution)/shard_map/all_to_all | solution.py:437
  119.8 13.4 %collective-permute-start.3 = (bf16[8,128,128]{2,1,0:T(8,128)(2,1)}, bf16[8,128,128]{2,1,0:T(8,128)(2,1)S(1)}, u32[]{:S(2)}, u32[]{:S(2)}) collective-permute-start(bf16[8,128,128]{2,1,0:T(8,128)(2,1)} %get-tuple-element.35), channel_id=1, source_target_pairs={{0,8},{4,12},{8,0},{12,4},{16,24},{20,28},{24,16},{28,20},{1,9},{5... | collective-permute-start | bytes 786440 | tf_op jit(solution)/shard_map/ppermute | solution.py:440
  133.1 0.7 copy-start.2
  136.8 0.8 copy-start.1

commit v3 on v2

v3 whole, which is shorter than its diff:
```python
import functools
import math

import jax
import jax.numpy as jnp
from jax import lax
from jax.experimental import pallas as pl
from jax.experimental.pallas import tpu as pltpu
from jax.sharding import PartitionSpec as P


EPSILON = 1e-05
EVERY = ("branch", "dap")
VMEM = pltpu.VMEM
F32 = jnp.float32
BF16 = jnp.bfloat16

NT = (((1,), (1,)), ((), ()))
TN = (((0,), (0,)), ((), ()))
NN = (((1,), (0,)), ((), ()))


def mm(a, b, dims=NN):
    return lax.dot_general(a, b, dims, preferred_element_type=F32)


def normalize(values, axis=-1):
    values = values.astype(F32)
    centred = values - jnp.mean(values, axis=axis, keepdims=True)
    spread = jnp.mean(centred * centred, axis=axis, keepdims=True)
    return centred * lax.rsqrt(spread + EPSILON)


def vspec():
    return pl.BlockSpec(memory_space=VMEM)


def sspec():
    return pl.BlockSpec(memory_space=pltpu.SMEM)


LANES = 128


def room(mebibytes):
    return pltpu.CompilerParams(vmem_limit_bytes=mebibytes * 2**20)


def sheets(rows, columns):
    return VMEM((columns // LANES, rows, LANES), F32)


def put(scr, start, values, stride):
    for k in range(scr.shape[0]):
        part = values[:, k * LANES : (k + 1) * LANES]
        scr[k, pl.ds(start, values.shape[0], stride=stride), :] = part


def take(scr, start, count, stride=1):
    parts = [scr[k, pl.ds(start, count, stride=stride), :] for k in range(scr.shape[0])]
    return parts[0] if len(parts) == 1 else jnp.concatenate(parts, axis=1)


def fill(scr, values):
    for k in range(scr.shape[0]):
        scr[k] = values[:, k * LANES : (k + 1) * LANES]


def stay(values):
    return pltpu.with_memory_space_constraint(values, pltpu.MemorySpace.HBM)


def call(body, out, args, scratch=(), in_specs=None, flops=0, need=8, **kw):
    single = not isinstance(out, (tuple, list))
    return pl.pallas_call(
        body,
        out_shape=out,
        in_specs=in_specs or [vspec() for _ in args],
        out_specs=vspec() if single else tuple(vspec() for _ in out),
        scratch_shapes=list(scratch),
        cost_estimate=pl.CostEstimate(flops=flops, bytes_accessed=2**20, transcendentals=0),
        compiler_params=room(need),
        **kw,
    )(*args)


def sigmoid(values):
    return 0.5 * jnp.tanh(0.5 * values) + 0.5


def bias_kernel(cores, side_ref, couple_ref, weight_ref, out_ref, mine_ref, theirs_ref, scr):
    rows, residues, _ = couple_ref.shape
    heads = weight_ref.shape[0]
    half = residues // 2
    mine = pl.multiple_of(side_ref[0] * half, half)
    theirs = pl.multiple_of((1 - side_ref[0]) * half, half)
    for i in range(rows):
        normed = normalize(couple_ref[i]).astype(BF16)
        put(scr, i, mm(weight_ref[...], normed, NT), rows)
        mine_ref[i] = couple_ref[i, pl.ds(mine, half), :]
        theirs_ref[i] = couple_ref[i, pl.ds(theirs, half), :]
    part = heads // 2 * rows
    halves = [take(scr, k * part, part).astype(BF16) for k in range(2)]
    for t, core in enumerate(cores):
        out_ref[t] = halves[core]


def prepare_small_kernel(seqs, halves_ref, left_ref, right_ref):
    width = halves_ref.shape[0] // 2
    left = halves_ref[:width].astype(F32).T.astype(BF16)
    for s in range(seqs):
        parts = [left if u == s else jnp.zeros_like(left) for u in range(seqs)]
        left_ref[s] = jnp.concatenate(parts, axis=1)
    right_ref[...] = halves_ref[width:]


def prepare_large_kernel(
    chunks,
    per,
    merge_ref,
    entry_ref,
    close_ref,
    table_ref,
    value_ref,
    gate_ref,
    final_ref,
    merge_scr,
    entry_scr,
    edge_scr,
):
    channels = merge_ref.shape[1]
    width = math.isqrt(merge_ref.shape[0])
    part = width // 2
    merge_scr[...] = merge_ref[...].astype(F32)
    for k in range(2):
        rows = [merge_scr[pl.ds(k * part + q, width, stride=width), :] for q in range(part)]
        table_ref[k] = jnp.concatenate(rows, axis=0).T.astype(BF16)
    for k in range(4):
        entry_scr[k * channels : (k + 1) * channels, :] = (
            entry_ref[:, k * channels : (k + 1) * channels].astype(F32).T
        )
    some = per // chunks
    n = channels // per
    for kind, ref in enumerate((value_ref, gate_ref)):
        for k in range(2):
            for c in range(per):
                source = (2 * k + kind) * channels + c
                at = c // some * n * 2 * some + k * some + c % some
                edge_scr[pl.ds(at, n, stride=2 * some), :] = entry_scr[
                    pl.ds(source, n, stride=per), :
                ]
        ref[...] = edge_scr[...].astype(BF16)
    entry_scr[:channels, :] = close_ref[...].astype(F32)
    for c in range(per):
        at = c // some * n * some + c % some
        edge_scr[pl.ds(at, n, stride=some), :] = entry_scr[pl.ds(c, n, stride=per), :]
    final_ref[...] = edge_scr[:channels, :].astype(BF16)


def project_kernel(seq_ref, qkv_w_ref, gate_w_ref, query_ref, key_ref, value_ref, gate_ref):
    inner = gate_w_ref.shape[1]
    normed = normalize(seq_ref[0]).astype(BF16)
    projected = mm(normed, qkv_w_ref[...])
    query_ref[0] = projected[:, :inner].astype(BF16)
    key_ref[0] = projected[:, inner : 2 * inner].T.astype(BF16)
    value_ref[0] = projected[:, 2 * inner :].astype(BF16)
    gate_ref[0] = sigmoid(mm(normed, gate_w_ref[...]))


def attend_kernel(
    heads,
    places,
    raw,
    core_ref,
    seq_ref,
    keep_ref,
    query_ref,
    key_ref,
    value_ref,
    gate_ref,
    own_ref,
    other_ref,
    merge_ref,
    left_w_ref,
    right_w_ref,
    new_ref,
    message_ref,
    left_scr,
    bias_scr,
    ones_scr,
):
    step = pl.program_id(0)
    batch = seq_ref.shape[0]
    seqs = keep_ref.shape[0]
    core = core_ref[0]
    inner = gate_ref.shape[2]
    residues = gate_ref.shape[1]
    half = inner // 2
    head_width = inner // heads
    scale = head_width ** (-0.5)
    some_heads = heads // 2
    zero = jnp.zeros((), BF16)
    blank = jnp.zeros((head_width, residues), BF16)
    lane_half = lax.broadcasted_iota(jnp.int32, (residues, half), 1) // head_width

    @pl.when(step == 0)
    def _():
        left_scr[...] = jnp.zeros_like(left_scr)
        for h in range(some_heads):
            ones_scr[h * residues : (h + 1) * residues, :] = jnp.where(
                lane_half == h, jnp.ones((), BF16), zero
            )
        for k, ref in enumerate((own_ref, other_ref)):
            for h in range(some_heads):
                if raw:
                    rows = residues // len(places)
                    tile = ref[:, h * rows : (h + 1) * rows, :].astype(F32)
                    tile = tile.reshape(residues, residues)
                else:
                    tile = ref[h].astype(F32)
                bias_scr[k * some_heads + h] = tile

    width = right_w_ref.shape[0]
    part = width // 2
    columns = message_ref.shape[2]
    span = seqs * part
    for u in range(batch):
        s = step * batch + u
        keep = keep_ref[pl.ds(s, 1), :]
        present = keep.astype(F32)
        masking = jnp.where(keep == 1, 0.0, -1000000000.0).astype(F32)
        mixed = []
        for k, group in ((0, core), (1, 1 - core)):
            queries, values = (
                jnp.where(group == 0, ref[u, :, :half], ref[u, :, half:])
                for ref in (query_ref, value_ref)
            )
            keys = jnp.where(group == 0, key_ref[u, :half, :], key_ref[u, half:, :])
            weights, tables = [], []
            for h in range(some_heads):
                only = [
                    keys[g * head_width : (g + 1) * head_width] if g == h else blank
                    for g in range(some_heads)
                ]
                logits = mm(queries, jnp.concatenate(only, axis=0)) * scale
                logits = logits + bias_scr[k * some_heads + h] + masking
                logits = logits - jnp.max(logits, axis=-1, keepdims=True)
                weights.append(jnp.exp(logits).astype(BF16))
                tables.append(jnp.where(lane_half == h, values, zero))
            table = jnp.concatenate([jnp.concatenate(tables, axis=0), ones_scr[...]], axis=1)
            total = mm(jnp.concatenate(weights, axis=1), table)
            mixed.append(total[:, :half] / total[:, half:])
        first = jnp.where(core == 0, mixed[0], mixed[1])
        second = jnp.where(core == 0, mixed[1], mixed[0])
        attended = (jnp.concatenate([first, second], axis=1) * gate_ref[u]).astype(BF16)
        updated = (seq_ref[u].astype(F32) + mm(attended, merge_ref[...])).astype(BF16)
        new_ref[u] = updated
        normed = normalize(updated).astype(BF16)
        right = (mm(right_w_ref[...], normed, NT) * present).astype(BF16)
        at = pl.multiple_of(s * part, part)
        for t, (core_of, side, _) in enumerate(places):
            message_ref[t, pl.ds(at, part), :] = right[
                core_of * part : (core_of + 1) * part, side * columns : (side + 1) * columns
            ]
        present_column = jnp.broadcast_to(present, (8, residues)).T[:, :1]
        left_scr[...] += mm(normed, left_w_ref[s]) * present_column

    @pl.when(step == pl.num_programs(0) - 1)
    def _():
        rows = residues // len(places)
        marks = keep_ref[...].astype(F32)
        marks = jnp.concatenate(
            [marks[:, k * columns : (k + 1) * columns] for k in range(2)], axis=0
        ).astype(BF16)
        for t, (_, _, mate) in enumerate(places):
            block = jnp.concatenate(
                [left_scr[u * rows : (u + 1) * rows, :] for u in (t, mate)], axis=0
            )
            message_ref[t, span : span + 2 * rows, :] = block.astype(BF16)
            message_ref[t, span + 2 * rows :, :] = marks


def multiply(seqs, width, left, ref, scr, products):
    n, _, columns = ref.shape
    part = width // 2
    span = seqs * part
    block = left.shape[0] // width
    scr[...] = ref[:, :span, :].astype(F32).reshape(n * span, columns)
    for q in range(0, part, 2):
        pair = [
            jnp.concatenate(
                [scr[pl.ds(s * part + q + d, n, stride=span), :] for s in range(seqs)], axis=0
            ).astype(BF16)
            for d in range(2)
        ]
        outer = mm(left, jnp.concatenate(pair, axis=1)).astype(BF16)
        for d in range(2):
            at = (q + d) * width
            for i in range(block):
                products[i, at : at + width, :] = outer[
                    i * width : (i + 1) * width, d * columns : (d + 1) * columns
                ]


def outer_own_kernel(
    seqs,
    width,
    rows,
    side_ref,
    first_mine_ref,
    first_theirs_ref,
    own_ref,
    left_ref,
    scale_ref,
    products_ref,
    right_scr,
    small_scr,
):
    n, depth, columns = own_ref.shape
    block = 2 * rows
    total_seqs = n * seqs
    span = seqs * width // 2
    side, first_mine, first_theirs = side_ref[0], first_mine_ref[0], first_theirs_ref[0]
    extra = depth - span
    small_scr[...] = own_ref[:, span:, :].astype(F32).reshape(n * extra, columns)
    left_rows = []
    for i in range(block):
        piece = small_scr[pl.ds(i, n, stride=extra), :]
        for s in range(seqs):
            left_rows.append(piece[:, s * width : (s + 1) * width])
    left_all = jnp.concatenate(left_rows, axis=0).T
    left = jnp.concatenate(
        [left_all[:, i * total_seqs : (i + 1) * total_seqs] for i in range(block)], axis=0
    ).astype(BF16)
    left_ref[...] = left
    keep_halves = []
    for k in range(2):
        at = block + k * seqs
        keep_halves.append(
            jnp.concatenate(
                [small_scr[pl.ds(at + s, n, stride=extra), :] for s in range(seqs)], axis=0
            )
        )
    keep_columns = jnp.where(side == 0, keep_halves[0], keep_halves[1]).astype(BF16)
    keep = jnp.concatenate(keep_halves, axis=1).astype(BF16)
    pad = scale_ref.shape[0]
    order = lax.broadcasted_iota(jnp.int32, (pad, 2 * columns), 0)
    row_ids = jnp.where(order < rows, first_mine + order, first_theirs + order - rows)
    chosen = (row_ids == lax.broadcasted_iota(jnp.int32, (pad, 2 * columns), 1)).astype(BF16)
    counts = mm(mm(chosen, keep, NT).astype(BF16), keep_columns)
    scale_ref[...] = 1.0 / jnp.maximum(counts, 1.0)
    multiply(seqs, width, left, own_ref, right_scr, products_ref)


def outer_kernel(
    seqs,
    width,
    core_ref,
    side_ref,
    first_mine_ref,
    first_theirs_ref,
    marks_ref,
    other_ref,
    left_ref,
    scale_ref,
    own_products_ref,
    couple_mine_ref,
    couple_theirs_ref,
    table_ref,
    value_w_ref,
    gate_w_ref,
    observed_ref,
    pair_mine_ref,
    pair_theirs_ref,
    *rest,
):
    edges_refs, (right_scr, products, edge_scr) = rest[:-3], rest[-3:]
    rows, columns, channels = couple_mine_ref.shape
    block = 2 * rows
    core, side = core_ref[0], side_ref[0]
    first_mine, first_theirs = first_mine_ref[0], first_theirs_ref[0]
    multiply(seqs, width, left_ref[...], other_ref, right_scr, products)
    scale = scale_ref[...]
    tables = ((table_ref[core], own_products_ref), (table_ref[1 - core], products))
    half = pl.multiple_of(side * columns, columns)
    observed = observed_ref[:, pl.ds(half, columns)].astype(F32)
    row_marks = [marks_ref[first_mine + r] for r in range(rows)]
    row_marks += [marks_ref[first_theirs + r] for r in range(rows)]
    for i in range(0, block, 2):
        update = sum(
            mm(table, jnp.concatenate([values[i], values[i + 1]], axis=1))
            for table, values in tables
        )
        normed = []
        for d in range(2):
            piece = update[:, d * columns : (d + 1) * columns] * scale[i + d : i + d + 1, :]
            couple_ref, pair_ref = (
                (couple_mine_ref, pair_mine_ref)
                if i + d < rows
                else (couple_theirs_ref, pair_theirs_ref)
            )
            r = (i + d) % rows
            pair = (couple_ref[r].astype(F32) + piece.T).astype(BF16)
            pair_ref[r] = pair
            normed.append(normalize(pair).astype(BF16))
        normed = jnp.concatenate(normed, axis=0)
        edge = mm(value_w_ref[...], normed, NT) * sigmoid(mm(gate_w_ref[...], normed, NT))
        for d in range(2):
            mark = observed * row_marks[i + d].astype(F32)
            edge_scr[pl.ds(i + d, 2 * channels, stride=block), :] = (
                edge[:, d * columns : (d + 1) * columns] * mark
            )
    size = edges_refs[0].shape[0]
    for k, ref in enumerate(edges_refs):
        ref[...] = edge_scr[k * size : (k + 1) * size, :].astype(BF16)


def close_gate_kernel(mine_ref, theirs_ref, weight_ref, mine_gate_ref, theirs_gate_ref):
    for pair_ref, gate_ref in ((mine_ref, mine_gate_ref), (theirs_ref, theirs_gate_ref)):
        for i in range(pair_ref.shape[0]):
            normed = normalize(pair_ref[i]).astype(BF16)
            gate_ref[i] = sigmoid(mm(normed, weight_ref[...]))


def triangle_kernel(per, rows, places, in_ref, out_ref, in_scr, out_scr):
    n = in_ref.shape[0]
    residues = n * rows
    in_scr[...] = in_ref[...].astype(F32)

    def whole(at):
        tiles = []
        for t, (_, side, mate) in enumerate(places):
            pair = []
            for k in range(2):
                source, shift = (t, 0) if side == k else (mate, rows)
                pair.append(in_scr[source, at + shift : at + shift + rows, :])
            tiles.append(jnp.concatenate(pair, axis=1))
        return jnp.concatenate(tiles, axis=0).astype(BF16)

    for c in range(per):
        left = whole(c * 2 * rows)
        right = whole((per + c) * 2 * rows)
        out_scr[:, c * rows : (c + 1) * rows, :] = mm(left, right, NT).reshape(n, rows, residues)
    out_ref[...] = out_scr[...].astype(BF16)


def plain_triangle_kernel(left_ref, right_ref, out_ref):
    for c in range(left_ref.shape[0]):
        out_ref[c] = mm(left_ref[c], right_ref[c], NT).astype(BF16)


def close_kernel(
    side_ref, mine_ref, theirs_ref, mine_gate_ref, theirs_gate_ref, weight_ref, *rest
):
    count = (len(rest) - 1) // 2
    in_refs, out_ref, scrs = rest[:count], rest[count], rest[count + 1 :]
    rows, columns, channels = mine_ref.shape
    for ref, scr in zip(in_refs, scrs):
        fill(scr, ref[...].astype(F32))
    side = side_ref[0]
    for half, pair_ref, gate_ref in (
        (side, mine_ref, mine_gate_ref),
        (1 - side, theirs_ref, theirs_gate_ref),
    ):
        at = pl.multiple_of(half * columns, columns)
        for i in range(rows):
            piece = [scr[half, pl.ds(i, channels // count, stride=rows), :] for scr in scrs]
            piece = jnp.concatenate(piece, axis=0)
            update = mm(normalize(piece, axis=0).astype(BF16), weight_ref[...], TN)
            out_ref[i, pl.ds(at, columns), :] = (
                pair_ref[i].astype(F32) + gate_ref[i] * update
            ).astype(BF16)


def per_device(
    branch,
    dap,
    homolog_embedding,
    couple_embedding,
    homolog_present,
    observed_position,
    couple_logit_kernel,
    lookup_kernels,
    heads_sigmoid_kernel,
    heads_merge_kernel,
    tensor_halves_kernel,
    tensor_merge_kernel,
    edge_entry_kernel,
    closing_sigmoid_kernel,
    closing_merge_kernel,
):
    n = branch * dap
    rows, residues, channels = couple_embedding.shape
    seqs = homolog_embedding.shape[0]
    features = homolog_embedding.shape[2]
    heads = couple_logit_kernel.shape[1]
    inner = heads_sigmoid_kernel.shape[1]
    width = tensor_halves_kernel.shape[1] // 2
    per = channels // n
    half = residues // 2
    block = 2 * rows

    chunks = 1
    some = per // chunks
    places = [((t // dap) % 2, (t // dap // 2) % 2, (t // dap ^ 2) * dap + t % dap) for t in range(n)]
    me = lax.axis_index("branch").astype(jnp.int32)
    core = (me % 2).reshape(1)
    side = (me // 2 % 2).reshape(1)
    place = lax.axis_index("dap").astype(jnp.int32)
    first_mine = (me * dap + place) * rows
    first_theirs = ((me ^ 2) * dap + place) * rows
    chip = [(b, b ^ 1) for b in range(branch)]
    across = [(b, b ^ 2) for b in range(branch)]

    def exchange(values):
        return lax.all_to_all(values, EVERY, split_axis=0, concat_axis=0, tiled=True)

    def permute(values, pairs):
        return lax.ppermute(values, "branch", pairs)

    left_w, right_w = call(
        functools.partial(prepare_small_kernel, seqs),
        (
            jax.ShapeDtypeStruct((seqs, features, seqs * width), BF16),
            jax.ShapeDtypeStruct((width, features), BF16),
        ),
        (tensor_halves_kernel.T,),
    )
    table, value_w, gate_w, final_w = call(
        functools.partial(prepare_large_kernel, chunks, per),
        (
            jax.ShapeDtypeStruct((2, channels, width // 2 * width), BF16),
            jax.ShapeDtypeStruct((2 * channels, channels), BF16),
            jax.ShapeDtypeStruct((2 * channels, channels), BF16),
            jax.ShapeDtypeStruct((channels, channels), BF16),
        ),
        (tensor_merge_kernel, edge_entry_kernel, closing_merge_kernel),
        [
            VMEM((width * width, channels), F32),
            VMEM((4 * channels, channels), F32),
            VMEM((2 * channels, channels), F32),
        ],
    )

    half_heads = heads // 2
    message, couple_mine, couple_send = call(
        functools.partial(bias_kernel, [place[0] for place in places]),
        (
            jax.ShapeDtypeStruct((n, half_heads * rows, residues), BF16),
            jax.ShapeDtypeStruct((rows, half, channels), BF16),
            jax.ShapeDtypeStruct((rows, half, channels), BF16),
        ),
        (side, stay(couple_embedding), stay(couple_logit_kernel.T)),
        [sheets(heads * rows, residues)],
        in_specs=[sspec(), vspec(), vspec()],
    )
    own_bias = exchange(message)
    raw = rows % 8 == 0
    if not raw:
        own_bias = own_bias.reshape(n, half_heads, rows, residues)
        own_bias = own_bias.transpose(1, 0, 2, 3).reshape(half_heads, residues, residues)
    other_bias = permute(own_bias, chip)
    couple_theirs = permute(couple_send, across)

    def whole(*shape):
        return pl.BlockSpec(shape, lambda s: (0,) * len(shape))

    def per_seq(batch, *shape):
        return pl.BlockSpec((batch, *shape), lambda s: (s,) + (0,) * len(shape))

    *parts, gates = pl.pallas_call(
        project_kernel,
        grid=(seqs,),
        out_shape=(
            jax.ShapeDtypeStruct((seqs, residues, inner), BF16),
            jax.ShapeDtypeStruct((seqs, inner, residues), BF16),
            jax.ShapeDtypeStruct((seqs, residues, inner), BF16),
            jax.ShapeDtypeStruct((seqs, residues, inner), F32),
        ),
        in_specs=[
            per_seq(1, residues, features),
            whole(features, 3 * inner),
            whole(features, inner),
        ],
        out_specs=(
            per_seq(1, residues, inner),
            per_seq(1, inner, residues),
            per_seq(1, residues, inner),
            per_seq(1, residues, inner),
        ),
        name="project",
        compiler_params=room(16),
        cost_estimate=pl.CostEstimate(flops=2**29, bytes_accessed=2**22, transcendentals=0),
    )(stay(homolog_embedding), stay(lookup_kernels), stay(heads_sigmoid_kernel))
    span = seqs * width // 2
    depth = span + block + 2 * seqs
    batch = 2 if seqs % 2 == 0 else 1
    homolog_refreshed, message = pl.pallas_call(
        functools.partial(attend_kernel, heads, places, raw),
        grid=(seqs // batch,),
        out_shape=(
            jax.ShapeDtypeStruct((seqs, residues, features), BF16),
            jax.ShapeDtypeStruct((n, depth, half), BF16),
        ),
        in_specs=[
            sspec(),
            per_seq(batch, residues, features),
            whole(seqs, residues),
            per_seq(batch, residues, inner),
            per_seq(batch, inner, residues),
            per_seq(batch, residues, inner),
            per_seq(batch, residues, inner),
            whole(*own_bias.shape),
            whole(*own_bias.shape),
            whole(inner, features),
            whole(seqs, features, seqs * width),
            whole(width, features),
        ],
        out_specs=(per_seq(batch, residues, features), whole(n, depth, half)),
        scratch_shapes=[
            VMEM((residues, seqs * width), F32),
            VMEM((heads, residues, residues), F32),
            VMEM((half_heads * residues, half), BF16),
        ],
        name="attend",
        compiler_params=room(24),
        cost_estimate=pl.CostEstimate(flops=2**31, bytes_accessed=2**22, transcendentals=0),
    )(
        core,
        stay(homolog_embedding),
        stay(homolog_present),
        *(stay(values) for values in parts),
        stay(gates),
        own_bias,
        other_bias,
        stay(heads_merge_kernel),
        left_w,
        right_w,
    )

    own = exchange(message)
    other = permute(own, chip)
    firsts = (first_mine.reshape(1), first_theirs.reshape(1))
    left, scale, products = call(
        functools.partial(outer_own_kernel, seqs, width, rows),
        (
            jax.ShapeDtypeStruct((block * width, n * seqs), BF16),
            jax.ShapeDtypeStruct((-(-block // 8) * 8, half), F32),
            jax.ShapeDtypeStruct((block, width // 2 * width, half), BF16),
        ),
        (side, *firsts, own),
        [VMEM((n * span, half), F32), VMEM((n * (depth - span), half), F32)],
        need=16,
        in_specs=[sspec()] * 3 + [vspec()],
        flops=2**30,
    )
    piece = jax.ShapeDtypeStruct((rows, half, channels), BF16)
    pair_mine, pair_send, *edges = call(
        functools.partial(outer_kernel, seqs, width),
        (piece, piece)
        + (jax.ShapeDtypeStruct((2 * channels * block // chunks, half), BF16),) * chunks,
        (
            core,
            side,
            *firsts,
            observed_position,
            other,
            left,
            scale,
            products,
            couple_mine,
            couple_theirs,
            table,
            value_w,
            gate_w,
            observed_position.reshape(1, residues),
        ),
        [
            VMEM((n * span, half), F32),
            VMEM((block, width // 2 * width, half), BF16),
            VMEM((2 * channels * block, half), F32),
        ],
        need=20,
        in_specs=[sspec()] * 5 + [vspec()] * 10,
        flops=2**31,
    )

    received = [exchange(values.reshape(n, 2 * some * block, half)) for values in edges]
    pair_theirs = permute(pair_send, across)
    gate_piece = jax.ShapeDtypeStruct((rows, half, channels), F32)
    gate_mine, gate_theirs = call(
        close_gate_kernel,
        (gate_piece, gate_piece),
        (pair_mine, pair_theirs, closing_sigmoid_kernel),
        flops=2**27,
    )

    def triangle(values):
        if rows % 8 == 0:
            return call(
                functools.partial(triangle_kernel, some, rows, places),
                jax.ShapeDtypeStruct((n, some * rows, residues), BF16),
                (values,),
                [
                    VMEM((n, 2 * some * block, half), F32),
                    VMEM((n, some * rows, residues), F32),
                ],
                need=12,
                flops=2**28,
            )
        both = values.reshape(branch // 4, 2, 2, dap, 2, some, 2, rows, half)
        both = jnp.stack([both[:, 0], both[:, 1, :, :, :, :, ::-1]], axis=1)
        both = both.transpose(4, 5, 0, 6, 2, 3, 7, 1, 8).reshape(2, some, residues, residues)
        combined = call(
            plain_triangle_kernel,
            jax.ShapeDtypeStruct((some, residues, residues), BF16),
            (both[0], both[1]),
            need=12,
            flops=2**28,
        )
        combined = combined.reshape(some, n, rows, residues).transpose(1, 0, 2, 3)
        return combined.reshape(n, some * rows, residues)

    returned = []
    for values in received:
        combined = triangle(values)
        combined = exchange(combined)
        returned.append(combined.reshape(n * some * rows, residues))
    pair_output = call(
        close_kernel,
        jax.ShapeDtypeStruct((rows, residues, channels), BF16),
        (side, pair_mine, pair_theirs, gate_mine, gate_theirs, final_w, *returned),
        [sheets(n * some * rows, residues) for _ in returned],
        in_specs=[sspec()] + [vspec()] * (5 + len(returned)),
        flops=2**27,
    )
    return (homolog_refreshed, pair_output)


def solution(mesh):
    split = P(EVERY, None, None)
    in_specs = (split, split, P(EVERY, None)) + (P(),) * 10

    def body(*args):
        return per_device(mesh.shape["branch"], mesh.shape["dap"], *args)

    return jax.shard_map(
        body, mesh=mesh, in_specs=in_specs, out_specs=(split, split), check_vma=False
    )
```

time: 141 us -> 127 us (0.901)
  Pallas kernels: 36.3 us -> 23.6 us
  waiting for transfers between devices: 18.3 us -> 16.6 us
    pallas_call x6 -> x8, Pallas kernels: 20.6 us -> 11.8 us  [call(): pl.pallas_call(body, out_shape=out, in_specs=in_specs or [vspec() for _ i...]
    pallas_call x2, Pallas kernels: 15.7 us -> 11.8 us  [the longest x1 8.28 us: per_device(): pl.pallas_call(functools.partial(attend_kernel, heads, places, raw), grid...]
    ppermute x4, waiting for transfers between devices: 18.3 us -> 16.6 us  [permute(): return lax.ppermute(values, 'branch', pairs)]
    unnamed x16 -> x20, local copies, waits for them, and re-layouts: 3.26 us -> 4.17 us
  transfers between devices with their start and end apart: 5 -> 5, of which waited for: 2 -> 2; matrix products, arithmetic and copies ran while one was open for 0% -> 0% of each run, Pallas kernels for 8% -> 5%
where the time goes in v3:
time: 127 us; the launch traced here: 126 us
  blocking collectives  70.5 us (56%)
  Pallas kernels  23.6 us (19%)
  waiting for transfers between devices  16.6 us (13%)
  starting transfers between devices  10.7 us (8%)
  local copies, waits for them, and re-layouts  4.17 us (3%)
    all_to_all x3, blocking collectives, exchange(): lax.all_to_all(values, EVERY, split_axis=0, concat_axis=0, tiled=True)  70.5 us
    ppermute x4, waiting for transfers between devices, permute(): return lax.ppermute(values, 'branch', pairs)  16.6 us
    pallas_call x8, Pallas kernels, call(): pl.pallas_call(body, out_shape=out, in_specs=in_specs or [vspec() for _ i...  11.8 us
    pallas_call x1, Pallas kernels, per_device(): pl.pallas_call(functools.partial(attend_kernel, heads, places, raw), grid...  8.28 us
    ppermute x4, starting transfers between devices, permute(): return lax.ppermute(values, 'branch', pairs)  6.13 us
    all_to_all x1, starting transfers between devices, exchange(): lax.all_to_all(values, EVERY, split_axis=0, concat_axis=0, tiled=True)  4.55 us
    unnamed x20, local copies, waits for them, and re-layouts  4.17 us
    pallas_call x1, Pallas kernels, per_device(): pl.pallas_call(project_kernel, grid=(seqs,), out_shape=(jax.ShapeDtypeStr...  3.52 us
  transfers between devices with their start and end apart: 5, of which 2 were waited for; matrix products, arithmetic and copies ran while one was open for 0% of the time, Pallas kernels for 5%

profile of v3, /device:TPU:0, one launch (start us, length us, event | category | flops | bytes accessed | tf_op | source)
XLA Modules:
  0.0 126.3 jit_solution(6095546594915281674)
XLA Ops:
  0.7 2.0 %shard_map.140 = (bf16[32,32,256]{2,1,0:T(8,128)(2,1)S(1)}, bf16[8,128,128]{2,1,0:T(8,128)(2,1)S(1)}, bf16[8,128,128]{2,1,0:T(8,128)(2,1)S(1)}) custom-call(s32[1]{0:T(128)} %bitcast.1.side_ref, bf16[8,256,128]{2,1,0:T(8,128)(2,1)} %couple_ref.1, bf16[8,128]{1,0:T(8,128)(2,1)} %bitcast.13), custom_call_target="tpu_custom_call" | custom-call | bytes 1048576 | tf_op jit(solution)/shard_map/pallas_call | solution.py:75
  2.7 21.4 %all_to_all.20.own_ref = bf16[32,32,256]{2,1,0:T(8,128)(2,1)S(1)} all-to-all(bf16[32,32,256]{2,1,0:T(8,128)(2,1)S(1)} %get-tuple-element.29), channel_id=1, replica_groups=mesh['branch'=8,'dap'=4] {'branch','dap'}, dimensions={0} | all-to-all | bytes 1048576 | tf_op jit(solution)/shard_map/all_to_all | solution.py:516
  24.1 1.3 %collective-permute-start = (bf16[32,32,256]{2,1,0:T(8,128)(2,1)S(1)}, bf16[32,32,256]{2,1,0:T(8,128)(2,1)S(1)}, u32[]{:S(2)}, u32[]{:S(2)}) collective-permute-start(bf16[32,32,256]{2,1,0:T(8,128)(2,1)S(1)} %all_to_all.20.own_ref), channel_id=1, source_target_pairs={{0,4},{4,0},{8,12},{12,8},{16,20},{20,16},{24,28},{28,24},{1,5},{5... | collective-permute-start | bytes 1572872 | tf_op jit(solution)/shard_map/ppermute | solution.py:519
  25.3 0.8 copy-done.3
  26.3 3.5 %project.1 = (bf16[4,256,256]{2,1,0:T(8,128)(2,1)S(1)}, bf16[4,256,256]{2,1,0:T(8,128)(2,1)S(1)}, bf16[4,256,256]{2,1,0:T(8,128)(2,1)S(1)}, f32[4,256,256]{2,1,0:T(8,128)S(1)}) custom-call(bf16[4,256,256]{2,1,0:T(8,128)(2,1)} %seq_ref.3, bf16[256,768]{1,0:T(8,128)(2,1)} %qkv_w_ref.1, bf16[256,256]{1,0:T(8,128)(2,1)} %gate_w_ref.1), custom_call_target="tpu_custom_call" | custom-call | flops 536870912 | bytes 4194304 | tf_op jit(solution)/shard_map/project/pallas_call | solution.py:571
  29.9 1.0 copy-done.6
  30.9 0.8 copy-done.7
  31.6 0.8 copy-done.8
  32.4 0.8 copy-done.9
  33.3 8.3 %attend.1 = (bf16[4,256,256]{2,1,0:T(8,128)(2,1)}, bf16[32,88,128]{2,1,0:T(8,128)(2,1)S(1)}) custom-call(s32[1]{0:T(128)} %bitcast.core_ref, bf16[4,256,256]{2,1,0:T(8,128)(2,1)} %seq_ref.3, s32[4,256]{1,0:T(4,128)} %keep_ref.1, bf16[4,256,256]{2,1,0:T(8,128)(2,1)} %copy-done.7, bf16[4,256,256]{2,1,0:T(8,128)(2,1)} %copy-done.8, ...), custom_call_target="tpu_custom_call" | custom-call | flops 2147483648 | bytes 4194304 | tf_op jit(solution)/shard_map/attend/pallas_call | solution.py:598
  41.6 20.9 %all_to_all.21.own_ref = bf16[32,88,128]{2,1,0:T(8,128)(2,1)S(1)} all-to-all(bf16[32,88,128]{2,1,0:T(8,128)(2,1)S(1)} %get-tuple-element.33), channel_id=1, replica_groups=mesh['branch'=8,'dap'=4] {'branch','dap'}, dimensions={0} | all-to-all | bytes 1441792 | tf_op jit(solution)/shard_map/all_to_all | solution.py:516
  62.5 1.5 %collective-permute-start.1 = (bf16[32,88,128]{2,1,0:T(8,128)(2,1)S(1)}, bf16[32,88,128]{2,1,0:T(8,128)(2,1)S(1)}, u32[]{:S(2)}, u32[]{:S(2)}) collective-permute-start(bf16[32,88,128]{2,1,0:T(8,128)(2,1)S(1)} %all_to_all.21.own_ref), channel_id=1, source_target_pairs={{0,4},{4,0},{8,12},{12,8},{16,20},{20,16},{24,28},{28,24},{1,5},{5... | collective-permute-start | bytes 2162696 | tf_op jit(solution)/shard_map/ppermute | solution.py:519
  64.0 1.5 %collective-permute-start.2 = (bf16[8,128,128]{2,1,0:T(8,128)(2,1)S(1)}, bf16[8,128,128]{2,1,0:T(8,128)(2,1)S(1)}, u32[]{:S(2)}, u32[]{:S(2)}) collective-permute-start(bf16[8,128,128]{2,1,0:T(8,128)(2,1)S(1)} %get-tuple-element.38), channel_id=1, source_target_pairs={{0,8},{4,12},{8,0},{12,4},{16,24},{20,28},{24,16},{28,20},{1,9},{5... | collective-permute-start | bytes 786440 | tf_op jit(solution)/shard_map/ppermute | solution.py:519
  65.5 0.5 shard_map.143
  66.0 1.2 shard_map.142
  67.2 5.1 %collective-permute-done.2.couple_theirs_ref = bf16[8,128,128]{2,1,0:T(8,128)(2,1)S(1)} collective-permute-done((bf16[8,128,128]{2,1,0:T(8,128)(2,1)S(1)}, bf16[8,128,128]{2,1,0:T(8,128)(2,1)S(1)}, u32[]{:S(2)}, u32[]{:S(2)}) %collective-permute-start.2) | collective-permute-done | bytes 262176 | tf_op jit(solution)/shard_map/ppermute | solution.py:519
  72.3 4.2 %shard_map.144 = (bf16[8,128,128]{2,1,0:T(8,128)(2,1)S(1)}, bf16[8,128,128]{2,1,0:T(8,128)(2,1)S(1)}, bf16[4096,128]{1,0:T(8,128)(2,1)S(1)}) custom-call(s32[1]{0:T(128)} %bitcast.core_ref, s32[1]{0:T(128)} %bitcast.1.side_ref, s32[1]{0:T(128)} %bitcast.4.first_mine_ref, s32[1]{0:T(128)} %bitcast.5.first_theirs_ref, s32[256]{0:T(256)S(1)} %copy-done.5, ...), custom_call_target="tpu_custom_call" | custom-call | flops 2147483648 | bytes 1048576 | tf_op jit(solution)/shard_map/pallas_call | solution.py:75
  76.5 28.1 %all_to_all.22.in_ref = bf16[32,128,128]{2,1,0:T(8,128)(2,1)S(1)} all-to-all(bf16[32,128,128]{2,1,0:T(8,128)(2,1)S(1)} %bitcast.10), channel_id=1, replica_groups=mesh['branch'=8,'dap'=4] {'branch','dap'}, dimensions={0} | all-to-all | bytes 2097152 | tf_op jit(solution)/shard_map/all_to_all | solution.py:516
  104.6 1.1 shard_map.146
  105.8 4.6 %all-to-all-start.3 = ((bf16[32,32,256]{2,1,0:T(8,128)(2,1)}), bf16[32,32,256]{2,1,0:T(8,128)(2,1)S(1)}, u32[]{:S(2)}, u32[]{:S(2)}) async-start(bf16[32,32,256]{2,1,0:T(8,128)(2,1)} %shard_map.146), calls=%async_computation.3 | async-start | bytes 1048576 | tf_op jit(solution)/shard_map/all_to_all | solution.py:516
  110.3 1.8 %collective-permute-start.3 = (bf16[8,128,128]{2,1,0:T(8,128)(2,1)S(1)}, bf16[8,128,128]{2,1,0:T(8,128)(2,1)S(1)}, u32[]{:S(2)}, u32[]{:S(2)}) collective-permute-start(bf16[8,128,128]{2,1,0:T(8,128)(2,1)S(1)} %get-tuple-element.43), channel_id=1, source_target_pairs={{0,8},{4,12},{8,0},{12,4},{16,24},{20,28},{24,16},{28,20},{1,9},{5... | collective-permute-start | bytes 786440 | tf_op jit(solution)/shard_map/ppermute | solution.py:519
  112.2 11.5 %collective-permute-done.3.theirs_ref = bf16[8,128,128]{2,1,0:T(8,128)(2,1)S(1)} collective-permute-done((bf16[8,128,128]{2,1,0:T(8,128)(2,1)S(1)}, bf16[8,128,128]{2,1,0:T(8,128)(2,1)S(1)}, u32[]{:S(2)}, u32[]{:S(2)}) %collective-permute-start.3) | collective-permute-done | bytes 262176 | tf_op jit(solution)/shard_map/ppermute | solution.py:519
  123.7 1.2 shard_map.145
  124.9 1.4 %shard_map.147 = bf16[8,256,128]{2,1,0:T(8,128)(2,1)} custom-call(s32[1]{0:T(128)} %bitcast.1.side_ref, bf16[8,128,128]{2,1,0:T(8,128)(2,1)S(1)} %get-tuple-element.42.mine_ref, bf16[8,128,128]{2,1,0:T(8,128)(2,1)S(1)} %collective-permute-done.3.theirs_ref, f32[8,128,128]{2,1,0:T(8,128)S(1)} %get-tuple-element.44.mine_gate_ref, ...), custom_call_target="tpu_custom_call" | custom-call | flops 134217728 | bytes 1048576 | tf_op jit(solution)/shard_map/pallas_call | solution.py:75
  (19 shorter events, 0.3 us)
Async XLA Ops:
  24.1 9.2 %collective-permute-start = (bf16[32,32,256]{2,1,0:T(8,128)(2,1)S(1)}, bf16[32,32,256]{2,1,0:T(8,128)(2,1)S(1)}, u32[]{:S(2)}, u32[]{:S(2)}) collective-permute-start(bf16[32,32,256]{2,1,0:T(8,128)(2,1)S(1)} %all_to_all.20.own_ref), channel_id=1, source_target_pairs={{0,4},{4,0},{8,12},{12,8},{16,20},{20,16},{24,28},{28,24},{1,5},{5... | collective-permute-start | bytes 1572872 | tf_op jit(solution)/shard_map/ppermute | solution.py:519
  25.3 0.8 copy-start.3
  29.9 1.0 copy-start.6
  30.9 0.8 copy-start.7
  31.6 0.8 copy-start.8
  32.4 0.8 copy-start.9
  33.3 32.3 %copy-start = (bf16[1024,128]{1,0:T(8,128)(2,1)S(1)}, bf16[1024,128]{1,0:T(8,128)(2,1)}, u32[]{:S(2)}) copy-start(bf16[1024,128]{1,0:T(8,128)(2,1)} %merge_ref.3) | copy-start | bytes 786436
  33.3 32.3 %copy-start.1 = (bf16[128,512]{1,0:T(8,128)(2,1)S(1)}, bf16[128,512]{1,0:T(8,128)(2,1)}, u32[]{:S(2)}) copy-start(bf16[128,512]{1,0:T(8,128)(2,1)} %entry_ref.1) | copy-start | bytes 393220
  33.3 32.3 %copy-start.4 = (bf16[128,128]{1,0:T(8,128)(2,1)S(1)}, bf16[128,128]{1,0:T(8,128)(2,1)}, u32[]{:S(2)}) copy-start(bf16[128,128]{1,0:T(8,128)(2,1)} %close_ref.1) | copy-start | bytes 98308
  62.5 9.8 %collective-permute-start.1 = (bf16[32,88,128]{2,1,0:T(8,128)(2,1)S(1)}, bf16[32,88,128]{2,1,0:T(8,128)(2,1)S(1)}, u32[]{:S(2)}, u32[]{:S(2)}) collective-permute-start(bf16[32,88,128]{2,1,0:T(8,128)(2,1)S(1)} %all_to_all.21.own_ref), channel_id=1, source_target_pairs={{0,4},{4,0},{8,12},{12,8},{16,20},{20,16},{24,28},{28,24},{1,5},{5... | collective-permute-start | bytes 2162696 | tf_op jit(solution)/shard_map/ppermute | solution.py:519
  64.0 8.2 %collective-permute-start.2 = (bf16[8,128,128]{2,1,0:T(8,128)(2,1)S(1)}, bf16[8,128,128]{2,1,0:T(8,128)(2,1)S(1)}, u32[]{:S(2)}, u32[]{:S(2)}) collective-permute-start(bf16[8,128,128]{2,1,0:T(8,128)(2,1)S(1)} %get-tuple-element.38), channel_id=1, source_target_pairs={{0,8},{4,12},{8,0},{12,4},{16,24},{20,28},{24,16},{28,20},{1,9},{5... | collective-permute-start | bytes 786440 | tf_op jit(solution)/shard_map/ppermute | solution.py:519
  66.0 6.2 %copy-start.5 = (s32[256]{0:T(256)S(1)}, s32[256]{0:T(256)}, u32[]{:S(2)}) copy-start(s32[256]{0:T(256)} %marks_ref.1) | copy-start | bytes 3076
  76.5 47.2 %copy-start.2 = (bf16[128,128]{1,0:T(8,128)(2,1)S(1)}, bf16[128,128]{1,0:T(8,128)(2,1)}, u32[]{:S(2)}) copy-start(bf16[128,128]{1,0:T(8,128)(2,1)} %weight_ref.1) | copy-start | bytes 98308
  105.8 19.1 %all-to-all-start.3 = ((bf16[32,32,256]{2,1,0:T(8,128)(2,1)}), bf16[32,32,256]{2,1,0:T(8,128)(2,1)S(1)}, u32[]{:S(2)}, u32[]{:S(2)}) async-start(bf16[32,32,256]{2,1,0:T(8,128)(2,1)} %shard_map.146), calls=%async_computation.3 | async-start | bytes 1048576 | tf_op jit(solution)/shard_map/all_to_all | solution.py:516
  110.3 13.4 %collective-permute-start.3 = (bf16[8,128,128]{2,1,0:T(8,128)(2,1)S(1)}, bf16[8,128,128]{2,1,0:T(8,128)(2,1)S(1)}, u32[]{:S(2)}, u32[]{:S(2)}) collective-permute-start(bf16[8,128,128]{2,1,0:T(8,128)(2,1)S(1)} %get-tuple-element.43), channel_id=1, source_target_pairs={{0,8},{4,12},{8,0},{12,4},{16,24},{20,28},{24,16},{28,20},{1,9},{5... | collective-permute-start | bytes 786440 | tf_op jit(solution)/shard_map/ppermute | solution.py:519

commit v4 on v3

--- a/solution.py
+++ b/solution.py
@@ -10,6 +10,7 @@
 
 
 EPSILON = 1e-05
+LOG2E = 1.4426950408889634
 EVERY = ("branch", "dap")
 VMEM = pltpu.VMEM
 F32 = jnp.float32
@@ -203,6 +204,97 @@
     blank = jnp.zeros((head_width, residues), BF16)
     lane_half = lax.broadcasted_iota(jnp.int32, (residues, half), 1) // head_width
 
+    width = right_w_ref.shape[0]
+    part = width // 2
+    columns = message_ref.shape[2]
+    span = seqs * part
+    first_lane = lax.broadcasted_iota(jnp.int32, (residues, half), 1) == 0
+    flat = jnp.where(first_lane, jnp.ones((), BF16), zero)
+    first_row = lax.broadcasted_iota(jnp.int32, (head_width, residues), 0) == 0
+
+    def run(plain):
+        waiting = []
+
+        def advance():
+            if waiting:
+                waiting.pop(0)()
+
+        def finish(u, mixed):
+            s = step * batch + u
+            present = keep_ref[pl.ds(s, 1), :].astype(F32)
+            held = {}
+
+            def merge():
+                first = jnp.where(core == 0, mixed[0], mixed[1])
+                second = jnp.where(core == 0, mixed[1], mixed[0])
+                attended = (jnp.concatenate([first, second], axis=1) * gate_ref[u]).astype(BF16)
+                updated = seq_ref[u].astype(F32) + mm(attended, merge_ref[...])
+                held["updated"] = updated.astype(BF16)
+                new_ref[u] = held["updated"]
+
+            def norm():
+                held["normed"] = normalize(held["updated"]).astype(BF16)
+
+            def right():
+                values = (mm(right_w_ref[...], held["normed"], NT) * present).astype(BF16)
+                at = pl.multiple_of(s * part, part)
+                for t, (core_of, side, _) in enumerate(places):
+                    message_ref[t, pl.ds(at, part), :] = values[
+                        core_of * part : (core_of + 1) * part, side * columns : (side + 1) * columns
+                    ]
+
+            def left():
+                present_column = jnp.broadcast_to(present, (8, residues)).T[:, :1]
+                left_scr[...] += mm(held["normed"], left_w_ref[s]) * present_column
+
+            waiting.extend([merge, norm, right, left])
+
+        for u in range(batch):
+            keep = keep_ref[pl.ds(step * batch + u, 1), :]
+            if plain:
+                masking = jnp.where(keep == 1, 0.0, -1000000000.0).astype(F32)
+            else:
+                mask = jnp.where(first_row & (keep == 0), -1e30, 0.0).astype(BF16)
+            mixed = []
+            for k, group in ((0, core), (1, 1 - core)):
+                queries, values = (
+                    jnp.where(group == 0, ref[u, :, :half], ref[u, :, half:])
+                    for ref in (query_ref, value_ref)
+                )
+                keys = jnp.where(group == 0, key_ref[u, :half, :], key_ref[u, half:, :])
+                if not plain:
+                    queries = jnp.concatenate([queries, flat], axis=1)
+                weights, tables = [], []
+                for h in range(some_heads):
+                    only = [
+                        keys[g * head_width : (g + 1) * head_width] if g == h else blank
+                        for g in range(some_heads)
+                    ]
+                    bias = bias_scr[k * some_heads + h]
+                    if plain:
+                        logits = mm(queries, jnp.concatenate(only, axis=0)) * scale
+                        logits = logits + bias + masking
+                        logits = logits - jnp.max(logits, axis=-1, keepdims=True)
+                        weights.append(jnp.exp(logits).astype(BF16))
+                    else:
+                        only += [mask] + [blank] * (some_heads - 1)
+                        logits = mm(queries, jnp.concatenate(only, axis=0)) * (scale * LOG2E)
+                        logits = logits + bias
+                        logits = logits - jnp.max(logits, axis=-1, keepdims=True)
+                        weights.append(jnp.exp2(logits).astype(BF16))
+                    tables.append(jnp.where(lane_half == h, values, zero))
+                    if h % 2 == 1:
+                        advance()
+                table = jnp.concatenate([jnp.concatenate(tables, axis=0), ones_scr[...]], axis=1)
+                total = mm(jnp.concatenate(weights, axis=1), table)
+                mixed.append(total[:, :half] * (1.0 / total[:, half:]))
+            finish(u, mixed)
+        while waiting:
+            advance()
+
+    some = jnp.max(keep_ref[...].astype(F32), axis=1, keepdims=True)
+    plain = jnp.min(some) == 0.0
+
     @pl.when(step == 0)
     def _():
         left_scr[...] = jnp.zeros_like(left_scr)
@@ -210,6 +302,7 @@
             ones_scr[h * residues : (h + 1) * residues, :] = jnp.where(
                 lane_half == h, jnp.ones((), BF16), zero
             )
+        unit = jnp.where(plain, 1.0, LOG2E)
         for k, ref in enumerate((own_ref, other_ref)):
             for h in range(some_heads):
                 if raw:
@@ -218,52 +311,10 @@
                     tile = tile.reshape(residues, residues)
                 else:
                     tile = ref[h].astype(F32)
-                bias_scr[k * some_heads + h] = tile
-
-    width = right_w_ref.shape[0]
-    part = width // 2
-    columns = message_ref.shape[2]
-    span = seqs * part
-    for u in range(batch):
-        s = step * batch + u
-        keep = keep_ref[pl.ds(s, 1), :]
-        present = keep.astype(F32)
-        masking = jnp.where(keep == 1, 0.0, -1000000000.0).astype(F32)
-        mixed = []
-        for k, group in ((0, core), (1, 1 - core)):
-            queries, values = (
-                jnp.where(group == 0, ref[u, :, :half], ref[u, :, half:])
-                for ref in (query_ref, value_ref)
-            )
-            keys = jnp.where(group == 0, key_ref[u, :half, :], key_ref[u, half:, :])
-            weights, tables = [], []
-            for h in range(some_heads):
-                only = [
-                    keys[g * head_width : (g + 1) * head_width] if g == h else blank
-                    for g in range(some_heads)
-                ]
-                logits = mm(queries, jnp.concatenate(only, axis=0)) * scale
-                logits = logits + bias_scr[k * some_heads + h] + masking
-                logits = logits - jnp.max(logits, axis=-1, keepdims=True)
-                weights.append(jnp.exp(logits).astype(BF16))
-                tables.append(jnp.where(lane_half == h, values, zero))
-            table = jnp.concatenate([jnp.concatenate(tables, axis=0), ones_scr[...]], axis=1)
-            total = mm(jnp.concatenate(weights, axis=1), table)
-            mixed.append(total[:, :half] / total[:, half:])
-        first = jnp.where(core == 0, mixed[0], mixed[1])
-        second = jnp.where(core == 0, mixed[1], mixed[0])
-        attended = (jnp.concatenate([first, second], axis=1) * gate_ref[u]).astype(BF16)
-        updated = (seq_ref[u].astype(F32) + mm(attended, merge_ref[...])).astype(BF16)
-        new_ref[u] = updated
-        normed = normalize(updated).astype(BF16)
-        right = (mm(right_w_ref[...], normed, NT) * present).astype(BF16)
-        at = pl.multiple_of(s * part, part)
-        for t, (core_of, side, _) in enumerate(places):
-            message_ref[t, pl.ds(at, part), :] = right[
-                core_of * part : (core_of + 1) * part, side * columns : (side + 1) * columns
-            ]
-        present_column = jnp.broadcast_to(present, (8, residues)).T[:, :1]
-        left_scr[...] += mm(normed, left_w_ref[s]) * present_column
+                bias_scr[k * some_heads + h] = tile * unit
+
+    pl.when(plain)(functools.partial(run, True))
+    pl.when(jnp.logical_not(plain))(functools.partial(run, False))
 
     @pl.when(step == pl.num_programs(0) - 1)
     def _():
@@ -386,14 +437,18 @@
     observed = observed_ref[:, pl.ds(half, columns)].astype(F32)
     row_marks = [marks_ref[first_mine + r] for r in range(rows)]
     row_marks += [marks_ref[first_theirs + r] for r in range(rows)]
-    for i in range(0, block, 2):
-        update = sum(
+    updates, norms = {}, {}
+
+    def project(i):
+        updates[i] = sum(
             mm(table, jnp.concatenate([values[i], values[i + 1]], axis=1))
             for table, values in tables
         )
+
+    def add(i):
         normed = []
         for d in range(2):
-            piece = update[:, d * columns : (d + 1) * columns] * scale[i + d : i + d + 1, :]
+            piece = updates[i][:, d * columns : (d + 1) * columns] * scale[i + d : i + d + 1, :]
             couple_ref, pair_ref = (
                 (couple_mine_ref, pair_mine_ref)
                 if i + d < rows
@@ -403,13 +458,20 @@
             pair = (couple_ref[r].astype(F32) + piece.T).astype(BF16)
             pair_ref[r] = pair
             normed.append(normalize(pair).astype(BF16))
-        normed = jnp.concatenate(normed, axis=0)
-        edge = mm(value_w_ref[...], normed, NT) * sigmoid(mm(gate_w_ref[...], normed, NT))
+        norms[i] = jnp.concatenate(normed, axis=0)
+
+    def edge(i):
+        values = mm(value_w_ref[...], norms[i], NT) * sigmoid(mm(gate_w_ref[...], norms[i], NT))
         for d in range(2):
             mark = observed * row_marks[i + d].astype(F32)
             edge_scr[pl.ds(i + d, 2 * channels, stride=block), :] = (
-                edge[:, d * columns : (d + 1) * columns] * mark
+                values[:, d * columns : (d + 1) * columns] * mark
             )
+
+    for i in range(0, block + 4, 2):
+        for stage, late in ((project, 0), (add, 2), (edge, 4)):
+            if 0 <= i - late < block:
+                stage(i - late)
     size = edges_refs[0].shape[0]
     for k, ref in enumerate(edges_refs):
         ref[...] = edge_scr[k * size : (k + 1) * size, :].astype(BF16)
@@ -594,7 +656,7 @@
     )(stay(homolog_embedding), stay(lookup_kernels), stay(heads_sigmoid_kernel))
     span = seqs * width // 2
     depth = span + block + 2 * seqs
-    batch = 2 if seqs % 2 == 0 else 1
+    batch = seqs
     homolog_refreshed, message = pl.pallas_call(
         functools.partial(attend_kernel, heads, places, raw),
         grid=(seqs // batch,),

time: 127 us -> 126 us (level)
  no operation moved by 1% of the time
where the time goes in v4:
time: 126 us; the launch traced here: 125 us
  blocking collectives  70.5 us (56%)
  Pallas kernels  22.5 us (18%)
  waiting for transfers between devices  16.6 us (13%)
  starting transfers between devices  10.7 us (8%)
  local copies, waits for them, and re-layouts  4.17 us (3%)
    all_to_all x3, blocking collectives, exchange(): lax.all_to_all(values, EVERY, split_axis=0, concat_axis=0, tiled=True)  70.5 us
    ppermute x4, waiting for transfers between devices, permute(): return lax.ppermute(values, 'branch', pairs)  16.6 us
    pallas_call x8, Pallas kernels, call(): pl.pallas_call(body, out_shape=out, in_specs=in_specs or [vspec() for _ i...  11.6 us
    pallas_call x1, Pallas kernels, per_device(): pl.pallas_call(functools.partial(attend_kernel, heads, places, raw), grid...  7.41 us
    ppermute x4, starting transfers between devices, permute(): return lax.ppermute(values, 'branch', pairs)  6.13 us
    all_to_all x1, starting transfers between devices, exchange(): lax.all_to_all(values, EVERY, split_axis=0, concat_axis=0, tiled=True)  4.55 us
    unnamed x20, local copies, waits for them, and re-layouts  4.17 us
    pallas_call x1, Pallas kernels, per_device(): pl.pallas_call(project_kernel, grid=(seqs,), out_shape=(jax.ShapeDtypeStr...  3.53 us
  transfers between devices with their start and end apart: 5, of which 2 were waited for; matrix products, arithmetic and copies ran while one was open for 0% of the time, Pallas kernels for 5%

profile of v4, /device:TPU:0, one launch (start us, length us, event | category | flops | bytes accessed | tf_op | source)
XLA Modules:
  0.0 125.2 jit_solution(125630242921213062)
XLA Ops:
  0.7 2.0 %shard_map.140 = (bf16[32,32,256]{2,1,0:T(8,128)(2,1)S(1)}, bf16[8,128,128]{2,1,0:T(8,128)(2,1)S(1)}, bf16[8,128,128]{2,1,0:T(8,128)(2,1)S(1)}) custom-call(s32[1]{0:T(128)} %bitcast.1.side_ref, bf16[8,256,128]{2,1,0:T(8,128)(2,1)} %couple_ref.1, bf16[8,128]{1,0:T(8,128)(2,1)} %bitcast.13), custom_call_target="tpu_custom_call" | custom-call | bytes 1048576 | tf_op jit(solution)/shard_map/pallas_call | solution.py:76
  2.7 21.4 %all_to_all.20.own_ref = bf16[32,32,256]{2,1,0:T(8,128)(2,1)S(1)} all-to-all(bf16[32,32,256]{2,1,0:T(8,128)(2,1)S(1)} %get-tuple-element.29), channel_id=1, replica_groups=mesh['branch'=8,'dap'=4] {'branch','dap'}, dimensions={0} | all-to-all | bytes 1048576 | tf_op jit(solution)/shard_map/all_to_all | solution.py:578
  24.1 1.3 %collective-permute-start = (bf16[32,32,256]{2,1,0:T(8,128)(2,1)S(1)}, bf16[32,32,256]{2,1,0:T(8,128)(2,1)S(1)}, u32[]{:S(2)}, u32[]{:S(2)}) collective-permute-start(bf16[32,32,256]{2,1,0:T(8,128)(2,1)S(1)} %all_to_all.20.own_ref), channel_id=1, source_target_pairs={{0,4},{4,0},{8,12},{12,8},{16,20},{20,16},{24,28},{28,24},{1,5},{5... | collective-permute-start | bytes 1572872 | tf_op jit(solution)/shard_map/ppermute | solution.py:581
  25.3 0.8 copy-done.3
  26.3 3.5 %project.1 = (bf16[4,256,256]{2,1,0:T(8,128)(2,1)S(1)}, bf16[4,256,256]{2,1,0:T(8,128)(2,1)S(1)}, bf16[4,256,256]{2,1,0:T(8,128)(2,1)S(1)}, f32[4,256,256]{2,1,0:T(8,128)S(1)}) custom-call(bf16[4,256,256]{2,1,0:T(8,128)(2,1)} %seq_ref.3, bf16[256,768]{1,0:T(8,128)(2,1)} %qkv_w_ref.1, bf16[256,256]{1,0:T(8,128)(2,1)} %gate_w_ref.1), custom_call_target="tpu_custom_call" | custom-call | flops 536870912 | bytes 4194304 | tf_op jit(solution)/shard_map/project/pallas_call | solution.py:633
  29.9 1.0 copy-done.6
  30.9 0.8 copy-done.7
  31.7 0.8 copy-done.8
  32.5 0.8 copy-done.9
  33.3 7.4 %attend.1 = (bf16[4,256,256]{2,1,0:T(8,128)(2,1)}, bf16[32,88,128]{2,1,0:T(8,128)(2,1)S(1)}) custom-call(s32[1]{0:T(128)} %bitcast.core_ref, bf16[4,256,256]{2,1,0:T(8,128)(2,1)} %seq_ref.3, s32[4,256]{1,0:T(4,128)} %keep_ref.1, bf16[4,256,256]{2,1,0:T(8,128)(2,1)} %copy-done.7, bf16[4,256,256]{2,1,0:T(8,128)(2,1)} %copy-done.8, ...), custom_call_target="tpu_custom_call" | custom-call | flops 2147483648 | bytes 4194304 | tf_op jit(solution)/shard_map/attend/pallas_call | solution.py:660
  40.7 20.9 %all_to_all.21.own_ref = bf16[32,88,128]{2,1,0:T(8,128)(2,1)S(1)} all-to-all(bf16[32,88,128]{2,1,0:T(8,128)(2,1)S(1)} %get-tuple-element.33), channel_id=1, replica_groups=mesh['branch'=8,'dap'=4] {'branch','dap'}, dimensions={0} | all-to-all | bytes 1441792 | tf_op jit(solution)/shard_map/all_to_all | solution.py:578
  61.6 1.5 %collective-permute-start.1 = (bf16[32,88,128]{2,1,0:T(8,128)(2,1)S(1)}, bf16[32,88,128]{2,1,0:T(8,128)(2,1)S(1)}, u32[]{:S(2)}, u32[]{:S(2)}) collective-permute-start(bf16[32,88,128]{2,1,0:T(8,128)(2,1)S(1)} %all_to_all.21.own_ref), channel_id=1, source_target_pairs={{0,4},{4,0},{8,12},{12,8},{16,20},{20,16},{24,28},{28,24},{1,5},{5... | collective-permute-start | bytes 2162696 | tf_op jit(solution)/shard_map/ppermute | solution.py:581
  63.2 1.5 %collective-permute-start.2 = (bf16[8,128,128]{2,1,0:T(8,128)(2,1)S(1)}, bf16[8,128,128]{2,1,0:T(8,128)(2,1)S(1)}, u32[]{:S(2)}, u32[]{:S(2)}) collective-permute-start(bf16[8,128,128]{2,1,0:T(8,128)(2,1)S(1)} %get-tuple-element.38), channel_id=1, source_target_pairs={{0,8},{4,12},{8,0},{12,4},{16,24},{20,28},{24,16},{28,20},{1,9},{5... | collective-permute-start | bytes 786440 | tf_op jit(solution)/shard_map/ppermute | solution.py:581
  64.7 0.5 shard_map.143
  65.2 1.2 shard_map.142
  66.3 5.1 %collective-permute-done.2.couple_theirs_ref = bf16[8,128,128]{2,1,0:T(8,128)(2,1)S(1)} collective-permute-done((bf16[8,128,128]{2,1,0:T(8,128)(2,1)S(1)}, bf16[8,128,128]{2,1,0:T(8,128)(2,1)S(1)}, u32[]{:S(2)}, u32[]{:S(2)}) %collective-permute-start.2) | collective-permute-done | bytes 262176 | tf_op jit(solution)/shard_map/ppermute | solution.py:581
  71.4 4.0 %shard_map.144 = (bf16[8,128,128]{2,1,0:T(8,128)(2,1)S(1)}, bf16[8,128,128]{2,1,0:T(8,128)(2,1)S(1)}, bf16[4096,128]{1,0:T(8,128)(2,1)S(1)}) custom-call(s32[1]{0:T(128)} %bitcast.core_ref, s32[1]{0:T(128)} %bitcast.1.side_ref, s32[1]{0:T(128)} %bitcast.4.first_mine_ref, s32[1]{0:T(128)} %bitcast.5.first_theirs_ref, s32[256]{0:T(256)S(1)} %copy-done.5, ...), custom_call_target="tpu_custom_call" | custom-call | flops 2147483648 | bytes 1048576 | tf_op jit(solution)/shard_map/pallas_call | solution.py:76
  75.4 28.1 %all_to_all.22.in_ref = bf16[32,128,128]{2,1,0:T(8,128)(2,1)S(1)} all-to-all(bf16[32,128,128]{2,1,0:T(8,128)(2,1)S(1)} %bitcast.10), channel_id=1, replica_groups=mesh['branch'=8,'dap'=4] {'branch','dap'}, dimensions={0} | all-to-all | bytes 2097152 | tf_op jit(solution)/shard_map/all_to_all | solution.py:578
  103.5 1.1 shard_map.146
  104.7 4.5 %all-to-all-start.3 = ((bf16[32,32,256]{2,1,0:T(8,128)(2,1)}), bf16[32,32,256]{2,1,0:T(8,128)(2,1)S(1)}, u32[]{:S(2)}, u32[]{:S(2)}) async-start(bf16[32,32,256]{2,1,0:T(8,128)(2,1)} %shard_map.146), calls=%async_computation.3 | async-start | bytes 1048576 | tf_op jit(solution)/shard_map/all_to_all | solution.py:578
  109.2 1.8 %collective-permute-start.3 = (bf16[8,128,128]{2,1,0:T(8,128)(2,1)S(1)}, bf16[8,128,128]{2,1,0:T(8,128)(2,1)S(1)}, u32[]{:S(2)}, u32[]{:S(2)}) collective-permute-start(bf16[8,128,128]{2,1,0:T(8,128)(2,1)S(1)} %get-tuple-element.43), channel_id=1, source_target_pairs={{0,8},{4,12},{8,0},{12,4},{16,24},{20,28},{24,16},{28,20},{1,9},{5... | collective-permute-start | bytes 786440 | tf_op jit(solution)/shard_map/ppermute | solution.py:581
  111.1 11.5 %collective-permute-done.3.theirs_ref = bf16[8,128,128]{2,1,0:T(8,128)(2,1)S(1)} collective-permute-done((bf16[8,128,128]{2,1,0:T(8,128)(2,1)S(1)}, bf16[8,128,128]{2,1,0:T(8,128)(2,1)S(1)}, u32[]{:S(2)}, u32[]{:S(2)}) %collective-permute-start.3) | collective-permute-done | bytes 262176 | tf_op jit(solution)/shard_map/ppermute | solution.py:581
  122.6 1.2 shard_map.145
  123.8 1.4 %shard_map.147 = bf16[8,256,128]{2,1,0:T(8,128)(2,1)} custom-call(s32[1]{0:T(128)} %bitcast.1.side_ref, bf16[8,128,128]{2,1,0:T(8,128)(2,1)S(1)} %get-tuple-element.42.mine_ref, bf16[8,128,128]{2,1,0:T(8,128)(2,1)S(1)} %collective-permute-done.3.theirs_ref, f32[8,128,128]{2,1,0:T(8,128)S(1)} %get-tuple-element.44.mine_gate_ref, ...), custom_call_target="tpu_custom_call" | custom-call | flops 134217728 | bytes 1048576 | tf_op jit(solution)/shard_map/pallas_call | solution.py:76
  (19 shorter events, 0.3 us)
Async XLA Ops:
  24.1 9.2 %collective-permute-start = (bf16[32,32,256]{2,1,0:T(8,128)(2,1)S(1)}, bf16[32,32,256]{2,1,0:T(8,128)(2,1)S(1)}, u32[]{:S(2)}, u32[]{:S(2)}) collective-permute-start(bf16[32,32,256]{2,1,0:T(8,128)(2,1)S(1)} %all_to_all.20.own_ref), channel_id=1, source_target_pairs={{0,4},{4,0},{8,12},{12,8},{16,20},{20,16},{24,28},{28,24},{1,5},{5... | collective-permute-start | bytes 1572872 | tf_op jit(solution)/shard_map/ppermute | solution.py:581
  25.3 0.8 copy-start.3
  29.9 1.0 copy-start.6
  30.9 0.8 copy-start.7
  31.7 0.8 copy-start.8
  32.5 0.8 copy-start.9
  33.3 31.4 %copy-start = (bf16[1024,128]{1,0:T(8,128)(2,1)S(1)}, bf16[1024,128]{1,0:T(8,128)(2,1)}, u32[]{:S(2)}) copy-start(bf16[1024,128]{1,0:T(8,128)(2,1)} %merge_ref.3) | copy-start | bytes 786436
  33.3 31.4 %copy-start.1 = (bf16[128,512]{1,0:T(8,128)(2,1)S(1)}, bf16[128,512]{1,0:T(8,128)(2,1)}, u32[]{:S(2)}) copy-start(bf16[128,512]{1,0:T(8,128)(2,1)} %entry_ref.1) | copy-start | bytes 393220
  33.3 31.4 %copy-start.4 = (bf16[128,128]{1,0:T(8,128)(2,1)S(1)}, bf16[128,128]{1,0:T(8,128)(2,1)}, u32[]{:S(2)}) copy-start(bf16[128,128]{1,0:T(8,128)(2,1)} %close_ref.1) | copy-start | bytes 98308
  61.6 9.8 %collective-permute-start.1 = (bf16[32,88,128]{2,1,0:T(8,128)(2,1)S(1)}, bf16[32,88,128]{2,1,0:T(8,128)(2,1)S(1)}, u32[]{:S(2)}, u32[]{:S(2)}) collective-permute-start(bf16[32,88,128]{2,1,0:T(8,128)(2,1)S(1)} %all_to_all.21.own_ref), channel_id=1, source_target_pairs={{0,4},{4,0},{8,12},{12,8},{16,20},{20,16},{24,28},{28,24},{1,5},{5... | collective-permute-start | bytes 2162696 | tf_op jit(solution)/shard_map/ppermute | solution.py:581
  63.2 8.2 %collective-permute-start.2 = (bf16[8,128,128]{2,1,0:T(8,128)(2,1)S(1)}, bf16[8,128,128]{2,1,0:T(8,128)(2,1)S(1)}, u32[]{:S(2)}, u32[]{:S(2)}) collective-permute-start(bf16[8,128,128]{2,1,0:T(8,128)(2,1)S(1)} %get-tuple-element.38), channel_id=1, source_target_pairs={{0,8},{4,12},{8,0},{12,4},{16,24},{20,28},{24,16},{28,20},{1,9},{5... | collective-permute-start | bytes 786440 | tf_op jit(solution)/shard_map/ppermute | solution.py:581
  65.1 6.2 %copy-start.5 = (s32[256]{0:T(256)S(1)}, s32[256]{0:T(256)}, u32[]{:S(2)}) copy-start(s32[256]{0:T(256)} %marks_ref.1) | copy-start | bytes 3076
  75.4 47.2 %copy-start.2 = (bf16[128,128]{1,0:T(8,128)(2,1)S(1)}, bf16[128,128]{1,0:T(8,128)(2,1)}, u32[]{:S(2)}) copy-start(bf16[128,128]{1,0:T(8,128)(2,1)} %weight_ref.1) | copy-start | bytes 98308
  104.7 19.1 %all-to-all-start.3 = ((bf16[32,32,256]{2,1,0:T(8,128)(2,1)}), bf16[32,32,256]{2,1,0:T(8,128)(2,1)S(1)}, u32[]{:S(2)}, u32[]{:S(2)}) async-start(bf16[32,32,256]{2,1,0:T(8,128)(2,1)} %shard_map.146), calls=%async_computation.3 | async-start | bytes 1048576 | tf_op jit(solution)/shard_map/all_to_all | solution.py:578
  109.2 13.4 %collective-permute-start.3 = (bf16[8,128,128]{2,1,0:T(8,128)(2,1)S(1)}, bf16[8,128,128]{2,1,0:T(8,128)(2,1)S(1)}, u32[]{:S(2)}, u32[]{:S(2)}) collective-permute-start(bf16[8,128,128]{2,1,0:T(8,128)(2,1)S(1)} %get-tuple-element.43), channel_id=1, source_target_pairs={{0,8},{4,12},{8,0},{12,4},{16,24},{20,28},{24,16},{28,20},{1,9},{5... | collective-permute-start | bytes 786440 | tf_op jit(solution)/shard_map/ppermute | solution.py:581

commit v5 on v4

--- a/solution.py
+++ b/solution.py
@@ -106,7 +106,8 @@
         out_ref[t] = halves[core]
 
 
-def prepare_small_kernel(seqs, halves_ref, left_ref, right_ref):
+def prepare_small_kernel(seqs, halves_ref, present_ref, left_ref, right_ref, keep_ref):
+    keep_ref[...] = present_ref[...]
     width = halves_ref.shape[0] // 2
     left = halves_ref[:width].astype(F32).T.astype(BF16)
     for s in range(seqs):
@@ -173,26 +174,28 @@
     places,
     raw,
     core_ref,
-    seq_ref,
     keep_ref,
-    query_ref,
-    key_ref,
-    value_ref,
-    gate_ref,
     own_ref,
     other_ref,
     merge_ref,
     left_w_ref,
     right_w_ref,
-    new_ref,
-    message_ref,
-    left_scr,
-    bias_scr,
-    ones_scr,
+    *rest,
 ):
-    step = pl.program_id(0)
-    batch = seq_ref.shape[0]
-    seqs = keep_ref.shape[0]
+    sources, (new_out, message_out) = rest[:5], rest[5:7]
+    seq_ref, query_ref, key_ref, value_ref, gate_ref = held_refs = rest[7:12]
+    new_ref, message_ref, left_scr, bias_scr, ones_scr, in_sems, new_sems, message_sems = rest[12:]
+    batch = seqs = keep_ref.shape[0]
+    arrivals = [
+        [
+            pltpu.make_async_copy(source.at[u], held.at[u], in_sems.at[k, u])
+            for k, (source, held) in enumerate(zip(sources, held_refs))
+        ]
+        for u in range(seqs)
+    ]
+    for copies in arrivals:
+        for copy in copies:
+            copy.start()
     core = core_ref[0]
     inner = gate_ref.shape[2]
     residues = gate_ref.shape[1]
@@ -212,6 +215,14 @@
     flat = jnp.where(first_lane, jnp.ones((), BF16), zero)
     first_row = lax.broadcasted_iota(jnp.int32, (head_width, residues), 0) == 0
 
+    pieces = message_ref.shape[1] % 8 == 0 and part % 16 == 0
+
+    def departure(u):
+        rows = pl.ds(u * part, part)
+        return pltpu.make_async_copy(
+            message_ref.at[:, rows, :], message_out.at[:, rows, :], message_sems.at[u]
+        )
+
     def run(plain):
         waiting = []
 
@@ -220,7 +231,7 @@
                 waiting.pop(0)()
 
         def finish(u, mixed):
-            s = step * batch + u
+            s = u
             present = keep_ref[pl.ds(s, 1), :].astype(F32)
             held = {}
 
@@ -231,17 +242,19 @@
                 updated = seq_ref[u].astype(F32) + mm(attended, merge_ref[...])
                 held["updated"] = updated.astype(BF16)
                 new_ref[u] = held["updated"]
+                pltpu.make_async_copy(new_ref.at[u], new_out.at[u], new_sems.at[u]).start()
 
             def norm():
                 held["normed"] = normalize(held["updated"]).astype(BF16)
 
             def right():
                 values = (mm(right_w_ref[...], held["normed"], NT) * present).astype(BF16)
-                at = pl.multiple_of(s * part, part)
                 for t, (core_of, side, _) in enumerate(places):
-                    message_ref[t, pl.ds(at, part), :] = values[
+                    message_ref[t, s * part : (s + 1) * part, :] = values[
                         core_of * part : (core_of + 1) * part, side * columns : (side + 1) * columns
                     ]
+                if pieces:
+                    departure(s).start()
 
             def left():
                 present_column = jnp.broadcast_to(present, (8, residues)).T[:, :1]
@@ -250,7 +263,9 @@
             waiting.extend([merge, norm, right, left])
 
         for u in range(batch):
-            keep = keep_ref[pl.ds(step * batch + u, 1), :]
+            for copy in arrivals[u]:
+                copy.wait()
+            keep = keep_ref[pl.ds(u, 1), :]
             if plain:
                 masking = jnp.where(keep == 1, 0.0, -1000000000.0).astype(F32)
             else:
@@ -295,40 +310,46 @@
     some = jnp.max(keep_ref[...].astype(F32), axis=1, keepdims=True)
     plain = jnp.min(some) == 0.0
 
-    @pl.when(step == 0)
-    def _():
-        left_scr[...] = jnp.zeros_like(left_scr)
+    left_scr[...] = jnp.zeros_like(left_scr)
+    for h in range(some_heads):
+        ones_scr[h * residues : (h + 1) * residues, :] = jnp.where(
+            lane_half == h, jnp.ones((), BF16), zero
+        )
+    unit = jnp.where(plain, 1.0, LOG2E)
+    for k, ref in enumerate((own_ref, other_ref)):
         for h in range(some_heads):
-            ones_scr[h * residues : (h + 1) * residues, :] = jnp.where(
-                lane_half == h, jnp.ones((), BF16), zero
-            )
-        unit = jnp.where(plain, 1.0, LOG2E)
-        for k, ref in enumerate((own_ref, other_ref)):
-            for h in range(some_heads):
-                if raw:
-                    rows = residues // len(places)
-                    tile = ref[:, h * rows : (h + 1) * rows, :].astype(F32)
-                    tile = tile.reshape(residues, residues)
-                else:
-                    tile = ref[h].astype(F32)
-                bias_scr[k * some_heads + h] = tile * unit
+            if raw:
+                rows = residues // len(places)
+                tile = ref[:, h * rows : (h + 1) * rows, :].astype(F32)
+                tile = tile.reshape(residues, residues)
+            else:
+                tile = ref[h].astype(F32)
+            bias_scr[k * some_heads + h] = tile * unit
 
     pl.when(plain)(functools.partial(run, True))
     pl.when(jnp.logical_not(plain))(functools.partial(run, False))
 
-    @pl.when(step == pl.num_programs(0) - 1)
-    def _():
-        rows = residues // len(places)
-        marks = keep_ref[...].astype(F32)
-        marks = jnp.concatenate(
-            [marks[:, k * columns : (k + 1) * columns] for k in range(2)], axis=0
-        ).astype(BF16)
-        for t, (_, _, mate) in enumerate(places):
-            block = jnp.concatenate(
-                [left_scr[u * rows : (u + 1) * rows, :] for u in (t, mate)], axis=0
-            )
-            message_ref[t, span : span + 2 * rows, :] = block.astype(BF16)
-            message_ref[t, span + 2 * rows :, :] = marks
+    rows = residues // len(places)
+    marks = keep_ref[...].astype(F32)
+    marks = jnp.concatenate(
+        [marks[:, k * columns : (k + 1) * columns] for k in range(2)], axis=0
+    ).astype(BF16)
+    for t, (_, _, mate) in enumerate(places):
+        tile = jnp.concatenate([left_scr[u * rows : (u + 1) * rows, :] for u in (t, mate)], axis=0)
+        message_ref[t, span : span + 2 * rows, :] = tile.astype(BF16)
+        message_ref[t, span + 2 * rows :, :] = marks
+    if pieces:
+        last = pltpu.make_async_copy(
+            message_ref.at[:, span:, :], message_out.at[:, span:, :], message_sems.at[seqs]
+        )
+    else:
+        last = pltpu.make_async_copy(message_ref, message_out, message_sems.at[seqs])
+    last.start()
+    for u in range(seqs):
+        pltpu.make_async_copy(new_ref.at[u], new_out.at[u], new_sems.at[u]).wait()
+        if pieces:
+            departure(u).wait()
+    last.wait()
 
 
 def multiply(seqs, width, left, ref, scr, products):
@@ -357,15 +378,20 @@
     seqs,
     width,
     rows,
+    core_ref,
     side_ref,
     first_mine_ref,
     first_theirs_ref,
     own_ref,
+    table_ref,
+    observed_ref,
     left_ref,
     scale_ref,
-    products_ref,
+    marks_ref,
+    update_ref,
     right_scr,
     small_scr,
+    products,
 ):
     n, depth, columns = own_ref.shape
     block = 2 * rows
@@ -400,27 +426,30 @@
     chosen = (row_ids == lax.broadcasted_iota(jnp.int32, (pad, 2 * columns), 1)).astype(BF16)
     counts = mm(mm(chosen, keep, NT).astype(BF16), keep_columns)
     scale_ref[...] = 1.0 / jnp.maximum(counts, 1.0)
-    multiply(seqs, width, left, own_ref, right_scr, products_ref)
+    observed = observed_ref[...].astype(F32)
+    row_marks = mm(chosen, jnp.broadcast_to(observed, (8, 2 * columns)).astype(BF16), NT)[:, :1]
+    column_marks = jnp.where(side == 0, observed[:, :columns], observed[:, columns:])
+    marks_ref[...] = row_marks * column_marks
+    multiply(seqs, width, left, own_ref, right_scr, products)
+    table = table_ref[core_ref[0]]
+    for i in range(0, block, 2):
+        update_ref[i // 2] = mm(table, jnp.concatenate([products[i], products[i + 1]], axis=1))
 
 
 def outer_kernel(
     seqs,
     width,
     core_ref,
-    side_ref,
-    first_mine_ref,
-    first_theirs_ref,
-    marks_ref,
     other_ref,
     left_ref,
     scale_ref,
-    own_products_ref,
+    marks_ref,
+    own_update_ref,
     couple_mine_ref,
     couple_theirs_ref,
     table_ref,
     value_w_ref,
     gate_w_ref,
-    observed_ref,
     pair_mine_ref,
     pair_theirs_ref,
     *rest,
@@ -428,22 +457,14 @@
     edges_refs, (right_scr, products, edge_scr) = rest[:-3], rest[-3:]
     rows, columns, channels = couple_mine_ref.shape
     block = 2 * rows
-    core, side = core_ref[0], side_ref[0]
-    first_mine, first_theirs = first_mine_ref[0], first_theirs_ref[0]
     multiply(seqs, width, left_ref[...], other_ref, right_scr, products)
     scale = scale_ref[...]
-    tables = ((table_ref[core], own_products_ref), (table_ref[1 - core], products))
-    half = pl.multiple_of(side * columns, columns)
-    observed = observed_ref[:, pl.ds(half, columns)].astype(F32)
-    row_marks = [marks_ref[first_mine + r] for r in range(rows)]
-    row_marks += [marks_ref[first_theirs + r] for r in range(rows)]
+    table = table_ref[1 - core_ref[0]]
     updates, norms = {}, {}
 
     def project(i):
-        updates[i] = sum(
-            mm(table, jnp.concatenate([values[i], values[i + 1]], axis=1))
-            for table, values in tables
-        )
+        part = mm(table, jnp.concatenate([products[i], products[i + 1]], axis=1))
+        updates[i] = own_update_ref[i // 2] + part
 
     def add(i):
         normed = []
@@ -463,7 +484,7 @@
     def edge(i):
         values = mm(value_w_ref[...], norms[i], NT) * sigmoid(mm(gate_w_ref[...], norms[i], NT))
         for d in range(2):
-            mark = observed * row_marks[i + d].astype(F32)
+            mark = marks_ref[i + d : i + d + 1, :]
             edge_scr[pl.ds(i + d, 2 * channels, stride=block), :] = (
                 values[:, d * columns : (d + 1) * columns] * mark
             )
@@ -580,13 +601,14 @@
     def permute(values, pairs):
         return lax.ppermute(values, "branch", pairs)
 
-    left_w, right_w = call(
+    left_w, right_w, keep = call(
         functools.partial(prepare_small_kernel, seqs),
         (
             jax.ShapeDtypeStruct((seqs, features, seqs * width), BF16),
             jax.ShapeDtypeStruct((width, features), BF16),
+            jax.ShapeDtypeStruct(homolog_present.shape, homolog_present.dtype),
         ),
-        (tensor_halves_kernel.T,),
+        (tensor_halves_kernel.T, stay(homolog_present)),
     )
     table, value_w, gate_w, final_w = call(
         functools.partial(prepare_large_kernel, chunks, per),
@@ -656,64 +678,66 @@
     )(stay(homolog_embedding), stay(lookup_kernels), stay(heads_sigmoid_kernel))
     span = seqs * width // 2
     depth = span + block + 2 * seqs
-    batch = seqs
+    anywhere = pl.BlockSpec(memory_space=pl.ANY)
+    new_shape = (seqs, residues, features)
     homolog_refreshed, message = pl.pallas_call(
         functools.partial(attend_kernel, heads, places, raw),
-        grid=(seqs // batch,),
         out_shape=(
-            jax.ShapeDtypeStruct((seqs, residues, features), BF16),
+            jax.ShapeDtypeStruct(new_shape, BF16),
             jax.ShapeDtypeStruct((n, depth, half), BF16),
         ),
-        in_specs=[
-            sspec(),
-            per_seq(batch, residues, features),
-            whole(seqs, residues),
-            per_seq(batch, residues, inner),
-            per_seq(batch, inner, residues),
-            per_seq(batch, residues, inner),
-            per_seq(batch, residues, inner),
-            whole(*own_bias.shape),
-            whole(*own_bias.shape),
-            whole(inner, features),
-            whole(seqs, features, seqs * width),
-            whole(width, features),
-        ],
-        out_specs=(per_seq(batch, residues, features), whole(n, depth, half)),
+        in_specs=[sspec()] + [vspec()] * 6 + [anywhere] * 5,
+        out_specs=(anywhere, anywhere),
         scratch_shapes=[
+            VMEM(new_shape, BF16),
+            VMEM((seqs, residues, inner), BF16),
+            VMEM((seqs, inner, residues), BF16),
+            VMEM((seqs, residues, inner), BF16),
+            VMEM((seqs, residues, inner), F32),
+            VMEM(new_shape, BF16),
+            VMEM((n, depth, half), BF16),
             VMEM((residues, seqs * width), F32),
             VMEM((heads, residues, residues), F32),
             VMEM((half_heads * residues, half), BF16),
+            pltpu.SemaphoreType.DMA((5, seqs)),
+            pltpu.SemaphoreType.DMA((seqs,)),
+            pltpu.SemaphoreType.DMA((seqs + 1,)),
         ],
         name="attend",
         compiler_params=room(24),
         cost_estimate=pl.CostEstimate(flops=2**31, bytes_accessed=2**22, transcendentals=0),
     )(
         core,
+        keep,
+        own_bias,
+        other_bias,
+        heads_merge_kernel,
+        left_w,
+        right_w,
         stay(homolog_embedding),
-        stay(homolog_present),
         *(stay(values) for values in parts),
         stay(gates),
-        own_bias,
-        other_bias,
-        stay(heads_merge_kernel),
-        left_w,
-        right_w,
     )
 
     own = exchange(message)
     other = permute(own, chip)
     firsts = (first_mine.reshape(1), first_theirs.reshape(1))
-    left, scale, products = call(
+    left, scale, marks, update = call(
         functools.partial(outer_own_kernel, seqs, width, rows),
         (
             jax.ShapeDtypeStruct((block * width, n * seqs), BF16),
             jax.ShapeDtypeStruct((-(-block // 8) * 8, half), F32),
-            jax.ShapeDtypeStruct((block, width // 2 * width, half), BF16),
+            jax.ShapeDtypeStruct((-(-block // 8) * 8, half), F32),
+            jax.ShapeDtypeStruct((block // 2, channels, 2 * half), F32),
         ),
-        (side, *firsts, own),
-        [VMEM((n * span, half), F32), VMEM((n * (depth - span), half), F32)],
+        (core, side, *firsts, own, table, stay(observed_position.reshape(1, residues))),
+        [
+            VMEM((n * span, half), F32),
+            VMEM((n * (depth - span), half), F32),
+            VMEM((block, width // 2 * width, half), BF16),
+        ],
         need=16,
-        in_specs=[sspec()] * 3 + [vspec()],
+        in_specs=[sspec()] * 4 + [vspec()] * 3,
         flops=2**30,
     )
     piece = jax.ShapeDtypeStruct((rows, half, channels), BF16)
@@ -723,19 +747,16 @@
         + (jax.ShapeDtypeStruct((2 * channels * block // chunks, half), BF16),) * chunks,
         (
             core,
-            side,
-            *firsts,
-            observed_position,
             other,
             left,
             scale,
-            products,
+            marks,
+            update,
             couple_mine,
             couple_theirs,
             table,
             value_w,
             gate_w,
-            observed_position.reshape(1, residues),
         ),
         [
             VMEM((n * span, half), F32),
@@ -743,7 +764,7 @@
             VMEM((2 * channels * block, half), F32),
         ],
         need=20,
-        in_specs=[sspec()] * 5 + [vspec()] * 10,
+        in_specs=[sspec()] + [vspec()] * 10,
         flops=2**31,
     )
 

time: 126 us -> 125 us (level)
  transfers between devices with their start and end apart: 5 -> 5, of which waited for: 2 -> 2; matrix products, arithmetic and copies ran while one was open for 0% -> 0% of each run, Pallas kernels for 5% -> 7%
where the time goes in v5:
time: 125 us
  blocking collectives  70.4 us (56%)
  Pallas kernels  23.6 us (19%)
  waiting for transfers between devices  15.6 us (12%)
  starting transfers between devices  10.7 us (9%)
  local copies, waits for them, and re-layouts  3.42 us (3%)
    all_to_all x3, blocking collectives, exchange(): lax.all_to_all(values, EVERY, split_axis=0, concat_axis=0, tiled=True)  70.4 us
    ppermute x4, waiting for transfers between devices, permute(): return lax.ppermute(values, 'branch', pairs)  15.6 us
    pallas_call x8, Pallas kernels, call(): pl.pallas_call(body, out_shape=out, in_specs=in_specs or [vspec() for _ i...  12.8 us
    pallas_call x1, Pallas kernels, per_device(): pl.pallas_call(functools.partial(attend_kernel, heads, places, raw), out_...  7.25 us
    ppermute x4, starting transfers between devices, permute(): return lax.ppermute(values, 'branch', pairs)  6.13 us
    all_to_all x1, starting transfers between devices, exchange(): lax.all_to_all(values, EVERY, split_axis=0, concat_axis=0, tiled=True)  4.55 us
    pallas_call x1, Pallas kernels, per_device(): pl.pallas_call(project_kernel, grid=(seqs,), out_shape=(jax.ShapeDtypeStr...  3.56 us
    unnamed x20, local copies, waits for them, and re-layouts  3.42 us
  transfers between devices with their start and end apart: 5, of which 2 were waited for; matrix products, arithmetic and copies ran while one was open for 0% of the time, Pallas kernels for 7%

profile of v5, /device:TPU:0, one launch (start us, length us, event | category | flops | bytes accessed | tf_op | source)
XLA Modules:
  0.0 124.5 jit_solution(17753702578599548290)
XLA Ops:
  0.7 2.0 %shard_map.141 = (bf16[32,32,256]{2,1,0:T(8,128)(2,1)S(1)}, bf16[8,128,128]{2,1,0:T(8,128)(2,1)S(1)}, bf16[8,128,128]{2,1,0:T(8,128)(2,1)S(1)}) custom-call(s32[1]{0:T(128)} %bitcast.2.side_ref, bf16[8,256,128]{2,1,0:T(8,128)(2,1)} %couple_ref.1, bf16[8,128]{1,0:T(8,128)(2,1)} %bitcast.12), custom_call_target="tpu_custom_call" | custom-call | bytes 1048576 | tf_op jit(solution)/shard_map/pallas_call | solution.py:76
  2.7 21.4 %all_to_all.20.own_ref = bf16[32,32,256]{2,1,0:T(8,128)(2,1)S(1)} all-to-all(bf16[32,32,256]{2,1,0:T(8,128)(2,1)S(1)} %get-tuple-element.28), channel_id=1, replica_groups=mesh['branch'=8,'dap'=4] {'branch','dap'}, dimensions={0} | all-to-all | bytes 1048576 | tf_op jit(solution)/shard_map/all_to_all | solution.py:599
  24.1 1.3 %collective-permute-start = (bf16[32,32,256]{2,1,0:T(8,128)(2,1)S(1)}, bf16[32,32,256]{2,1,0:T(8,128)(2,1)S(1)}, u32[]{:S(2)}, u32[]{:S(2)}) collective-permute-start(bf16[32,32,256]{2,1,0:T(8,128)(2,1)S(1)} %all_to_all.20.own_ref), channel_id=1, source_target_pairs={{0,4},{4,0},{8,12},{12,8},{16,20},{20,16},{24,28},{28,24},{1,5},{5... | collective-permute-start | bytes 1572872 | tf_op jit(solution)/shard_map/ppermute | solution.py:602
  25.4 0.9 shard_map.140
  26.3 3.6 %project.1 = (bf16[4,256,256]{2,1,0:T(8,128)(2,1)S(1)}, bf16[4,256,256]{2,1,0:T(8,128)(2,1)S(1)}, bf16[4,256,256]{2,1,0:T(8,128)(2,1)S(1)}, f32[4,256,256]{2,1,0:T(8,128)S(1)}) custom-call(bf16[4,256,256]{2,1,0:T(8,128)(2,1)} %rest_0_.1, bf16[256,768]{1,0:T(8,128)(2,1)} %qkv_w_ref.1, bf16[256,256]{1,0:T(8,128)(2,1)} %gate_w_ref.1), custom_call_target="tpu_custom_call" | custom-call | flops 536870912 | bytes 4194304 | tf_op jit(solution)/shard_map/project/pallas_call | solution.py:655
  29.9 1.0 copy-done.6
  30.8 0.8 copy-done.7
  31.6 0.8 copy-done.8
  32.4 0.8 copy-done.9
  33.2 7.2 %attend.1 = (bf16[4,256,256]{2,1,0:T(8,128)(2,1)}, bf16[32,88,128]{2,1,0:T(8,128)(2,1)S(1)}) custom-call(s32[1]{0:T(128)} %bitcast.core_ref, s32[4,256]{1,0:T(4,128)S(1)} %get-tuple-element.27.keep_ref, bf16[32,32,256]{2,1,0:T(8,128)(2,1)S(1)} %all_to_all.20.own_ref, bf16[32,32,256]{2,1,0:T(8,128)(2,1)S(1)} %collective-permute-done.other_ref, ...), custom_call_target="tpu_custom_call" | custom-call | flops 2147483648 | bytes 4194304 | tf_op jit(solution)/shard_map/attend/pallas_call | solution.py:683
  40.5 20.9 %all_to_all.21.own_ref = bf16[32,88,128]{2,1,0:T(8,128)(2,1)S(1)} all-to-all(bf16[32,88,128]{2,1,0:T(8,128)(2,1)S(1)} %get-tuple-element.36), channel_id=1, replica_groups=mesh['branch'=8,'dap'=4] {'branch','dap'}, dimensions={0} | all-to-all | bytes 1441792 | tf_op jit(solution)/shard_map/all_to_all | solution.py:599
  61.5 1.5 %collective-permute-start.1 = (bf16[32,88,128]{2,1,0:T(8,128)(2,1)S(1)}, bf16[32,88,128]{2,1,0:T(8,128)(2,1)S(1)}, u32[]{:S(2)}, u32[]{:S(2)}) collective-permute-start(bf16[32,88,128]{2,1,0:T(8,128)(2,1)S(1)} %all_to_all.21.own_ref), channel_id=1, source_target_pairs={{0,4},{4,0},{8,12},{12,8},{16,20},{20,16},{24,28},{28,24},{1,5},{5... | collective-permute-start | bytes 2162696 | tf_op jit(solution)/shard_map/ppermute | solution.py:602
  63.0 1.5 %collective-permute-start.2 = (bf16[8,128,128]{2,1,0:T(8,128)(2,1)S(1)}, bf16[8,128,128]{2,1,0:T(8,128)(2,1)S(1)}, u32[]{:S(2)}, u32[]{:S(2)}) collective-permute-start(bf16[8,128,128]{2,1,0:T(8,128)(2,1)S(1)} %get-tuple-element.43), channel_id=1, source_target_pairs={{0,8},{4,12},{8,0},{12,4},{16,24},{20,28},{24,16},{28,20},{1,9},{5... | collective-permute-start | bytes 786440 | tf_op jit(solution)/shard_map/ppermute | solution.py:602
  64.5 0.5 shard_map.142
  65.0 2.1 %shard_map.143 = (bf16[512,128]{1,0:T(8,128)(2,1)S(1)}, f32[16,128]{1,0:T(8,128)S(1)}, f32[16,128]{1,0:T(8,128)S(1)}, f32[8,128,256]{2,1,0:T(8,128)S(1)}) custom-call(s32[1]{0:T(128)} %bitcast.core_ref, s32[1]{0:T(128)} %bitcast.2.side_ref, s32[1]{0:T(128)} %bitcast.4.first_mine_ref, s32[1]{0:T(128)} %bitcast.5.first_theirs_ref, ...), custom_call_target="tpu_custom_call" | custom-call | flops 1073741824 | bytes 1048576 | tf_op jit(solution)/shard_map/pallas_call | solution.py:76
  67.1 4.1 %collective-permute-done.2.couple_theirs_ref = bf16[8,128,128]{2,1,0:T(8,128)(2,1)S(1)} collective-permute-done((bf16[8,128,128]{2,1,0:T(8,128)(2,1)S(1)}, bf16[8,128,128]{2,1,0:T(8,128)(2,1)S(1)}, u32[]{:S(2)}, u32[]{:S(2)}) %collective-permute-start.2) | collective-permute-done | bytes 262176 | tf_op jit(solution)/shard_map/ppermute | solution.py:602
  71.2 3.5 %shard_map.144 = (bf16[8,128,128]{2,1,0:T(8,128)(2,1)S(1)}, bf16[8,128,128]{2,1,0:T(8,128)(2,1)S(1)}, bf16[4096,128]{1,0:T(8,128)(2,1)S(1)}) custom-call(s32[1]{0:T(128)} %bitcast.core_ref, bf16[32,88,128]{2,1,0:T(8,128)(2,1)S(1)} %collective-permute-done.1.other_ref, bf16[512,128]{1,0:T(8,128)(2,1)S(1)} %get-tuple-element.38.left_ref, ...), custom_call_target="tpu_custom_call" | custom-call | flops 2147483648 | bytes 1048576 | tf_op jit(solution)/shard_map/pallas_call | solution.py:76
  74.8 28.1 %all_to_all.22.in_ref = bf16[32,128,128]{2,1,0:T(8,128)(2,1)S(1)} all-to-all(bf16[32,128,128]{2,1,0:T(8,128)(2,1)S(1)} %bitcast.10), channel_id=1, replica_groups=mesh['branch'=8,'dap'=4] {'branch','dap'}, dimensions={0} | all-to-all | bytes 2097152 | tf_op jit(solution)/shard_map/all_to_all | solution.py:599
  102.9 1.1 shard_map.146
  104.0 4.6 %all-to-all-start.3 = ((bf16[32,32,256]{2,1,0:T(8,128)(2,1)}), bf16[32,32,256]{2,1,0:T(8,128)(2,1)S(1)}, u32[]{:S(2)}, u32[]{:S(2)}) async-start(bf16[32,32,256]{2,1,0:T(8,128)(2,1)} %shard_map.146), calls=%async_computation.3 | async-start | bytes 1048576 | tf_op jit(solution)/shard_map/all_to_all | solution.py:599
  108.6 1.8 %collective-permute-start.3 = (bf16[8,128,128]{2,1,0:T(8,128)(2,1)S(1)}, bf16[8,128,128]{2,1,0:T(8,128)(2,1)S(1)}, u32[]{:S(2)}, u32[]{:S(2)}) collective-permute-start(bf16[8,128,128]{2,1,0:T(8,128)(2,1)S(1)} %get-tuple-element.47), channel_id=1, source_target_pairs={{0,8},{4,12},{8,0},{12,4},{16,24},{20,28},{24,16},{28,20},{1,9},{5... | collective-permute-start | bytes 786440 | tf_op jit(solution)/shard_map/ppermute | solution.py:602
  110.4 11.5 %collective-permute-done.3.theirs_ref = bf16[8,128,128]{2,1,0:T(8,128)(2,1)S(1)} collective-permute-done((bf16[8,128,128]{2,1,0:T(8,128)(2,1)S(1)}, bf16[8,128,128]{2,1,0:T(8,128)(2,1)S(1)}, u32[]{:S(2)}, u32[]{:S(2)}) %collective-permute-start.3) | collective-permute-done | bytes 262176 | tf_op jit(solution)/shard_map/ppermute | solution.py:602
  121.9 1.2 shard_map.145
  123.1 1.4 %shard_map.147 = bf16[8,256,128]{2,1,0:T(8,128)(2,1)} custom-call(s32[1]{0:T(128)} %bitcast.2.side_ref, bf16[8,128,128]{2,1,0:T(8,128)(2,1)S(1)} %get-tuple-element.46.mine_ref, bf16[8,128,128]{2,1,0:T(8,128)(2,1)S(1)} %collective-permute-done.3.theirs_ref, f32[8,128,128]{2,1,0:T(8,128)S(1)} %get-tuple-element.48.mine_gate_ref, ...), custom_call_target="tpu_custom_call" | custom-call | flops 134217728 | bytes 1048576 | tf_op jit(solution)/shard_map/pallas_call | solution.py:76
  (19 shorter events, 0.1 us)
Async XLA Ops:
  2.7 22.7 %copy-start.3 = (bf16[256,64]{0,1:T(8,128)(2,1)S(1)}, bf16[256,64]{0,1:T(8,128)(2,1)}, u32[]{:S(2)}) copy-start(bf16[256,64]{0,1:T(8,128)(2,1)} %param.21) | copy-start | bytes 98308
  24.1 9.2 %collective-permute-start = (bf16[32,32,256]{2,1,0:T(8,128)(2,1)S(1)}, bf16[32,32,256]{2,1,0:T(8,128)(2,1)S(1)}, u32[]{:S(2)}, u32[]{:S(2)}) collective-permute-start(bf16[32,32,256]{2,1,0:T(8,128)(2,1)S(1)} %all_to_all.20.own_ref), channel_id=1, source_target_pairs={{0,4},{4,0},{8,12},{12,8},{16,20},{20,16},{24,28},{28,24},{1,5},{5... | collective-permute-start | bytes 1572872 | tf_op jit(solution)/shard_map/ppermute | solution.py:602
  26.3 7.0 %copy-start.5 = (bf16[256,256]{1,0:T(8,128)(2,1)S(1)}, bf16[256,256]{1,0:T(8,128)(2,1)}, u32[]{:S(2)}) copy-start(bf16[256,256]{1,0:T(8,128)(2,1)} %merge_ref.2) | copy-start | bytes 393220
  29.8 1.0 copy-start.6
  30.8 0.8 copy-start.7
  31.6 0.8 copy-start.8
  32.4 0.8 copy-start.9
  40.5 24.0 %copy-start = (bf16[1024,128]{1,0:T(8,128)(2,1)S(1)}, bf16[1024,128]{1,0:T(8,128)(2,1)}, u32[]{:S(2)}) copy-start(bf16[1024,128]{1,0:T(8,128)(2,1)} %merge_ref.3) | copy-start | bytes 786436
  40.5 24.0 %copy-start.1 = (bf16[128,512]{1,0:T(8,128)(2,1)S(1)}, bf16[128,512]{1,0:T(8,128)(2,1)}, u32[]{:S(2)}) copy-start(bf16[128,512]{1,0:T(8,128)(2,1)} %entry_ref.1) | copy-start | bytes 393220
  40.5 24.0 %copy-start.4 = (bf16[128,128]{1,0:T(8,128)(2,1)S(1)}, bf16[128,128]{1,0:T(8,128)(2,1)}, u32[]{:S(2)}) copy-start(bf16[128,128]{1,0:T(8,128)(2,1)} %close_ref.1) | copy-start | bytes 98308
  61.5 9.8 %collective-permute-start.1 = (bf16[32,88,128]{2,1,0:T(8,128)(2,1)S(1)}, bf16[32,88,128]{2,1,0:T(8,128)(2,1)S(1)}, u32[]{:S(2)}, u32[]{:S(2)}) collective-permute-start(bf16[32,88,128]{2,1,0:T(8,128)(2,1)S(1)} %all_to_all.21.own_ref), channel_id=1, source_target_pairs={{0,4},{4,0},{8,12},{12,8},{16,20},{20,16},{24,28},{28,24},{1,5},{5... | collective-permute-start | bytes 2162696 | tf_op jit(solution)/shard_map/ppermute | solution.py:602
  63.0 8.2 %collective-permute-start.2 = (bf16[8,128,128]{2,1,0:T(8,128)(2,1)S(1)}, bf16[8,128,128]{2,1,0:T(8,128)(2,1)S(1)}, u32[]{:S(2)}, u32[]{:S(2)}) collective-permute-start(bf16[8,128,128]{2,1,0:T(8,128)(2,1)S(1)} %get-tuple-element.43), channel_id=1, source_target_pairs={{0,8},{4,12},{8,0},{12,4},{16,24},{20,28},{24,16},{28,20},{1,9},{5... | collective-permute-start | bytes 786440 | tf_op jit(solution)/shard_map/ppermute | solution.py:602
  104.0 17.9 %copy-start.2 = (bf16[128,128]{1,0:T(8,128)(2,1)S(1)}, bf16[128,128]{1,0:T(8,128)(2,1)}, u32[]{:S(2)}) copy-start(bf16[128,128]{1,0:T(8,128)(2,1)} %weight_ref.1) | copy-start | bytes 98308
  104.0 19.1 %all-to-all-start.3 = ((bf16[32,32,256]{2,1,0:T(8,128)(2,1)}), bf16[32,32,256]{2,1,0:T(8,128)(2,1)S(1)}, u32[]{:S(2)}, u32[]{:S(2)}) async-start(bf16[32,32,256]{2,1,0:T(8,128)(2,1)} %shard_map.146), calls=%async_computation.3 | async-start | bytes 1048576 | tf_op jit(solution)/shard_map/all_to_all | solution.py:599
  108.6 13.4 %collective-permute-start.3 = (bf16[8,128,128]{2,1,0:T(8,128)(2,1)S(1)}, bf16[8,128,128]{2,1,0:T(8,128)(2,1)S(1)}, u32[]{:S(2)}, u32[]{:S(2)}) collective-permute-start(bf16[8,128,128]{2,1,0:T(8,128)(2,1)S(1)} %get-tuple-element.47), channel_id=1, source_target_pairs={{0,8},{4,12},{8,0},{12,4},{16,24},{20,28},{24,16},{28,20},{1,9},{5... | collective-permute-start | bytes 786440 | tf_op jit(solution)/shard_map/ppermute | solution.py:602

commit v6 on v5

--- a/solution.py
+++ b/solution.py
@@ -95,8 +95,16 @@
     half = residues // 2
     mine = pl.multiple_of(side_ref[0] * half, half)
     theirs = pl.multiple_of((1 - side_ref[0]) * half, half)
+    channels = couple_ref.shape[2]
+    exact = channels & (channels - 1) == 0
+    share = jnp.full((channels, channels), 1.0 / channels, BF16)
     for i in range(rows):
-        normed = normalize(couple_ref[i]).astype(BF16)
+        if exact:
+            centred = couple_ref[i].astype(F32) - mm(couple_ref[i], share)
+            spread = jnp.mean(centred * centred, axis=-1, keepdims=True)
+            normed = (centred * lax.rsqrt(spread + EPSILON)).astype(BF16)
+        else:
+            normed = normalize(couple_ref[i]).astype(BF16)
         put(scr, i, mm(weight_ref[...], normed, NT), rows)
         mine_ref[i] = couple_ref[i, pl.ds(mine, half), :]
         theirs_ref[i] = couple_ref[i, pl.ds(theirs, half), :]
@@ -106,8 +114,15 @@
         out_ref[t] = halves[core]
 
 
-def prepare_small_kernel(seqs, halves_ref, present_ref, left_ref, right_ref, keep_ref):
+def prepare_small_kernel(
+    seqs, heads, halves_ref, present_ref, left_ref, right_ref, keep_ref, ones_ref
+):
     keep_ref[...] = present_ref[...]
+    residues, half = ones_ref.shape[0] // (heads // 2), ones_ref.shape[1]
+    lane = lax.broadcasted_iota(jnp.int32, (residues, half), 1) // (half // (heads // 2))
+    for h in range(heads // 2):
+        mine = jnp.where(lane == h, jnp.ones((), BF16), jnp.zeros((), BF16))
+        ones_ref[h * residues : (h + 1) * residues, :] = mine
     width = halves_ref.shape[0] // 2
     left = halves_ref[:width].astype(F32).T.astype(BF16)
     for s in range(seqs):
@@ -180,11 +195,12 @@
     merge_ref,
     left_w_ref,
     right_w_ref,
+    ones_scr,
     *rest,
 ):
     sources, (new_out, message_out) = rest[:5], rest[5:7]
     seq_ref, query_ref, key_ref, value_ref, gate_ref = held_refs = rest[7:12]
-    new_ref, message_ref, left_scr, bias_scr, ones_scr, in_sems, new_sems, message_sems = rest[12:]
+    new_ref, message_ref, left_scr, bias_scr, in_sems, new_sems, message_sems = rest[12:]
     batch = seqs = keep_ref.shape[0]
     arrivals = [
         [
@@ -311,10 +327,6 @@
     plain = jnp.min(some) == 0.0
 
     left_scr[...] = jnp.zeros_like(left_scr)
-    for h in range(some_heads):
-        ones_scr[h * residues : (h + 1) * residues, :] = jnp.where(
-            lane_half == h, jnp.ones((), BF16), zero
-        )
     unit = jnp.where(plain, 1.0, LOG2E)
     for k, ref in enumerate((own_ref, other_ref)):
         for h in range(some_heads):
@@ -601,12 +613,13 @@
     def permute(values, pairs):
         return lax.ppermute(values, "branch", pairs)
 
-    left_w, right_w, keep = call(
-        functools.partial(prepare_small_kernel, seqs),
+    left_w, right_w, keep, ones = call(
+        functools.partial(prepare_small_kernel, seqs, heads),
         (
             jax.ShapeDtypeStruct((seqs, features, seqs * width), BF16),
             jax.ShapeDtypeStruct((width, features), BF16),
             jax.ShapeDtypeStruct(homolog_present.shape, homolog_present.dtype),
+            jax.ShapeDtypeStruct((heads // 2 * residues, inner // 2), BF16),
         ),
         (tensor_halves_kernel.T, stay(homolog_present)),
     )
@@ -686,7 +699,7 @@
             jax.ShapeDtypeStruct(new_shape, BF16),
             jax.ShapeDtypeStruct((n, depth, half), BF16),
         ),
-        in_specs=[sspec()] + [vspec()] * 6 + [anywhere] * 5,
+        in_specs=[sspec()] + [vspec()] * 7 + [anywhere] * 5,
         out_specs=(anywhere, anywhere),
         scratch_shapes=[
             VMEM(new_shape, BF16),
@@ -698,7 +711,6 @@
             VMEM((n, depth, half), BF16),
             VMEM((residues, seqs * width), F32),
             VMEM((heads, residues, residues), F32),
-            VMEM((half_heads * residues, half), BF16),
             pltpu.SemaphoreType.DMA((5, seqs)),
             pltpu.SemaphoreType.DMA((seqs,)),
             pltpu.SemaphoreType.DMA((seqs + 1,)),
@@ -714,6 +726,7 @@
         heads_merge_kernel,
         left_w,
         right_w,
+        ones,
         stay(homolog_embedding),
         *(stay(values) for values in parts),
         stay(gates),

time: 125 us -> 125 us (level)
  no operation moved by 1% of the time
where the time goes in v6:
time: 125 us; the launch traced here: 124 us
  blocking collectives  70.5 us (56%)
  Pallas kernels  23.3 us (19%)
  waiting for transfers between devices  15.6 us (12%)
  starting transfers between devices  10.7 us (9%)
  local copies, waits for them, and re-layouts  3.42 us (3%)
    all_to_all x3, blocking collectives, exchange(): lax.all_to_all(values, EVERY, split_axis=0, concat_axis=0, tiled=True)  70.5 us
    ppermute x4, waiting for transfers between devices, permute(): return lax.ppermute(values, 'branch', pairs)  15.6 us
    pallas_call x8, Pallas kernels, call(): pl.pallas_call(body, out_shape=out, in_specs=in_specs or [vspec() for _ i...  12.4 us
    pallas_call x1, Pallas kernels, per_device(): pl.pallas_call(functools.partial(attend_kernel, heads, places, raw), out_...  7.3 us
    ppermute x4, starting transfers between devices, permute(): return lax.ppermute(values, 'branch', pairs)  6.13 us
    all_to_all x1, starting transfers between devices, exchange(): lax.all_to_all(values, EVERY, split_axis=0, concat_axis=0, tiled=True)  4.55 us
    pallas_call x1, Pallas kernels, per_device(): pl.pallas_call(project_kernel, grid=(seqs,), out_shape=(jax.ShapeDtypeStr...  3.56 us
    unnamed x20, local copies, waits for them, and re-layouts  3.42 us
  transfers between devices with their start and end apart: 5, of which 2 were waited for; matrix products, arithmetic and copies ran while one was open for 0% of the time, Pallas kernels for 7%

profile of v6, /device:TPU:0, one launch (start us, length us, event | category | flops | bytes accessed | tf_op | source)
XLA Modules:
  0.0 124.3 jit_solution(13056281943673316652)
XLA Ops:
  0.7 1.7 %shard_map.141 = (bf16[32,32,256]{2,1,0:T(8,128)(2,1)S(1)}, bf16[8,128,128]{2,1,0:T(8,128)(2,1)S(1)}, bf16[8,128,128]{2,1,0:T(8,128)(2,1)S(1)}) custom-call(s32[1]{0:T(128)} %bitcast.2.side_ref, bf16[8,256,128]{2,1,0:T(8,128)(2,1)} %couple_ref.1, bf16[8,128]{1,0:T(8,128)(2,1)} %bitcast.12), custom_call_target="tpu_custom_call" | custom-call | bytes 1048576 | tf_op jit(solution)/shard_map/pallas_call | solution.py:76
  2.4 21.4 %all_to_all.20.own_ref = bf16[32,32,256]{2,1,0:T(8,128)(2,1)S(1)} all-to-all(bf16[32,32,256]{2,1,0:T(8,128)(2,1)S(1)} %get-tuple-element.29), channel_id=1, replica_groups=mesh['branch'=8,'dap'=4] {'branch','dap'}, dimensions={0} | all-to-all | bytes 1048576 | tf_op jit(solution)/shard_map/all_to_all | solution.py:611
  23.8 1.3 %collective-permute-start = (bf16[32,32,256]{2,1,0:T(8,128)(2,1)S(1)}, bf16[32,32,256]{2,1,0:T(8,128)(2,1)S(1)}, u32[]{:S(2)}, u32[]{:S(2)}) collective-permute-start(bf16[32,32,256]{2,1,0:T(8,128)(2,1)S(1)} %all_to_all.20.own_ref), channel_id=1, source_target_pairs={{0,4},{4,0},{8,12},{12,8},{16,20},{20,16},{24,28},{28,24},{1,5},{5... | collective-permute-start | bytes 1572872 | tf_op jit(solution)/shard_map/ppermute | solution.py:614
  25.1 0.9 shard_map.140
  26.0 3.6 %project.1 = (bf16[4,256,256]{2,1,0:T(8,128)(2,1)S(1)}, bf16[4,256,256]{2,1,0:T(8,128)(2,1)S(1)}, bf16[4,256,256]{2,1,0:T(8,128)(2,1)S(1)}, f32[4,256,256]{2,1,0:T(8,128)S(1)}) custom-call(bf16[4,256,256]{2,1,0:T(8,128)(2,1)} %rest_0_.1, bf16[256,768]{1,0:T(8,128)(2,1)} %qkv_w_ref.1, bf16[256,256]{1,0:T(8,128)(2,1)} %gate_w_ref.1), custom_call_target="tpu_custom_call" | custom-call | flops 536870912 | bytes 4194304 | tf_op jit(solution)/shard_map/project/pallas_call | solution.py:668
  29.6 1.0 copy-done.6
  30.6 0.8 copy-done.7
  31.3 0.8 copy-done.8
  32.1 0.8 copy-done.9
  33.0 7.3 %attend.1 = (bf16[4,256,256]{2,1,0:T(8,128)(2,1)}, bf16[32,88,128]{2,1,0:T(8,128)(2,1)S(1)}) custom-call(s32[1]{0:T(128)} %bitcast.core_ref, s32[4,256]{1,0:T(4,128)S(1)} %get-tuple-element.28.keep_ref, bf16[32,32,256]{2,1,0:T(8,128)(2,1)S(1)} %all_to_all.20.own_ref, bf16[32,32,256]{2,1,0:T(8,128)(2,1)S(1)} %collective-permute-done.other_ref, ...), custom_call_target="tpu_custom_call" | custom-call | flops 2147483648 | bytes 4194304 | tf_op jit(solution)/shard_map/attend/pallas_call | solution.py:696
  40.3 20.9 %all_to_all.21.own_ref = bf16[32,88,128]{2,1,0:T(8,128)(2,1)S(1)} all-to-all(bf16[32,88,128]{2,1,0:T(8,128)(2,1)S(1)} %get-tuple-element.38), channel_id=1, replica_groups=mesh['branch'=8,'dap'=4] {'branch','dap'}, dimensions={0} | all-to-all | bytes 1441792 | tf_op jit(solution)/shard_map/all_to_all | solution.py:611
  61.2 1.5 %collective-permute-start.1 = (bf16[32,88,128]{2,1,0:T(8,128)(2,1)S(1)}, bf16[32,88,128]{2,1,0:T(8,128)(2,1)S(1)}, u32[]{:S(2)}, u32[]{:S(2)}) collective-permute-start(bf16[32,88,128]{2,1,0:T(8,128)(2,1)S(1)} %all_to_all.21.own_ref), channel_id=1, source_target_pairs={{0,4},{4,0},{8,12},{12,8},{16,20},{20,16},{24,28},{28,24},{1,5},{5... | collective-permute-start | bytes 2162696 | tf_op jit(solution)/shard_map/ppermute | solution.py:614
  62.8 1.5 %collective-permute-start.2 = (bf16[8,128,128]{2,1,0:T(8,128)(2,1)S(1)}, bf16[8,128,128]{2,1,0:T(8,128)(2,1)S(1)}, u32[]{:S(2)}, u32[]{:S(2)}) collective-permute-start(bf16[8,128,128]{2,1,0:T(8,128)(2,1)S(1)} %get-tuple-element.45), channel_id=1, source_target_pairs={{0,8},{4,12},{8,0},{12,4},{16,24},{20,28},{24,16},{28,20},{1,9},{5... | collective-permute-start | bytes 786440 | tf_op jit(solution)/shard_map/ppermute | solution.py:614
  64.3 0.5 shard_map.142
  64.8 2.1 %shard_map.143 = (bf16[512,128]{1,0:T(8,128)(2,1)S(1)}, f32[16,128]{1,0:T(8,128)S(1)}, f32[16,128]{1,0:T(8,128)S(1)}, f32[8,128,256]{2,1,0:T(8,128)S(1)}) custom-call(s32[1]{0:T(128)} %bitcast.core_ref, s32[1]{0:T(128)} %bitcast.2.side_ref, s32[1]{0:T(128)} %bitcast.4.first_mine_ref, s32[1]{0:T(128)} %bitcast.5.first_theirs_ref, ...), custom_call_target="tpu_custom_call" | custom-call | flops 1073741824 | bytes 1048576 | tf_op jit(solution)/shard_map/pallas_call | solution.py:76
  66.9 4.1 %collective-permute-done.2.couple_theirs_ref = bf16[8,128,128]{2,1,0:T(8,128)(2,1)S(1)} collective-permute-done((bf16[8,128,128]{2,1,0:T(8,128)(2,1)S(1)}, bf16[8,128,128]{2,1,0:T(8,128)(2,1)S(1)}, u32[]{:S(2)}, u32[]{:S(2)}) %collective-permute-start.2) | collective-permute-done | bytes 262176 | tf_op jit(solution)/shard_map/ppermute | solution.py:614
  71.0 3.5 %shard_map.144 = (bf16[8,128,128]{2,1,0:T(8,128)(2,1)S(1)}, bf16[8,128,128]{2,1,0:T(8,128)(2,1)S(1)}, bf16[4096,128]{1,0:T(8,128)(2,1)S(1)}) custom-call(s32[1]{0:T(128)} %bitcast.core_ref, bf16[32,88,128]{2,1,0:T(8,128)(2,1)S(1)} %collective-permute-done.1.other_ref, bf16[512,128]{1,0:T(8,128)(2,1)S(1)} %get-tuple-element.40.left_ref, ...), custom_call_target="tpu_custom_call" | custom-call | flops 2147483648 | bytes 1048576 | tf_op jit(solution)/shard_map/pallas_call | solution.py:76
  74.5 28.1 %all_to_all.22.in_ref = bf16[32,128,128]{2,1,0:T(8,128)(2,1)S(1)} all-to-all(bf16[32,128,128]{2,1,0:T(8,128)(2,1)S(1)} %bitcast.10), channel_id=1, replica_groups=mesh['branch'=8,'dap'=4] {'branch','dap'}, dimensions={0} | all-to-all | bytes 2097152 | tf_op jit(solution)/shard_map/all_to_all | solution.py:611
  102.6 1.1 shard_map.146
  103.8 4.5 %all-to-all-start.3 = ((bf16[32,32,256]{2,1,0:T(8,128)(2,1)}), bf16[32,32,256]{2,1,0:T(8,128)(2,1)S(1)}, u32[]{:S(2)}, u32[]{:S(2)}) async-start(bf16[32,32,256]{2,1,0:T(8,128)(2,1)} %shard_map.146), calls=%async_computation.3 | async-start | bytes 1048576 | tf_op jit(solution)/shard_map/all_to_all | solution.py:611
  108.3 1.8 %collective-permute-start.3 = (bf16[8,128,128]{2,1,0:T(8,128)(2,1)S(1)}, bf16[8,128,128]{2,1,0:T(8,128)(2,1)S(1)}, u32[]{:S(2)}, u32[]{:S(2)}) collective-permute-start(bf16[8,128,128]{2,1,0:T(8,128)(2,1)S(1)} %get-tuple-element.49), channel_id=1, source_target_pairs={{0,8},{4,12},{8,0},{12,4},{16,24},{20,28},{24,16},{28,20},{1,9},{5... | collective-permute-start | bytes 786440 | tf_op jit(solution)/shard_map/ppermute | solution.py:614
  110.2 11.5 %collective-permute-done.3.theirs_ref = bf16[8,128,128]{2,1,0:T(8,128)(2,1)S(1)} collective-permute-done((bf16[8,128,128]{2,1,0:T(8,128)(2,1)S(1)}, bf16[8,128,128]{2,1,0:T(8,128)(2,1)S(1)}, u32[]{:S(2)}, u32[]{:S(2)}) %collective-permute-start.3) | collective-permute-done | bytes 262176 | tf_op jit(solution)/shard_map/ppermute | solution.py:614
  121.7 1.2 shard_map.145
  122.9 1.4 %shard_map.147 = bf16[8,256,128]{2,1,0:T(8,128)(2,1)} custom-call(s32[1]{0:T(128)} %bitcast.2.side_ref, bf16[8,128,128]{2,1,0:T(8,128)(2,1)S(1)} %get-tuple-element.48.mine_ref, bf16[8,128,128]{2,1,0:T(8,128)(2,1)S(1)} %collective-permute-done.3.theirs_ref, f32[8,128,128]{2,1,0:T(8,128)S(1)} %get-tuple-element.50.mine_gate_ref, ...), custom_call_target="tpu_custom_call" | custom-call | flops 134217728 | bytes 1048576 | tf_op jit(solution)/shard_map/pallas_call | solution.py:76
  (19 shorter events, 0.1 us)
Async XLA Ops:
  2.4 22.7 %copy-start.3 = (bf16[256,64]{0,1:T(8,128)(2,1)S(1)}, bf16[256,64]{0,1:T(8,128)(2,1)}, u32[]{:S(2)}) copy-start(bf16[256,64]{0,1:T(8,128)(2,1)} %param.21) | copy-start | bytes 98308
  23.8 9.2 %collective-permute-start = (bf16[32,32,256]{2,1,0:T(8,128)(2,1)S(1)}, bf16[32,32,256]{2,1,0:T(8,128)(2,1)S(1)}, u32[]{:S(2)}, u32[]{:S(2)}) collective-permute-start(bf16[32,32,256]{2,1,0:T(8,128)(2,1)S(1)} %all_to_all.20.own_ref), channel_id=1, source_target_pairs={{0,4},{4,0},{8,12},{12,8},{16,20},{20,16},{24,28},{28,24},{1,5},{5... | collective-permute-start | bytes 1572872 | tf_op jit(solution)/shard_map/ppermute | solution.py:614
  26.0 7.0 %copy-start.5 = (bf16[256,256]{1,0:T(8,128)(2,1)S(1)}, bf16[256,256]{1,0:T(8,128)(2,1)}, u32[]{:S(2)}) copy-start(bf16[256,256]{1,0:T(8,128)(2,1)} %merge_ref.2) | copy-start | bytes 393220
  29.6 1.0 copy-start.6
  30.6 0.8 copy-start.7
  31.3 0.8 copy-start.8
  32.1 0.8 copy-start.9
  40.3 24.0 %copy-start = (bf16[1024,128]{1,0:T(8,128)(2,1)S(1)}, bf16[1024,128]{1,0:T(8,128)(2,1)}, u32[]{:S(2)}) copy-start(bf16[1024,128]{1,0:T(8,128)(2,1)} %merge_ref.3) | copy-start | bytes 786436
  40.3 24.0 %copy-start.1 = (bf16[128,512]{1,0:T(8,128)(2,1)S(1)}, bf16[128,512]{1,0:T(8,128)(2,1)}, u32[]{:S(2)}) copy-start(bf16[128,512]{1,0:T(8,128)(2,1)} %entry_ref.1) | copy-start | bytes 393220
  40.3 24.0 %copy-start.4 = (bf16[128,128]{1,0:T(8,128)(2,1)S(1)}, bf16[128,128]{1,0:T(8,128)(2,1)}, u32[]{:S(2)}) copy-start(bf16[128,128]{1,0:T(8,128)(2,1)} %close_ref.1) | copy-start | bytes 98308
  61.2 9.8 %collective-permute-start.1 = (bf16[32,88,128]{2,1,0:T(8,128)(2,1)S(1)}, bf16[32,88,128]{2,1,0:T(8,128)(2,1)S(1)}, u32[]{:S(2)}, u32[]{:S(2)}) collective-permute-start(bf16[32,88,128]{2,1,0:T(8,128)(2,1)S(1)} %all_to_all.21.own_ref), channel_id=1, source_target_pairs={{0,4},{4,0},{8,12},{12,8},{16,20},{20,16},{24,28},{28,24},{1,5},{5... | collective-permute-start | bytes 2162696 | tf_op jit(solution)/shard_map/ppermute | solution.py:614
  62.8 8.2 %collective-permute-start.2 = (bf16[8,128,128]{2,1,0:T(8,128)(2,1)S(1)}, bf16[8,128,128]{2,1,0:T(8,128)(2,1)S(1)}, u32[]{:S(2)}, u32[]{:S(2)}) collective-permute-start(bf16[8,128,128]{2,1,0:T(8,128)(2,1)S(1)} %get-tuple-element.45), channel_id=1, source_target_pairs={{0,8},{4,12},{8,0},{12,4},{16,24},{20,28},{24,16},{28,20},{1,9},{5... | collective-permute-start | bytes 786440 | tf_op jit(solution)/shard_map/ppermute | solution.py:614
  103.8 17.9 %copy-start.2 = (bf16[128,128]{1,0:T(8,128)(2,1)S(1)}, bf16[128,128]{1,0:T(8,128)(2,1)}, u32[]{:S(2)}) copy-start(bf16[128,128]{1,0:T(8,128)(2,1)} %weight_ref.1) | copy-start | bytes 98308
  103.8 19.1 %all-to-all-start.3 = ((bf16[32,32,256]{2,1,0:T(8,128)(2,1)}), bf16[32,32,256]{2,1,0:T(8,128)(2,1)S(1)}, u32[]{:S(2)}, u32[]{:S(2)}) async-start(bf16[32,32,256]{2,1,0:T(8,128)(2,1)} %shard_map.146), calls=%async_computation.3 | async-start | bytes 1048576 | tf_op jit(solution)/shard_map/all_to_all | solution.py:611
  108.3 13.4 %collective-permute-start.3 = (bf16[8,128,128]{2,1,0:T(8,128)(2,1)S(1)}, bf16[8,128,128]{2,1,0:T(8,128)(2,1)S(1)}, u32[]{:S(2)}, u32[]{:S(2)}) collective-permute-start(bf16[8,128,128]{2,1,0:T(8,128)(2,1)S(1)} %get-tuple-element.49), channel_id=1, source_target_pairs={{0,8},{4,12},{8,0},{12,4},{16,24},{20,28},{24,16},{28,20},{1,9},{5... | collective-permute-start | bytes 786440 | tf_op jit(solution)/shard_map/ppermute | solution.py:614

commit v7 on v6

--- a/solution.py
+++ b/solution.py
@@ -29,6 +29,16 @@
     values = values.astype(F32)
     centred = values - jnp.mean(values, axis=axis, keepdims=True)
     spread = jnp.mean(centred * centred, axis=axis, keepdims=True)
+    return centred * lax.rsqrt(spread + EPSILON)
+
+
+def normalize_rows(values):
+    channels = values.shape[-1]
+    if channels & (channels - 1):
+        return normalize(values)
+    share = jnp.full((channels, channels), 1.0 / channels, BF16)
+    centred = values.astype(F32) - mm(values, share)
+    spread = jnp.mean(centred * centred, axis=-1, keepdims=True)
     return centred * lax.rsqrt(spread + EPSILON)
 
 
@@ -261,7 +271,7 @@
                 pltpu.make_async_copy(new_ref.at[u], new_out.at[u], new_sems.at[u]).start()
 
             def norm():
-                held["normed"] = normalize(held["updated"]).astype(BF16)
+                held["normed"] = normalize_rows(held["updated"]).astype(BF16)
 
             def right():
                 values = (mm(right_w_ref[...], held["normed"], NT) * present).astype(BF16)
@@ -490,7 +500,7 @@
             r = (i + d) % rows
             pair = (couple_ref[r].astype(F32) + piece.T).astype(BF16)
             pair_ref[r] = pair
-            normed.append(normalize(pair).astype(BF16))
+            normed.append(normalize_rows(pair).astype(BF16))
         norms[i] = jnp.concatenate(normed, axis=0)
 
     def edge(i):

time: 125 us -> 125 us (level)
  no operation moved by 1% of the time
where the time goes in v7:
time: 125 us; the launch traced here: 124 us
  blocking collectives  70.5 us (56%)
  Pallas kernels  23.4 us (19%)
  waiting for transfers between devices  15.6 us (12%)
  starting transfers between devices  10.7 us (9%)
  local copies, waits for them, and re-layouts  3.42 us (3%)
    all_to_all x3, blocking collectives, exchange(): lax.all_to_all(values, EVERY, split_axis=0, concat_axis=0, tiled=True)  70.5 us
    ppermute x4, waiting for transfers between devices, permute(): return lax.ppermute(values, 'branch', pairs)  15.6 us
    pallas_call x8, Pallas kernels, call(): pl.pallas_call(body, out_shape=out, in_specs=in_specs or [vspec() for _ i...  12.6 us
    pallas_call x1, Pallas kernels, per_device(): pl.pallas_call(functools.partial(attend_kernel, heads, places, raw), out_...  7.29 us
    ppermute x4, starting transfers between devices, permute(): return lax.ppermute(values, 'branch', pairs)  6.13 us
    all_to_all x1, starting transfers between devices, exchange(): lax.all_to_all(values, EVERY, split_axis=0, concat_axis=0, tiled=True)  4.55 us
    pallas_call x1, Pallas kernels, per_device(): pl.pallas_call(project_kernel, grid=(seqs,), out_shape=(jax.ShapeDtypeStr...  3.56 us
    unnamed x20, local copies, waits for them, and re-layouts  3.42 us
  transfers between devices with their start and end apart: 5, of which 2 were waited for; matrix products, arithmetic and copies ran while one was open for 0% of the time, Pallas kernels for 7%

profile of v7, /device:TPU:0, one launch (start us, length us, event | category | flops | bytes accessed | tf_op | source)
XLA Modules:
  0.0 124.4 jit_solution(14910493273237854608)
XLA Ops:
  0.7 1.7 %shard_map.141 = (bf16[32,32,256]{2,1,0:T(8,128)(2,1)S(1)}, bf16[8,128,128]{2,1,0:T(8,128)(2,1)S(1)}, bf16[8,128,128]{2,1,0:T(8,128)(2,1)S(1)}) custom-call(s32[1]{0:T(128)} %bitcast.2.side_ref, bf16[8,256,128]{2,1,0:T(8,128)(2,1)} %couple_ref.1, bf16[8,128]{1,0:T(8,128)(2,1)} %bitcast.12), custom_call_target="tpu_custom_call" | custom-call | bytes 1048576 | tf_op jit(solution)/shard_map/pallas_call | solution.py:86
  2.4 21.4 %all_to_all.20.own_ref = bf16[32,32,256]{2,1,0:T(8,128)(2,1)S(1)} all-to-all(bf16[32,32,256]{2,1,0:T(8,128)(2,1)S(1)} %get-tuple-element.29), channel_id=1, replica_groups=mesh['branch'=8,'dap'=4] {'branch','dap'}, dimensions={0} | all-to-all | bytes 1048576 | tf_op jit(solution)/shard_map/all_to_all | solution.py:621
  23.8 1.3 %collective-permute-start = (bf16[32,32,256]{2,1,0:T(8,128)(2,1)S(1)}, bf16[32,32,256]{2,1,0:T(8,128)(2,1)S(1)}, u32[]{:S(2)}, u32[]{:S(2)}) collective-permute-start(bf16[32,32,256]{2,1,0:T(8,128)(2,1)S(1)} %all_to_all.20.own_ref), channel_id=1, source_target_pairs={{0,4},{4,0},{8,12},{12,8},{16,20},{20,16},{24,28},{28,24},{1,5},{5... | collective-permute-start | bytes 1572872 | tf_op jit(solution)/shard_map/ppermute | solution.py:624
  25.1 0.9 shard_map.140
  26.0 3.6 %project.1 = (bf16[4,256,256]{2,1,0:T(8,128)(2,1)S(1)}, bf16[4,256,256]{2,1,0:T(8,128)(2,1)S(1)}, bf16[4,256,256]{2,1,0:T(8,128)(2,1)S(1)}, f32[4,256,256]{2,1,0:T(8,128)S(1)}) custom-call(bf16[4,256,256]{2,1,0:T(8,128)(2,1)} %rest_0_.1, bf16[256,768]{1,0:T(8,128)(2,1)} %qkv_w_ref.1, bf16[256,256]{1,0:T(8,128)(2,1)} %gate_w_ref.1), custom_call_target="tpu_custom_call" | custom-call | flops 536870912 | bytes 4194304 | tf_op jit(solution)/shard_map/project/pallas_call | solution.py:678
  29.6 1.0 copy-done.6
  30.6 0.8 copy-done.7
  31.3 0.8 copy-done.8
  32.1 0.8 copy-done.9
  33.0 7.3 %attend.1 = (bf16[4,256,256]{2,1,0:T(8,128)(2,1)}, bf16[32,88,128]{2,1,0:T(8,128)(2,1)S(1)}) custom-call(s32[1]{0:T(128)} %bitcast.core_ref, s32[4,256]{1,0:T(4,128)S(1)} %get-tuple-element.28.keep_ref, bf16[32,32,256]{2,1,0:T(8,128)(2,1)S(1)} %all_to_all.20.own_ref, bf16[32,32,256]{2,1,0:T(8,128)(2,1)S(1)} %collective-permute-done.other_ref, ...), custom_call_target="tpu_custom_call" | custom-call | flops 2147483648 | bytes 4194304 | tf_op jit(solution)/shard_map/attend/pallas_call | solution.py:706
  40.3 20.9 %all_to_all.21.own_ref = bf16[32,88,128]{2,1,0:T(8,128)(2,1)S(1)} all-to-all(bf16[32,88,128]{2,1,0:T(8,128)(2,1)S(1)} %get-tuple-element.38), channel_id=1, replica_groups=mesh['branch'=8,'dap'=4] {'branch','dap'}, dimensions={0} | all-to-all | bytes 1441792 | tf_op jit(solution)/shard_map/all_to_all | solution.py:621
  61.2 1.5 %collective-permute-start.1 = (bf16[32,88,128]{2,1,0:T(8,128)(2,1)S(1)}, bf16[32,88,128]{2,1,0:T(8,128)(2,1)S(1)}, u32[]{:S(2)}, u32[]{:S(2)}) collective-permute-start(bf16[32,88,128]{2,1,0:T(8,128)(2,1)S(1)} %all_to_all.21.own_ref), channel_id=1, source_target_pairs={{0,4},{4,0},{8,12},{12,8},{16,20},{20,16},{24,28},{28,24},{1,5},{5... | collective-permute-start | bytes 2162696 | tf_op jit(solution)/shard_map/ppermute | solution.py:624
  62.8 1.5 %collective-permute-start.2 = (bf16[8,128,128]{2,1,0:T(8,128)(2,1)S(1)}, bf16[8,128,128]{2,1,0:T(8,128)(2,1)S(1)}, u32[]{:S(2)}, u32[]{:S(2)}) collective-permute-start(bf16[8,128,128]{2,1,0:T(8,128)(2,1)S(1)} %get-tuple-element.45), channel_id=1, source_target_pairs={{0,8},{4,12},{8,0},{12,4},{16,24},{20,28},{24,16},{28,20},{1,9},{5... | collective-permute-start | bytes 786440 | tf_op jit(solution)/shard_map/ppermute | solution.py:624
  64.3 0.5 shard_map.142
  64.8 2.1 %shard_map.143 = (bf16[512,128]{1,0:T(8,128)(2,1)S(1)}, f32[16,128]{1,0:T(8,128)S(1)}, f32[16,128]{1,0:T(8,128)S(1)}, f32[8,128,256]{2,1,0:T(8,128)S(1)}) custom-call(s32[1]{0:T(128)} %bitcast.core_ref, s32[1]{0:T(128)} %bitcast.2.side_ref, s32[1]{0:T(128)} %bitcast.4.first_mine_ref, s32[1]{0:T(128)} %bitcast.5.first_theirs_ref, ...), custom_call_target="tpu_custom_call" | custom-call | flops 1073741824 | bytes 1048576 | tf_op jit(solution)/shard_map/pallas_call | solution.py:86
  66.9 4.1 %collective-permute-done.2.couple_theirs_ref = bf16[8,128,128]{2,1,0:T(8,128)(2,1)S(1)} collective-permute-done((bf16[8,128,128]{2,1,0:T(8,128)(2,1)S(1)}, bf16[8,128,128]{2,1,0:T(8,128)(2,1)S(1)}, u32[]{:S(2)}, u32[]{:S(2)}) %collective-permute-start.2) | collective-permute-done | bytes 262176 | tf_op jit(solution)/shard_map/ppermute | solution.py:624
  71.0 3.6 %shard_map.144 = (bf16[8,128,128]{2,1,0:T(8,128)(2,1)S(1)}, bf16[8,128,128]{2,1,0:T(8,128)(2,1)S(1)}, bf16[4096,128]{1,0:T(8,128)(2,1)S(1)}) custom-call(s32[1]{0:T(128)} %bitcast.core_ref, bf16[32,88,128]{2,1,0:T(8,128)(2,1)S(1)} %collective-permute-done.1.other_ref, bf16[512,128]{1,0:T(8,128)(2,1)S(1)} %get-tuple-element.40.left_ref, ...), custom_call_target="tpu_custom_call" | custom-call | flops 2147483648 | bytes 1048576 | tf_op jit(solution)/shard_map/pallas_call | solution.py:86
  74.6 28.1 %all_to_all.22.in_ref = bf16[32,128,128]{2,1,0:T(8,128)(2,1)S(1)} all-to-all(bf16[32,128,128]{2,1,0:T(8,128)(2,1)S(1)} %bitcast.10), channel_id=1, replica_groups=mesh['branch'=8,'dap'=4] {'branch','dap'}, dimensions={0} | all-to-all | bytes 2097152 | tf_op jit(solution)/shard_map/all_to_all | solution.py:621
  102.8 1.1 shard_map.146
  103.9 4.5 %all-to-all-start.3 = ((bf16[32,32,256]{2,1,0:T(8,128)(2,1)}), bf16[32,32,256]{2,1,0:T(8,128)(2,1)S(1)}, u32[]{:S(2)}, u32[]{:S(2)}) async-start(bf16[32,32,256]{2,1,0:T(8,128)(2,1)} %shard_map.146), calls=%async_computation.3 | async-start | bytes 1048576 | tf_op jit(solution)/shard_map/all_to_all | solution.py:621
  108.5 1.8 %collective-permute-start.3 = (bf16[8,128,128]{2,1,0:T(8,128)(2,1)S(1)}, bf16[8,128,128]{2,1,0:T(8,128)(2,1)S(1)}, u32[]{:S(2)}, u32[]{:S(2)}) collective-permute-start(bf16[8,128,128]{2,1,0:T(8,128)(2,1)S(1)} %get-tuple-element.49), channel_id=1, source_target_pairs={{0,8},{4,12},{8,0},{12,4},{16,24},{20,28},{24,16},{28,20},{1,9},{5... | collective-permute-start | bytes 786440 | tf_op jit(solution)/shard_map/ppermute | solution.py:624
  110.3 11.5 %collective-permute-done.3.theirs_ref = bf16[8,128,128]{2,1,0:T(8,128)(2,1)S(1)} collective-permute-done((bf16[8,128,128]{2,1,0:T(8,128)(2,1)S(1)}, bf16[8,128,128]{2,1,0:T(8,128)(2,1)S(1)}, u32[]{:S(2)}, u32[]{:S(2)}) %collective-permute-start.3) | collective-permute-done | bytes 262176 | tf_op jit(solution)/shard_map/ppermute | solution.py:624
  121.8 1.2 shard_map.145
  123.0 1.4 %shard_map.147 = bf16[8,256,128]{2,1,0:T(8,128)(2,1)} custom-call(s32[1]{0:T(128)} %bitcast.2.side_ref, bf16[8,128,128]{2,1,0:T(8,128)(2,1)S(1)} %get-tuple-element.48.mine_ref, bf16[8,128,128]{2,1,0:T(8,128)(2,1)S(1)} %collective-permute-done.3.theirs_ref, f32[8,128,128]{2,1,0:T(8,128)S(1)} %get-tuple-element.50.mine_gate_ref, ...), custom_call_target="tpu_custom_call" | custom-call | flops 134217728 | bytes 1048576 | tf_op jit(solution)/shard_map/pallas_call | solution.py:86
  (19 shorter events, 0.1 us)
Async XLA Ops:
  2.4 22.7 %copy-start.3 = (bf16[256,64]{0,1:T(8,128)(2,1)S(1)}, bf16[256,64]{0,1:T(8,128)(2,1)}, u32[]{:S(2)}) copy-start(bf16[256,64]{0,1:T(8,128)(2,1)} %param.21) | copy-start | bytes 98308
  23.8 9.2 %collective-permute-start = (bf16[32,32,256]{2,1,0:T(8,128)(2,1)S(1)}, bf16[32,32,256]{2,1,0:T(8,128)(2,1)S(1)}, u32[]{:S(2)}, u32[]{:S(2)}) collective-permute-start(bf16[32,32,256]{2,1,0:T(8,128)(2,1)S(1)} %all_to_all.20.own_ref), channel_id=1, source_target_pairs={{0,4},{4,0},{8,12},{12,8},{16,20},{20,16},{24,28},{28,24},{1,5},{5... | collective-permute-start | bytes 1572872 | tf_op jit(solution)/shard_map/ppermute | solution.py:624
  26.0 7.0 %copy-start.5 = (bf16[256,256]{1,0:T(8,128)(2,1)S(1)}, bf16[256,256]{1,0:T(8,128)(2,1)}, u32[]{:S(2)}) copy-start(bf16[256,256]{1,0:T(8,128)(2,1)} %merge_ref.2) | copy-start | bytes 393220
  29.6 1.0 copy-start.6
  30.6 0.8 copy-start.7
  31.3 0.8 copy-start.8
  32.1 0.8 copy-start.9
  40.3 24.0 %copy-start = (bf16[1024,128]{1,0:T(8,128)(2,1)S(1)}, bf16[1024,128]{1,0:T(8,128)(2,1)}, u32[]{:S(2)}) copy-start(bf16[1024,128]{1,0:T(8,128)(2,1)} %merge_ref.3) | copy-start | bytes 786436
  40.3 24.0 %copy-start.1 = (bf16[128,512]{1,0:T(8,128)(2,1)S(1)}, bf16[128,512]{1,0:T(8,128)(2,1)}, u32[]{:S(2)}) copy-start(bf16[128,512]{1,0:T(8,128)(2,1)} %entry_ref.1) | copy-start | bytes 393220
  40.3 24.0 %copy-start.4 = (bf16[128,128]{1,0:T(8,128)(2,1)S(1)}, bf16[128,128]{1,0:T(8,128)(2,1)}, u32[]{:S(2)}) copy-start(bf16[128,128]{1,0:T(8,128)(2,1)} %close_ref.1) | copy-start | bytes 98308
  61.2 9.8 %collective-permute-start.1 = (bf16[32,88,128]{2,1,0:T(8,128)(2,1)S(1)}, bf16[32,88,128]{2,1,0:T(8,128)(2,1)S(1)}, u32[]{:S(2)}, u32[]{:S(2)}) collective-permute-start(bf16[32,88,128]{2,1,0:T(8,128)(2,1)S(1)} %all_to_all.21.own_ref), channel_id=1, source_target_pairs={{0,4},{4,0},{8,12},{12,8},{16,20},{20,16},{24,28},{28,24},{1,5},{5... | collective-permute-start | bytes 2162696 | tf_op jit(solution)/shard_map/ppermute | solution.py:624
  62.8 8.2 %collective-permute-start.2 = (bf16[8,128,128]{2,1,0:T(8,128)(2,1)S(1)}, bf16[8,128,128]{2,1,0:T(8,128)(2,1)S(1)}, u32[]{:S(2)}, u32[]{:S(2)}) collective-permute-start(bf16[8,128,128]{2,1,0:T(8,128)(2,1)S(1)} %get-tuple-element.45), channel_id=1, source_target_pairs={{0,8},{4,12},{8,0},{12,4},{16,24},{20,28},{24,16},{28,20},{1,9},{5... | collective-permute-start | bytes 786440 | tf_op jit(solution)/shard_map/ppermute | solution.py:624
  103.9 17.9 %copy-start.2 = (bf16[128,128]{1,0:T(8,128)(2,1)S(1)}, bf16[128,128]{1,0:T(8,128)(2,1)}, u32[]{:S(2)}) copy-start(bf16[128,128]{1,0:T(8,128)(2,1)} %weight_ref.1) | copy-start | bytes 98308
  103.9 19.1 %all-to-all-start.3 = ((bf16[32,32,256]{2,1,0:T(8,128)(2,1)}), bf16[32,32,256]{2,1,0:T(8,128)(2,1)S(1)}, u32[]{:S(2)}, u32[]{:S(2)}) async-start(bf16[32,32,256]{2,1,0:T(8,128)(2,1)} %shard_map.146), calls=%async_computation.3 | async-start | bytes 1048576 | tf_op jit(solution)/shard_map/all_to_all | solution.py:621
  108.5 13.4 %collective-permute-start.3 = (bf16[8,128,128]{2,1,0:T(8,128)(2,1)S(1)}, bf16[8,128,128]{2,1,0:T(8,128)(2,1)S(1)}, u32[]{:S(2)}, u32[]{:S(2)}) collective-permute-start(bf16[8,128,128]{2,1,0:T(8,128)(2,1)S(1)} %get-tuple-element.49), channel_id=1, source_target_pairs={{0,8},{4,12},{8,0},{12,4},{16,24},{20,28},{24,16},{28,20},{1,9},{5... | collective-permute-start | bytes 786440 | tf_op jit(solution)/shard_map/ppermute | solution.py:624
